TPU v7x, 32 devices: a whole 2x2x4 slice. The times are simulated.
32 devices in a mesh: row: 8 (over z, y), col: 4 (over x, core).
Axes of the slice: x: 2, y: 2, z: 4, core: 2. Of those that a mesh axis runs over, the one named last changes fastest.
Arguments:
- amps: bfloat16 [1024, 4096], P('col', 'row'), may hold values from -6 to 6, as said below
- ints: bfloat16 [2048, 8192], P('col', 'row'), may hold values from -0.125 to 0.125
- block_list: int32 [4, 4], replicated, may hold values from 0 to 1, as said below
Outputs:
- residual: float32 [32, 256, 1024], P(('row', 'col'))
Inputs may be any that keep to these rules, and one draw needn't show every extreme that they name: amps blocks (c, r) and (c, r2) are equal whenever r and r2 agree mod 4. block_list[c, k] is 1 exactly when occupied block c and cd block k carry the same irrep; each block carries one of min(8, 2) irreps, every irrep equally often among occupied blocks and among cd blocks.
All inputs are finite; a program needn't handle non-finite values.
Results may differ from a plain program's by a relative error of at most 0.0003.
Values may be sent and summed in bfloat16 or wider, within the bound.
No kernel may reach another device: no remote copies, remote signals or barrier semaphores. Data moves between devices by JAX's collectives and lax.ppermute only.
A program may use at most 64 MiB of HBM per device.

v0:
```python
import jax
import jax.numpy as jnp
from jax import lax
from jax.sharding import PartitionSpec as P


def shifted(block, axis, distance):
    devices = range(lax.axis_size(axis))
    route = [((i - distance) % len(devices), i) for i in devices]
    return lax.ppermute(block, axis, route)


def shards(amps, ints, block_list):
    row_pos = lax.axis_index("row")
    col_pos = lax.axis_index("col")
    col_count = lax.axis_size("col")
    running = jnp.zeros((amps.shape[0], ints.shape[1]), jnp.float32)
    held_amps = amps
    held_ints = ints
    for offset in range(col_count):
        block_id = (row_pos + col_pos - offset) % col_count
        factor = block_list[col_pos, block_id].astype(jnp.float32)
        running = running + factor * jnp.dot(
            held_amps, held_ints, preferred_element_type=jnp.float32
        )
        if offset + 1 < col_count:
            held_amps = shifted(held_amps, "row", 1)
            held_ints = shifted(held_ints, "col", 1)
    owned = lax.all_to_all(running, "col", split_axis=1, concat_axis=1, tiled=True)
    return owned.reshape(1, owned.shape[0], owned.shape[1])


def solution(mesh):
    placed = (P("col", "row"), P("col", "row"), P())
    return jax.shard_map(
        shards, mesh=mesh, in_specs=placed, out_specs=P(("row", "col"), None, None), check_vma=False
    )
```

profile of v0, /device:TPU:0, one launch (start us, length us, event | category | flops | bytes accessed | tf_op | source)
XLA Modules:
  0.0 75.8 jit_solution(10635011079526394941)
XLA Ops:
  0.0 0.5 collective-permute-start.1
  0.5 14.6 %collective-permute-done.1 = bf16[512,1024]{1,0:T(8,128)(2,1)S(1)} collective-permute-done((bf16[512,1024]{1,0:T(8,128)(2,1)}, bf16[512,1024]{1,0:T(8,128)(2,1)S(1)}, u32[]{:S(2)}, u32[]{:S(2)}) %collective-permute-start.1) | collective-permute-done | bytes 1048608 | tf_op jit(solution)/shard_map/ppermute | solution.py:10
  15.1 0.0 collective-permute-start.3
  15.1 2.3 %collective-permute-start = (bf16[256,512]{1,0:T(8,128)(2,1)}, bf16[256,512]{1,0:T(8,128)(2,1)S(1)}, u32[]{:S(2)}, u32[]{:S(2)}) collective-permute-start(bf16[256,512]{1,0:T(8,128)(2,1)} %param.3), channel_id=1, source_target_pairs={{28,0},{0,4},{4,8},{8,12},{12,16},{16,20},{20,24},{24,28},{29,1},{... | collective-permute-start | bytes 786440 | tf_op jit(solution)/shard_map/ppermute | solution.py:10
  17.4 11.9 %collective-permute-done.3 = bf16[512,1024]{1,0:T(8,128)(2,1)S(1)} collective-permute-done((bf16[512,1024]{1,0:T(8,128)(2,1)S(1)}, bf16[512,1024]{1,0:T(8,128)(2,1)S(1)}, u32[]{:S(2)}, u32[]{:S(2)}) %collective-permute-start.3) | collective-permute-done | bytes 1048608 | tf_op jit(solution)/shard_map/ppermute | solution.py:10
  29.3 0.0 collective-permute-start.5
  29.3 0.0 copy-start
  29.3 0.7 copy-done
  30.0 0.7 fusion.3
  33.2 0.0 collective-permute-done
  33.2 2.4 %collective-permute-start.2 = (bf16[256,512]{1,0:T(8,128)(2,1)S(1)}, bf16[256,512]{1,0:T(8,128)(2,1)S(1)}, u32[]{:S(2)}, u32[]{:S(2)}) collective-permute-start(bf16[256,512]{1,0:T(8,128)(2,1)S(1)} %collective-permute-done), channel_id=1, source_target_pairs={{28,0},{0,4},{4,8},{8,12},{12,16},{16,20},{20,24},{24,28},{29,1},{... | collective-permute-start | bytes 786440 | tf_op jit(solution)/shard_map/ppermute | solution.py:10
  35.6 1.8 %convolution_multiply_fusion.3 = f32[256,1024]{1,0:T(8,128)S(1)} fusion(bf16[256,512]{1,0:T(8,128)(2,1)} %param.3, bf16[512,1024]{1,0:T(8,128)(2,1)} %param.4, f32[]{:T(128)} %bitcast), kind=kOutput, calls=%fused_computation.6 | convolution fusion | flops 268697600 | bytes 2359300 | tf_op jit(solution)/shard_map/dot_general | solution.py:23
  37.4 7.5 %collective-permute-done.2 = bf16[256,512]{1,0:T(8,128)(2,1)S(1)} collective-permute-done((bf16[256,512]{1,0:T(8,128)(2,1)S(1)}, bf16[256,512]{1,0:T(8,128)(2,1)S(1)}, u32[]{:S(2)}, u32[]{:S(2)}) %collective-permute-start.2) | collective-permute-done | bytes 262176 | tf_op jit(solution)/shard_map/ppermute | solution.py:10
  44.9 0.0 collective-permute-start.4
  44.9 0.4 fusion.2
  45.4 0.4 fusion.1
  45.8 10.7 %collective-permute-done.4 = bf16[256,512]{1,0:T(8,128)(2,1)S(1)} collective-permute-done((bf16[256,512]{1,0:T(8,128)(2,1)S(1)}, bf16[256,512]{1,0:T(8,128)(2,1)S(1)}, u32[]{:S(2)}, u32[]{:S(2)}) %collective-permute-start.4) | collective-permute-done | bytes 262176 | tf_op jit(solution)/shard_map/ppermute | solution.py:10
  56.6 0.0 collective-permute-done.5
  56.6 0.4 fusion
  57.0 0.1 copy.10
  57.1 17.1 %all_to_all.9 = f32[256,4,256]{2,0,1:T(8,128)S(1)} all-to-all(f32[256,4,256]{2,0,1:T(8,128)S(1)} %bitcast.18), channel_id=1, replica_groups=mesh['row'=8,'col'=4] {'col'}, dimensions={1} | all-to-all | bytes 2097152 | tf_op jit(solution)/shard_map/all_to_all | solution.py:29
  74.2 0.3 copy.6
  74.5 1.3 %copy.7 = f32[1,256,1024]{2,1,0:T(8,128)} copy(f32[1,256,1024]{1,2,0:T(8,128)S(1)} %bitcast.19) | data formatting | bytes 2097152 | tf_op jit(solution)/shard_map/reshape | solution.py:30
Async XLA Ops:
  0.0 15.1 %collective-permute-start.1 = (bf16[512,1024]{1,0:T(8,128)(2,1)}, bf16[512,1024]{1,0:T(8,128)(2,1)S(1)}, u32[]{:S(2)}, u32[]{:S(2)}) collective-permute-start(bf16[512,1024]{1,0:T(8,128)(2,1)} %param.4), channel_id=1, source_target_pairs={{3,0},{0,1},{1,2},{2,3},{7,4},{4,5},{5,6},{6,7},{11,8},{8,9},{9,10... | collective-permute-start | bytes 3145736 | tf_op jit(solution)/shard_map/ppermute | solution.py:10
  15.1 14.2 %collective-permute-start.3 = (bf16[512,1024]{1,0:T(8,128)(2,1)S(1)}, bf16[512,1024]{1,0:T(8,128)(2,1)S(1)}, u32[]{:S(2)}, u32[]{:S(2)}) collective-permute-start(bf16[512,1024]{1,0:T(8,128)(2,1)S(1)} %collective-permute-done.1), channel_id=1, source_target_pairs={{3,0},{0,1},{1,2},{2,3},{7,4},{4,5},{5,6},{6,7},{11,8},{8,9},{9,10... | collective-permute-start | bytes 3145736 | tf_op jit(solution)/shard_map/ppermute | solution.py:10
  15.1 18.1 %collective-permute-start = (bf16[256,512]{1,0:T(8,128)(2,1)}, bf16[256,512]{1,0:T(8,128)(2,1)S(1)}, u32[]{:S(2)}, u32[]{:S(2)}) collective-permute-start(bf16[256,512]{1,0:T(8,128)(2,1)} %param.3), channel_id=1, source_target_pairs={{28,0},{0,4},{4,8},{8,12},{12,16},{16,20},{20,24},{24,28},{29,1},{... | collective-permute-start | bytes 786440 | tf_op jit(solution)/shard_map/ppermute | solution.py:10
  29.3 27.3 %collective-permute-start.5 = (bf16[512,1024]{1,0:T(8,128)(2,1)S(1)}, bf16[512,1024]{1,0:T(8,128)(2,1)S(1)}, u32[]{:S(2)}, u32[]{:S(2)}) collective-permute-start(bf16[512,1024]{1,0:T(8,128)(2,1)S(1)} %collective-permute-done.3), channel_id=1, source_target_pairs={{3,0},{0,1},{1,2},{2,3},{7,4},{4,5},{5,6},{6,7},{11,8},{8,9},{9,10... | collective-permute-start | bytes 3145736 | tf_op jit(solution)/shard_map/ppermute | solution.py:10
  29.3 0.7 copy-start
  33.2 11.7 %collective-permute-start.2 = (bf16[256,512]{1,0:T(8,128)(2,1)S(1)}, bf16[256,512]{1,0:T(8,128)(2,1)S(1)}, u32[]{:S(2)}, u32[]{:S(2)}) collective-permute-start(bf16[256,512]{1,0:T(8,128)(2,1)S(1)} %collective-permute-done), channel_id=1, source_target_pairs={{28,0},{0,4},{4,8},{8,12},{12,16},{16,20},{20,24},{24,28},{29,1},{... | collective-permute-start | bytes 786440 | tf_op jit(solution)/shard_map/ppermute | solution.py:10
  44.9 11.6 %collective-permute-start.4 = (bf16[256,512]{1,0:T(8,128)(2,1)S(1)}, bf16[256,512]{1,0:T(8,128)(2,1)S(1)}, u32[]{:S(2)}, u32[]{:S(2)}) collective-permute-start(bf16[256,512]{1,0:T(8,128)(2,1)S(1)} %collective-permute-done.2), channel_id=1, source_target_pairs={{28,0},{0,4},{4,8},{8,12},{12,16},{16,20},{20,24},{24,28},{29,1},{... | collective-permute-start | bytes 786440 | tf_op jit(solution)/shard_map/ppermute | solution.py:10
where the time goes:
time: 76.1 us; the launch traced here: 75.8 us
  waiting for transfers between devices  44.8 us (59%)
  blocking collectives  17.1 us (22%)
  starting transfers between devices  5.18 us (7%)
  matrix products  3.08 us (4%)
  local copies, waits for them, and re-layouts  3.07 us (4%)
  between operations  2.66 us (3%)
    ppermute x6, waiting for transfers between devices, shifted(): return lax.ppermute(block, axis, route)  44.8 us
    all_to_all x1, blocking collectives, shards(): lax.all_to_all(running, 'col', split_axis=1, concat_axis=1, tiled=True)  17.1 us
    ppermute x6, starting transfers between devices, shifted(): return lax.ppermute(block, axis, route)  5.18 us
    dot_general x4, matrix products, shards(): jnp.dot(held_amps, held_ints, preferred_element_type=jnp.float32)  3.08 us
  transfers between devices with their start and end apart: 6, of which 4 were waited for; matrix products, arithmetic and copies ran while one was open for 4% of the time, Pallas kernels for 0%

commit v1 on v0

--- a/solution.py
+++ b/solution.py
@@ -1,7 +1,13 @@
+import functools
+
 import jax
 import jax.numpy as jnp
 from jax import lax
+from jax.experimental import pallas as pl
+from jax.experimental.pallas import tpu as pltpu
 from jax.sharding import PartitionSpec as P
+
+GRID = ("row", "col")
 
 
 def shifted(block, axis, distance):
@@ -10,7 +16,7 @@
     return lax.ppermute(block, axis, route)
 
 
-def shards(amps, ints, block_list):
+def shift_shards(amps, ints, block_list):
     row_pos = lax.axis_index("row")
     col_pos = lax.axis_index("col")
     col_count = lax.axis_size("col")
@@ -30,8 +36,95 @@
     return owned.reshape(1, owned.shape[0], owned.shape[1])
 
 
+def swapped(label):
+    return ((label & 1) << 1) | (label >> 1)
+
+
+def multiply_kernel(place, pairs, *refs, width):
+    blocks, v_all, out, held, sems = refs[:16], refs[16], refs[17], refs[18], refs[19]
+    row, col = place[0], place[1]
+    copies = []
+    for part, offset in enumerate((0, 2, 1, 3)):
+        owner = col ^ offset
+        held[part] = jnp.zeros(held.shape[1:], held.dtype)
+        for slot in range(4):
+            step = jnp.where((owner & 1) == 0, slot, swapped(slot))
+            kind = ((row ^ step) + owner) & 3
+            source = ((kind - row) & 3) ^ col
+
+            @pl.when(pairs[owner, kind] != 0)
+            def _(part=part, slot=slot, source=source):
+                held[part] += jnp.dot(
+                    blocks[part * 4 + slot][...], v_all[source], preferred_element_type=jnp.float32
+                )
+
+        start = pl.multiple_of(owner * width, width)
+        copy = pltpu.make_async_copy(held.at[part], out.at[:, pl.ds(start, width)], sems.at[part])
+        copy.start()
+        copies.append(copy)
+    for copy in copies:
+        copy.wait()
+
+
+def gather_shards(amps, ints, block_list):
+    rows, cols = lax.axis_size("row"), lax.axis_size("col")
+    row_pos, col_pos = lax.axis_index("row"), lax.axis_index("col")
+    width = ints.shape[1] // cols
+
+    def moved(block, target):
+        route = [
+            (r * cols + c, target(r, c)[0] * cols + target(r, c)[1])
+            for r in range(rows)
+            for c in range(cols)
+        ]
+        return lax.ppermute(block, GRID, route)
+
+    first = functools.partial(moved, target=lambda r, c: (r ^ (1 + (c & 1)), c))
+    second = functools.partial(moved, target=lambda r, c: (r ^ (2 - (c & 1)), c))
+    across = functools.partial(moved, target=lambda r, c: (r, c ^ 2))
+    cross = functools.partial(moved, target=lambda r, c: (r, c ^ 3))
+    beside = functools.partial(moved, target=lambda r, c: (r, c ^ 1))
+
+    def piece(offset):
+        return lax.dynamic_slice_in_dim(ints, (col_pos ^ offset) * width, width, 1)
+
+    far0 = across(amps)
+    near1 = first(amps)
+    near2 = second(amps)
+    v2 = across(piece(2))
+    v3 = cross(piece(3))
+    near3 = second(near1)
+    v1 = beside(piece(1))
+    far1 = first(far0)
+    far2 = second(far0)
+    far3 = second(far1)
+    own = [amps, near1, near2, near3, far0, far1, far2, far3]
+    blocks = own + [beside(b) for b in own]
+    v_all = jnp.stack([piece(0), v1, v2, v3])
+    place = jnp.stack([row_pos, col_pos]).astype(jnp.int32)
+    smem = pl.BlockSpec(memory_space=pltpu.SMEM)
+    vmem = pl.BlockSpec(memory_space=pltpu.VMEM)
+    out = pl.pallas_call(
+        functools.partial(multiply_kernel, width=width),
+        out_shape=jax.ShapeDtypeStruct((amps.shape[0], ints.shape[1]), jnp.float32),
+        in_specs=[smem, smem] + [vmem] * 17,
+        out_specs=pl.BlockSpec(memory_space=pl.ANY),
+        scratch_shapes=[
+            pltpu.VMEM((4, amps.shape[0], width), jnp.float32),
+            pltpu.SemaphoreType.DMA((4,)),
+        ],
+        name="multiply",
+    )(place, block_list, *blocks, v_all)
+    return out[None]
+
+
 def solution(mesh):
     placed = (P("col", "row"), P("col", "row"), P())
+    whole_gather = mesh.shape["col"] == 4 and mesh.shape["row"] % 4 == 0
     return jax.shard_map(
-        shards, mesh=mesh, in_specs=placed, out_specs=P(("row", "col"), None, None), check_vma=False
+        gather_shards if whole_gather else shift_shards,
+        mesh=mesh,
+        in_specs=placed,
+        out_specs=P(("row", "col"), None, None),
+        check_vma=False,
     )

time: 76.1 us -> 42.1 us (0.55)
  waiting for transfers between devices: 44.8 us -> 18.6 us
  blocking collectives: 17.1 us -> 0 us
  starting transfers between devices: 5.18 us -> 13 us
  Pallas kernels: 0 us -> 5.25 us
  matrix products: 3.08 us -> 0 us
  other arithmetic: 0 us -> 2.81 us
  between operations: 2.66 us -> 0.18 us
  local copies, waits for them, and re-layouts: 3.07 us -> 2.07 us
    ppermute x6 -> x18, waiting for transfers between devices: 44.8 us -> 18.6 us  [moved(): return lax.ppermute(block, GRID, route)]
    all_to_all x1 -> x0, blocking collectives: 17.1 us -> none  [shards(): lax.all_to_all(running, 'col', split_axis=1, concat_axis=1, tiled=True)]
    ppermute x6 -> x18, starting transfers between devices: 5.18 us -> 13 us  [moved(): return lax.ppermute(block, GRID, route)]
    pallas_call x0 -> x1, Pallas kernels: none -> 5.25 us  [gather_shards(): pl.pallas_call(functools.partial(multiply_kernel, width=width), out_shape...]
    dot_general x4 -> x0, matrix products: 3.08 us -> none  [shards(): jnp.dot(held_amps, held_ints, preferred_element_type=jnp.float32)]
    another operation x0 -> x2, other arithmetic: none -> 2.81 us  [the longest x1 2.21 us: gather_shards(): v_all = jnp.stack([piece(0), v1, v2, v3])]
    reshape x1 -> x0, local copies, waits for them, and re-layouts: 1.31 us -> none  [shards(): return owned.reshape(1, owned.shape[0], owned.shape[1])]
    another operation x0 -> x1, local copies, waits for them, and re-layouts: none -> 1.27 us  [gather_shards(): v_all = jnp.stack([piece(0), v1, v2, v3])]
  transfers between devices with their start and end apart: 6 -> 18, of which waited for: 4 -> 6; matrix products, arithmetic and copies ran while one was open for 4% -> 10% of each run, Pallas kernels for 0% -> 0%
where the time goes in v1:
time: 42.1 us; the launch traced here: 41.9 us
  waiting for transfers between devices  18.6 us (44%)
  starting transfers between devices  13 us (31%)
  Pallas kernels  5.25 us (12%)
  other arithmetic  2.81 us (7%)
  local copies, waits for them, and re-layouts  2.07 us (5%)
    ppermute x18, waiting for transfers between devices, moved(): return lax.ppermute(block, GRID, route)  18.6 us
    ppermute x18, starting transfers between devices, moved(): return lax.ppermute(block, GRID, route)  13 us
    pallas_call x1, Pallas kernels, gather_shards(): pl.pallas_call(functools.partial(multiply_kernel, width=width), out_shape...  5.25 us
    another operation x1, other arithmetic, gather_shards(): v_all = jnp.stack([piece(0), v1, v2, v3])  2.21 us
    another operation x1, local copies, waits for them, and re-layouts, gather_shards(): v_all = jnp.stack([piece(0), v1, v2, v3])  1.27 us
  transfers between devices with their start and end apart: 18, of which 6 were waited for; matrix products, arithmetic and copies ran while one was open for 10% of the time, Pallas kernels for 0%

profile of v1, /device:TPU:0, one launch (start us, length us, event | category | flops | bytes accessed | tf_op | source)
XLA Modules:
  0.0 41.9 jit_solution(6927128910444268633)
XLA Ops:
  0.0 2.9 %collective-permute-start.3 = (bf16[256,512]{1,0:T(8,128)(2,1)}, bf16[256,512]{1,0:T(8,128)(2,1)S(1)}, u32[]{:S(2)}, u32[]{:S(2)}) collective-permute-start(bf16[256,512]{1,0:T(8,128)(2,1)} %refs_0_.1), channel_id=1, source_target_pairs={{0,2},{1,3},{2,0},{3,1},{4,6},{5,7},{6,4},{7,5},{8,10},{9,11},{10,... | collective-permute-start | bytes 786440 | tf_op jit(solution)/shard_map/ppermute | solution.py:80
  2.9 1.6 %collective-permute-start.1 = (bf16[256,512]{1,0:T(8,128)(2,1)}, bf16[256,512]{1,0:T(8,128)(2,1)S(1)}, u32[]{:S(2)}, u32[]{:S(2)}) collective-permute-start(bf16[256,512]{1,0:T(8,128)(2,1)} %refs_0_.1), channel_id=1, source_target_pairs={{0,8},{1,5},{2,10},{3,7},{4,12},{5,1},{6,14},{7,3},{8,0},{9,13},{1... | collective-permute-start | bytes 786440 | tf_op jit(solution)/shard_map/ppermute | solution.py:80
  4.5 1.5 %collective-permute-start = (bf16[256,512]{1,0:T(8,128)(2,1)}, bf16[256,512]{1,0:T(8,128)(2,1)S(1)}, u32[]{:S(2)}, u32[]{:S(2)}) collective-permute-start(bf16[256,512]{1,0:T(8,128)(2,1)} %refs_0_.1), channel_id=1, source_target_pairs={{0,4},{1,9},{2,6},{3,11},{4,0},{5,13},{6,2},{7,15},{8,12},{9,1},{1... | collective-permute-start | bytes 786440 | tf_op jit(solution)/shard_map/ppermute | solution.py:80
  6.0 1.3 %dynamic-slice_bitcast_fusion = (bf16[1,512,256]{2,1,0:T(8,128)(2,1)S(1)}, bf16[512,256]{1,0:T(8,128)(2,1)S(1)}, bf16[512,256]{1,0:T(8,128)(2,1)S(1)}, bf16[512,256]{1,0:T(8,128)(2,1)S(1)}) fusion(bf16[512,1024]{1,0:T(8,128)(2,1)} %param.4, s32[]{:T(128)S(6)} %select_n.12, s32[]{:T(128)S(6)} %select_n.13, s32[]{:T(128)S(6)} %select_n.15, s32[]{:T(128)S(6)} %select_n.14), kind=kLoop, calls=%fused_computation.1 | loop fusion | bytes 2097168 | tf_op jit(solution)/shard_map/stack | solution.py:103
  7.3 0.6 %collective-permute-start.15 = (bf16[512,256]{1,0:T(8,128)(2,1)S(1)}, bf16[512,256]{1,0:T(8,128)(2,1)S(1)}, u32[]{:S(2)}, u32[]{:S(2)}) collective-permute-start(bf16[512,256]{1,0:T(8,128)(2,1)S(1)} %get-tuple-element.6), channel_id=1, source_target_pairs={{0,1},{1,0},{2,3},{3,2},{4,5},{5,4},{6,7},{7,6},{8,9},{9,8},{10,11... | collective-permute-start | bytes 786440 | tf_op jit(solution)/shard_map/ppermute | solution.py:80
  7.9 1.6 %collective-permute-done.3.refs_4_ = bf16[256,512]{1,0:T(8,128)(2,1)S(1)} collective-permute-done((bf16[256,512]{1,0:T(8,128)(2,1)}, bf16[256,512]{1,0:T(8,128)(2,1)S(1)}, u32[]{:S(2)}, u32[]{:S(2)}) %collective-permute-start.3) | collective-permute-done | bytes 262176 | tf_op jit(solution)/shard_map/ppermute | solution.py:80
  9.5 0.3 collective-permute-start.17
  9.8 2.4 %collective-permute-done.1.refs_2_ = bf16[256,512]{1,0:T(8,128)(2,1)S(1)} collective-permute-done((bf16[256,512]{1,0:T(8,128)(2,1)}, bf16[256,512]{1,0:T(8,128)(2,1)S(1)}, u32[]{:S(2)}, u32[]{:S(2)}) %collective-permute-start.1) | collective-permute-done | bytes 262176 | tf_op jit(solution)/shard_map/ppermute | solution.py:80
  12.2 0.9 %collective-permute-start.4 = (bf16[256,512]{1,0:T(8,128)(2,1)S(1)}, bf16[256,512]{1,0:T(8,128)(2,1)S(1)}, u32[]{:S(2)}, u32[]{:S(2)}) collective-permute-start(bf16[256,512]{1,0:T(8,128)(2,1)S(1)} %collective-permute-done.3.refs_4_), channel_id=1, source_target_pairs={{0,4},{1,9},{2,6},{3,11},{4,0},{5,13},{6,2},{7,15},{8,12},{9,1},{1... | collective-permute-start | bytes 786440 | tf_op jit(solution)/shard_map/ppermute | solution.py:80
  13.1 0.3 collective-permute-start.11
  13.4 1.5 %collective-permute-start.5 = (bf16[256,512]{1,0:T(8,128)(2,1)S(1)}, bf16[256,512]{1,0:T(8,128)(2,1)S(1)}, u32[]{:S(2)}, u32[]{:S(2)}) collective-permute-start(bf16[256,512]{1,0:T(8,128)(2,1)S(1)} %collective-permute-done.3.refs_4_), channel_id=1, source_target_pairs={{0,8},{1,5},{2,10},{3,7},{4,12},{5,1},{6,14},{7,3},{8,0},{9,13},{1... | collective-permute-start | bytes 786440 | tf_op jit(solution)/shard_map/ppermute | solution.py:80
  14.9 2.9 %collective-permute-done.17 = bf16[512,256]{1,0:T(8,128)(2,1)S(1)} collective-permute-done((bf16[512,256]{1,0:T(8,128)(2,1)S(1)}, bf16[512,256]{1,0:T(8,128)(2,1)S(1)}, u32[]{:S(2)}, u32[]{:S(2)}) %collective-permute-start.17) | collective-permute-done | bytes 262176 | tf_op jit(solution)/shard_map/ppermute | solution.py:80
  17.8 0.7 %collective-permute-start.9 = (bf16[256,512]{1,0:T(8,128)(2,1)S(1)}, bf16[256,512]{1,0:T(8,128)(2,1)S(1)}, u32[]{:S(2)}, u32[]{:S(2)}) collective-permute-start(bf16[256,512]{1,0:T(8,128)(2,1)S(1)} %collective-permute-done.1.refs_2_), channel_id=1, source_target_pairs={{0,1},{1,0},{2,3},{3,2},{4,5},{5,4},{6,7},{7,6},{8,9},{9,8},{10,11... | collective-permute-start | bytes 786440 | tf_op jit(solution)/shard_map/ppermute | solution.py:80
  18.5 5.2 %collective-permute-done.16 = bf16[512,256]{1,0:T(8,128)(2,1)S(1)} collective-permute-done((bf16[512,256]{1,0:T(8,128)(2,1)S(1)}, bf16[512,256]{1,0:T(8,128)(2,1)S(1)}, u32[]{:S(2)}, u32[]{:S(2)}) %collective-permute-start.16) | collective-permute-done | bytes 262176 | tf_op jit(solution)/shard_map/ppermute | solution.py:80
  23.7 1.8 %collective-permute-start.2 = (bf16[256,512]{1,0:T(8,128)(2,1)S(1)}, bf16[256,512]{1,0:T(8,128)(2,1)S(1)}, u32[]{:S(2)}, u32[]{:S(2)}) collective-permute-start(bf16[256,512]{1,0:T(8,128)(2,1)S(1)} %collective-permute-done.refs_1_), channel_id=1, source_target_pairs={{0,8},{1,5},{2,10},{3,7},{4,12},{5,1},{6,14},{7,3},{8,0},{9,13},{1... | collective-permute-start | bytes 786440 | tf_op jit(solution)/shard_map/ppermute | solution.py:80
  25.5 0.2 collective-permute-start.6
  25.7 0.5 %collective-permute-start.12 = (bf16[256,512]{1,0:T(8,128)(2,1)S(1)}, bf16[256,512]{1,0:T(8,128)(2,1)S(1)}, u32[]{:S(2)}, u32[]{:S(2)}) collective-permute-start(bf16[256,512]{1,0:T(8,128)(2,1)S(1)} %collective-permute-done.4.refs_5_), channel_id=1, source_target_pairs={{0,1},{1,0},{2,3},{3,2},{4,5},{5,4},{6,7},{7,6},{8,9},{9,8},{10,11... | collective-permute-start | bytes 786440 | tf_op jit(solution)/shard_map/ppermute | solution.py:80
  26.3 3.7 %collective-permute-done.2.refs_3_ = bf16[256,512]{1,0:T(8,128)(2,1)S(1)} collective-permute-done((bf16[256,512]{1,0:T(8,128)(2,1)S(1)}, bf16[256,512]{1,0:T(8,128)(2,1)S(1)}, u32[]{:S(2)}, u32[]{:S(2)}) %collective-permute-start.2) | collective-permute-done | bytes 262176 | tf_op jit(solution)/shard_map/ppermute | solution.py:80
  30.1 2.8 %collective-permute-done.6.refs_7_ = bf16[256,512]{1,0:T(8,128)(2,1)S(1)} collective-permute-done((bf16[256,512]{1,0:T(8,128)(2,1)S(1)}, bf16[256,512]{1,0:T(8,128)(2,1)S(1)}, u32[]{:S(2)}, u32[]{:S(2)}) %collective-permute-start.6) | collective-permute-done | bytes 262176 | tf_op jit(solution)/shard_map/ppermute | solution.py:80
  33.0 0.6 %pad_add_fusion.place = s32[2]{0:T(128)} fusion(s32[1]{0:T(128)} %bitcast.1, s32[1]{0:T(128)} %bitcast), kind=kLoop, calls=%fused_computation.5 | loop fusion | flops 2 | bytes 16 | tf_op jit(solution)/shard_map/stack | solution.py:104
  33.6 2.2 %pad_maximum_fusion.refs_16_ = bf16[4,512,256]{2,1,0:T(8,128)(2,1)} fusion(bf16[1,512,256]{2,1,0:T(8,128)(2,1)} %bitcast.9, bf16[1,512,256]{2,1,0:T(8,128)(2,1)} %bitcast.10, bf16[1,512,256]{2,1,0:T(8,128)(2,1)} %bitcast.8, bf16[1,512,256]{2,1,0:T(8,128)(2,1)S(1)} %get-tuple-element.5), kind=kLoop, calls=%fused_computation | loop fusion | flops 1572864 | bytes 2097152 | tf_op jit(solution)/shard_map/stack | solution.py:103
  35.9 0.6 %copy-done.10 = bf16[256,512]{1,0:T(8,128)(2,1)} copy-done((bf16[256,512]{1,0:T(8,128)(2,1)}, bf16[256,512]{1,0:T(8,128)(2,1)S(1)}, u32[]{:S(2)}) %copy-start.10) | copy-done | bytes 262168
  36.6 0.1 copy-done.11
  36.7 5.3 %multiply.1 = f32[256,1024]{1,0:T(8,128)} custom-call(s32[2]{0:T(128)} %pad_add_fusion.place, s32[4,4]{1,0:T(4,128)} %pairs.1, bf16[256,512]{1,0:T(8,128)(2,1)} %refs_0_.1, bf16[256,512]{1,0:T(8,128)(2,1)} %copy-done.2, bf16[256,512]{1,0:T(8,128)(2,1)} %copy-done.1, bf16[256,512]{1,0:T(8,128)(2,1)} %copy-done.8, bf16[256,512]{1,0:T(8,128)(2,1)} %copy-done, ...), custom_call_target="tpu_custom_call" | custom-call | tf_op jit(solution)/shard_map/multiply/pallas_call | solution.py:107
  (46 shorter events, 0.3 us)
Async XLA Ops:
  0.0 9.5 %collective-permute-start.3 = (bf16[256,512]{1,0:T(8,128)(2,1)}, bf16[256,512]{1,0:T(8,128)(2,1)S(1)}, u32[]{:S(2)}, u32[]{:S(2)}) collective-permute-start(bf16[256,512]{1,0:T(8,128)(2,1)} %refs_0_.1), channel_id=1, source_target_pairs={{0,2},{1,3},{2,0},{3,1},{4,6},{5,7},{6,4},{7,5},{8,10},{9,11},{10,... | collective-permute-start | bytes 786440 | tf_op jit(solution)/shard_map/ppermute | solution.py:80
  2.9 9.2 %collective-permute-start.1 = (bf16[256,512]{1,0:T(8,128)(2,1)}, bf16[256,512]{1,0:T(8,128)(2,1)S(1)}, u32[]{:S(2)}, u32[]{:S(2)}) collective-permute-start(bf16[256,512]{1,0:T(8,128)(2,1)} %refs_0_.1), channel_id=1, source_target_pairs={{0,8},{1,5},{2,10},{3,7},{4,12},{5,1},{6,14},{7,3},{8,0},{9,13},{1... | collective-permute-start | bytes 786440 | tf_op jit(solution)/shard_map/ppermute | solution.py:80
  4.5 7.7 %collective-permute-start = (bf16[256,512]{1,0:T(8,128)(2,1)}, bf16[256,512]{1,0:T(8,128)(2,1)S(1)}, u32[]{:S(2)}, u32[]{:S(2)}) collective-permute-start(bf16[256,512]{1,0:T(8,128)(2,1)} %refs_0_.1), channel_id=1, source_target_pairs={{0,4},{1,9},{2,6},{3,11},{4,0},{5,13},{6,2},{7,15},{8,12},{9,1},{1... | collective-permute-start | bytes 786440 | tf_op jit(solution)/shard_map/ppermute | solution.py:80
  6.0 7.0 %collective-permute-start.7 = (bf16[256,512]{1,0:T(8,128)(2,1)}, bf16[256,512]{1,0:T(8,128)(2,1)S(1)}, u32[]{:S(2)}, u32[]{:S(2)}) collective-permute-start(bf16[256,512]{1,0:T(8,128)(2,1)} %refs_0_.1), channel_id=1, source_target_pairs={{0,1},{1,0},{2,3},{3,2},{4,5},{5,4},{6,7},{7,6},{8,9},{9,8},{10,11... | collective-permute-start | bytes 786440 | tf_op jit(solution)/shard_map/ppermute | solution.py:80
  7.3 6.1 %collective-permute-start.15 = (bf16[512,256]{1,0:T(8,128)(2,1)S(1)}, bf16[512,256]{1,0:T(8,128)(2,1)S(1)}, u32[]{:S(2)}, u32[]{:S(2)}) collective-permute-start(bf16[512,256]{1,0:T(8,128)(2,1)S(1)} %get-tuple-element.6), channel_id=1, source_target_pairs={{0,1},{1,0},{2,3},{3,2},{4,5},{5,4},{6,7},{7,6},{8,9},{9,8},{10,11... | collective-permute-start | bytes 786440 | tf_op jit(solution)/shard_map/ppermute | solution.py:80
  9.5 26.3 %copy-start = (bf16[256,512]{1,0:T(8,128)(2,1)}, bf16[256,512]{1,0:T(8,128)(2,1)S(1)}, u32[]{:S(2)}) copy-start(bf16[256,512]{1,0:T(8,128)(2,1)S(1)} %collective-permute-done.3.refs_4_) | copy-start | bytes 786436
  9.5 8.3 %collective-permute-start.17 = (bf16[512,256]{1,0:T(8,128)(2,1)S(1)}, bf16[512,256]{1,0:T(8,128)(2,1)S(1)}, u32[]{:S(2)}, u32[]{:S(2)}) collective-permute-start(bf16[512,256]{1,0:T(8,128)(2,1)S(1)} %get-tuple-element.7), channel_id=1, source_target_pairs={{0,3},{1,2},{2,1},{3,0},{4,7},{5,6},{6,5},{7,4},{8,11},{9,10},{10,... | collective-permute-start | bytes 786440 | tf_op jit(solution)/shard_map/ppermute | solution.py:80
  12.2 23.6 %copy-start.1 = (bf16[256,512]{1,0:T(8,128)(2,1)}, bf16[256,512]{1,0:T(8,128)(2,1)S(1)}, u32[]{:S(2)}) copy-start(bf16[256,512]{1,0:T(8,128)(2,1)S(1)} %collective-permute-done.1.refs_2_) | copy-start | bytes 786436
  12.2 11.5 %collective-permute-start.16 = (bf16[512,256]{1,0:T(8,128)(2,1)S(1)}, bf16[512,256]{1,0:T(8,128)(2,1)S(1)}, u32[]{:S(2)}, u32[]{:S(2)}) collective-permute-start(bf16[512,256]{1,0:T(8,128)(2,1)S(1)} %get-tuple-element.8), channel_id=1, source_target_pairs={{0,2},{1,3},{2,0},{3,1},{4,6},{5,7},{6,4},{7,5},{8,10},{9,11},{10,... | collective-permute-start | bytes 786440 | tf_op jit(solution)/shard_map/ppermute | solution.py:80
  12.2 23.6 %copy-start.2 = (bf16[256,512]{1,0:T(8,128)(2,1)}, bf16[256,512]{1,0:T(8,128)(2,1)S(1)}, u32[]{:S(2)}) copy-start(bf16[256,512]{1,0:T(8,128)(2,1)S(1)} %collective-permute-done.refs_1_) | copy-start | bytes 786436
  12.2 13.3 %collective-permute-start.4 = (bf16[256,512]{1,0:T(8,128)(2,1)S(1)}, bf16[256,512]{1,0:T(8,128)(2,1)S(1)}, u32[]{:S(2)}, u32[]{:S(2)}) collective-permute-start(bf16[256,512]{1,0:T(8,128)(2,1)S(1)} %collective-permute-done.3.refs_4_), channel_id=1, source_target_pairs={{0,4},{1,9},{2,6},{3,11},{4,0},{5,13},{6,2},{7,15},{8,12},{9,1},{1... | collective-permute-start | bytes 786440 | tf_op jit(solution)/shard_map/ppermute | solution.py:80
  13.1 22.7 %copy-start.3 = (bf16[256,512]{1,0:T(8,128)(2,1)}, bf16[256,512]{1,0:T(8,128)(2,1)S(1)}, u32[]{:S(2)}) copy-start(bf16[256,512]{1,0:T(8,128)(2,1)S(1)} %collective-permute-done.7.refs_8_) | copy-start | bytes 786436
  13.1 12.6 %collective-permute-start.11 = (bf16[256,512]{1,0:T(8,128)(2,1)S(1)}, bf16[256,512]{1,0:T(8,128)(2,1)S(1)}, u32[]{:S(2)}, u32[]{:S(2)}) collective-permute-start(bf16[256,512]{1,0:T(8,128)(2,1)S(1)} %collective-permute-done.3.refs_4_), channel_id=1, source_target_pairs={{0,1},{1,0},{2,3},{3,2},{4,5},{5,4},{6,7},{7,6},{8,9},{9,8},{10,11... | collective-permute-start | bytes 786440 | tf_op jit(solution)/shard_map/ppermute | solution.py:80
  13.4 19.5 %copy-start.12 = (bf16[512,256]{1,0:T(8,128)(2,1)}, bf16[512,256]{1,0:T(8,128)(2,1)S(1)}, u32[]{:S(2)}) copy-start(bf16[512,256]{1,0:T(8,128)(2,1)S(1)} %collective-permute-done.15) | copy-start | bytes 786436
  13.4 12.3 %collective-permute-start.5 = (bf16[256,512]{1,0:T(8,128)(2,1)S(1)}, bf16[256,512]{1,0:T(8,128)(2,1)S(1)}, u32[]{:S(2)}, u32[]{:S(2)}) collective-permute-start(bf16[256,512]{1,0:T(8,128)(2,1)S(1)} %collective-permute-done.3.refs_4_), channel_id=1, source_target_pairs={{0,8},{1,5},{2,10},{3,7},{4,12},{5,1},{6,14},{7,3},{8,0},{9,13},{1... | collective-permute-start | bytes 786440 | tf_op jit(solution)/shard_map/ppermute | solution.py:80
  17.8 15.1 %copy-start.13 = (bf16[512,256]{1,0:T(8,128)(2,1)}, bf16[512,256]{1,0:T(8,128)(2,1)S(1)}, u32[]{:S(2)}) copy-start(bf16[512,256]{1,0:T(8,128)(2,1)S(1)} %collective-permute-done.17) | copy-start | bytes 786436
  17.8 8.5 %collective-permute-start.9 = (bf16[256,512]{1,0:T(8,128)(2,1)S(1)}, bf16[256,512]{1,0:T(8,128)(2,1)S(1)}, u32[]{:S(2)}, u32[]{:S(2)}) collective-permute-start(bf16[256,512]{1,0:T(8,128)(2,1)S(1)} %collective-permute-done.1.refs_2_), channel_id=1, source_target_pairs={{0,1},{1,0},{2,3},{3,2},{4,5},{5,4},{6,7},{7,6},{8,9},{9,8},{10,11... | collective-permute-start | bytes 786440 | tf_op jit(solution)/shard_map/ppermute | solution.py:80
  23.7 6.4 %collective-permute-start.2 = (bf16[256,512]{1,0:T(8,128)(2,1)S(1)}, bf16[256,512]{1,0:T(8,128)(2,1)S(1)}, u32[]{:S(2)}, u32[]{:S(2)}) collective-permute-start(bf16[256,512]{1,0:T(8,128)(2,1)S(1)} %collective-permute-done.refs_1_), channel_id=1, source_target_pairs={{0,8},{1,5},{2,10},{3,7},{4,12},{5,1},{6,14},{7,3},{8,0},{9,13},{1... | collective-permute-start | bytes 786440 | tf_op jit(solution)/shard_map/ppermute | solution.py:80
  25.5 7.3 %collective-permute-start.6 = (bf16[256,512]{1,0:T(8,128)(2,1)S(1)}, bf16[256,512]{1,0:T(8,128)(2,1)S(1)}, u32[]{:S(2)}, u32[]{:S(2)}) collective-permute-start(bf16[256,512]{1,0:T(8,128)(2,1)S(1)} %collective-permute-done.4.refs_5_), channel_id=1, source_target_pairs={{0,8},{1,5},{2,10},{3,7},{4,12},{5,1},{6,14},{7,3},{8,0},{9,13},{1... | collective-permute-start | bytes 786440 | tf_op jit(solution)/shard_map/ppermute | solution.py:80
  25.7 10.1 %collective-permute-start.8 = (bf16[256,512]{1,0:T(8,128)(2,1)S(1)}, bf16[256,512]{1,0:T(8,128)(2,1)S(1)}, u32[]{:S(2)}, u32[]{:S(2)}) collective-permute-start(bf16[256,512]{1,0:T(8,128)(2,1)S(1)} %collective-permute-done.refs_1_), channel_id=1, source_target_pairs={{0,1},{1,0},{2,3},{3,2},{4,5},{5,4},{6,7},{7,6},{8,9},{9,8},{10,11... | collective-permute-start | bytes 786440 | tf_op jit(solution)/shard_map/ppermute | solution.py:80
  25.7 10.1 %collective-permute-start.12 = (bf16[256,512]{1,0:T(8,128)(2,1)S(1)}, bf16[256,512]{1,0:T(8,128)(2,1)S(1)}, u32[]{:S(2)}, u32[]{:S(2)}) collective-permute-start(bf16[256,512]{1,0:T(8,128)(2,1)S(1)} %collective-permute-done.4.refs_5_), channel_id=1, source_target_pairs={{0,1},{1,0},{2,3},{3,2},{4,5},{5,4},{6,7},{7,6},{8,9},{9,8},{10,11... | collective-permute-start | bytes 786440 | tf_op jit(solution)/shard_map/ppermute | solution.py:80
  26.2 9.6 %collective-permute-start.13 = (bf16[256,512]{1,0:T(8,128)(2,1)S(1)}, bf16[256,512]{1,0:T(8,128)(2,1)}, u32[]{:S(2)}, u32[]{:S(2)}) collective-permute-start(bf16[256,512]{1,0:T(8,128)(2,1)S(1)} %collective-permute-done.5.refs_6_), channel_id=1, source_target_pairs={{0,1},{1,0},{2,3},{3,2},{4,5},{5,4},{6,7},{7,6},{8,9},{9,8},{10,11... | collective-permute-start | bytes 786440 | tf_op jit(solution)/shard_map/ppermute | solution.py:80
  30.1 5.9 %collective-permute-start.10 = (bf16[256,512]{1,0:T(8,128)(2,1)S(1)}, bf16[256,512]{1,0:T(8,128)(2,1)}, u32[]{:S(2)}, u32[]{:S(2)}) collective-permute-start(bf16[256,512]{1,0:T(8,128)(2,1)S(1)} %collective-permute-done.2.refs_3_), channel_id=1, source_target_pairs={{0,1},{1,0},{2,3},{3,2},{4,5},{5,4},{6,7},{7,6},{8,9},{9,8},{10,11... | collective-permute-start | bytes 786440 | tf_op jit(solution)/shard_map/ppermute | solution.py:80
  32.9 3.0 %collective-permute-start.14 = (bf16[256,512]{1,0:T(8,128)(2,1)S(1)}, bf16[256,512]{1,0:T(8,128)(2,1)}, u32[]{:S(2)}, u32[]{:S(2)}) collective-permute-start(bf16[256,512]{1,0:T(8,128)(2,1)S(1)} %collective-permute-done.6.refs_7_), channel_id=1, source_target_pairs={{0,1},{1,0},{2,3},{3,2},{4,5},{5,4},{6,7},{7,6},{8,9},{9,8},{10,11... | collective-permute-start | bytes 786440 | tf_op jit(solution)/shard_map/ppermute | solution.py:80
  (9 other events, 59.5 us)

commit v2 on v1

--- a/solution.py
+++ b/solution.py
@@ -40,30 +40,75 @@
     return ((label & 1) << 1) | (label >> 1)
 
 
-def multiply_kernel(place, pairs, *refs, width):
-    blocks, v_all, out, held, sems = refs[:16], refs[16], refs[17], refs[18], refs[19]
-    row, col = place[0], place[1]
+def met_offsets(part, slot):
+    met = set()
+    for row in range(4):
+        for col in range(4):
+            owner = col ^ part
+            step = swapped(slot) if owner & 1 else slot
+            met.add((((row ^ step) + owner - row) & 3) ^ col)
+    return sorted(met)
+
+
+def multiply_kernel(pairs, *refs, parts, width):
+    count = 4 * len(parts)
+    blocks, pieces = refs[:count], refs[count : count + 4]
+    out, sums, sems = refs[-3:]
+    row, col = lax.axis_index("row"), lax.axis_index("col")
     copies = []
-    for part, offset in enumerate((0, 2, 1, 3)):
-        owner = col ^ offset
-        held[part] = jnp.zeros(held.shape[1:], held.dtype)
+    for index, part in enumerate(parts):
+        owner = col ^ part
+        sums[index] = jnp.zeros(sums.shape[1:], sums.dtype)
         for slot in range(4):
             step = jnp.where((owner & 1) == 0, slot, swapped(slot))
             kind = ((row ^ step) + owner) & 3
             source = ((kind - row) & 3) ^ col
+            listed = pairs[owner, kind] != 0
+            for offset in met_offsets(part, slot):
 
-            @pl.when(pairs[owner, kind] != 0)
-            def _(part=part, slot=slot, source=source):
-                held[part] += jnp.dot(
-                    blocks[part * 4 + slot][...], v_all[source], preferred_element_type=jnp.float32
-                )
+                @pl.when(listed & (source == offset))
+                def _(index=index, slot=slot, offset=offset):
+                    sums[index] += jnp.dot(
+                        blocks[index * 4 + slot][...],
+                        pieces[offset][...],
+                        preferred_element_type=jnp.float32,
+                    )
 
         start = pl.multiple_of(owner * width, width)
-        copy = pltpu.make_async_copy(held.at[part], out.at[:, pl.ds(start, width)], sems.at[part])
+        copy = pltpu.make_async_copy(
+            sums.at[index], out.at[:, pl.ds(start, width)], sems.at[index]
+        )
         copy.start()
         copies.append(copy)
     for copy in copies:
         copy.wait()
+
+
+def multiply(block_list, blocks, pieces, parts, earlier, shape, cost):
+    anywhere = pl.BlockSpec(memory_space=pl.ANY)
+    vmem = pl.BlockSpec(memory_space=pltpu.VMEM)
+    width = pieces[0].shape[1]
+    operands = [block_list, *blocks, *pieces] + ([] if earlier is None else [earlier])
+    return pl.pallas_call(
+        functools.partial(multiply_kernel, parts=parts, width=width),
+        out_shape=jax.ShapeDtypeStruct(shape, jnp.float32),
+        in_specs=[pl.BlockSpec(memory_space=pltpu.SMEM)]
+        + [vmem] * (len(blocks) + len(pieces))
+        + ([] if earlier is None else [anywhere]),
+        out_specs=anywhere,
+        scratch_shapes=[
+            pltpu.VMEM((len(parts), shape[0], width), jnp.float32),
+            pltpu.SemaphoreType.DMA((len(parts),)),
+        ],
+        input_output_aliases={} if earlier is None else {len(operands) - 1: 0},
+        cost_estimate=pl.CostEstimate(flops=cost, transcendentals=0, bytes_accessed=2**20),
+        compiler_params=pltpu.CompilerParams(vmem_limit_bytes=16 * 2**20),
+        name="multiply",
+    )(*operands)
+
+
+def after(value, *others):
+    return lax.optimization_barrier((value,) + others)[0]
 
 
 def gather_shards(amps, ints, block_list):
@@ -91,30 +136,21 @@
     far0 = across(amps)
     near1 = first(amps)
     near2 = second(amps)
-    v2 = across(piece(2))
-    v3 = cross(piece(3))
+    v2 = across(after(piece(2), near1))
+    v3 = cross(after(piece(3), near1))
     near3 = second(near1)
-    v1 = beside(piece(1))
     far1 = first(far0)
-    far2 = second(far0)
+    far2 = second(after(far0, near3))
     far3 = second(far1)
-    own = [amps, near1, near2, near3, far0, far1, far2, far3]
-    blocks = own + [beside(b) for b in own]
-    v_all = jnp.stack([piece(0), v1, v2, v3])
-    place = jnp.stack([row_pos, col_pos]).astype(jnp.int32)
-    smem = pl.BlockSpec(memory_space=pltpu.SMEM)
-    vmem = pl.BlockSpec(memory_space=pltpu.VMEM)
-    out = pl.pallas_call(
-        functools.partial(multiply_kernel, width=width),
-        out_shape=jax.ShapeDtypeStruct((amps.shape[0], ints.shape[1]), jnp.float32),
-        in_specs=[smem, smem] + [vmem] * 17,
-        out_specs=pl.BlockSpec(memory_space=pl.ANY),
-        scratch_shapes=[
-            pltpu.VMEM((4, amps.shape[0], width), jnp.float32),
-            pltpu.SemaphoreType.DMA((4,)),
-        ],
-        name="multiply",
-    )(place, block_list, *blocks, v_all)
+    pieces = [piece(0), beside(piece(1)), v2, v3]
+    near = [amps, near1, near2, near3]
+    far = [far0, far1, far2, far3]
+    shape = (amps.shape[0], ints.shape[1])
+    cost = 4 * 2 * amps.shape[0] * amps.shape[1] * width
+    near += [beside(b) for b in near]
+    far += [beside(b) for b in far]
+    out = multiply(block_list, near, pieces, (0, 1), None, shape, 1 * cost)
+    out = multiply(block_list, far, pieces, (2, 3), out, shape, cost)
     return out[None]
 
 

time: 42.1 us -> 33.9 us (0.81)
  the two profiles are of different devices: /device:TPU:0 before, /device:TPU:15 now
where the time goes in v2:
time: 33.9 us; the launch traced here: 33.7 us
  starting transfers between devices  17.7 us (52%)
  waiting for transfers between devices  9.87 us (29%)
  Pallas kernels  4.7 us (14%)
  local copies, waits for them, and re-layouts  1.32 us (4%)
    ppermute x18, starting transfers between devices, moved(): return lax.ppermute(block, GRID, route)  17.7 us
    ppermute x18, waiting for transfers between devices, moved(): return lax.ppermute(block, GRID, route)  9.87 us
    pallas_call x2, Pallas kernels, multiply(): pl.pallas_call(functools.partial(multiply_kernel, parts=parts, width=widt...  4.7 us
    dynamic_slice x1, local copies, waits for them, and re-layouts, piece(): return lax.dynamic_slice_in_dim(ints, (col_pos ^ offset) * width, width, 1)  1.31 us
  transfers between devices with their start and end apart: 18, of which 7 were waited for; matrix products, arithmetic and copies ran while one was open for 4% of the time, Pallas kernels for 7%

profile of v2, /device:TPU:15, one launch (start us, length us, event | category | flops | bytes accessed | tf_op | source)
XLA Modules:
  0.0 33.7 jit_solution(9153399053173250911)
XLA Ops:
  0.0 0.2 collective-permute-start.2
  0.2 1.3 %constant_dynamic-slice_fusion = (bf16[512,256]{1,0:T(8,128)(2,1)S(1)}, bf16[512,256]{1,0:T(8,128)(2,1)S(1)}, bf16[512,256]{1,0:T(8,128)(2,1)S(1)}, bf16[512,256]{1,0:T(8,128)(2,1)S(1)}) fusion(bf16[512,1024]{1,0:T(8,128)(2,1)} %param.4, s32[]{:T(128)S(6)} %select_n.15, s32[]{:T(128)S(6)} %select_n.13, s32[]{:T(128)S(6)} %select_n.12, s32[]{:T(128)S(6)} %select_n.14), kind=kLoop, calls=%fused_computation | loop fusion | bytes 2097168 | tf_op jit(solution)/shard_map/dynamic_slice | solution.py:134
  1.5 1.1 %collective-permute-start.10 = (bf16[512,256]{1,0:T(8,128)(2,1)S(1)}, bf16[512,256]{1,0:T(8,128)(2,1)S(1)}, u32[]{:S(2)}, u32[]{:S(2)}) collective-permute-start(bf16[512,256]{1,0:T(8,128)(2,1)S(1)} %get-tuple-element.12), channel_id=1, source_target_pairs={{0,1},{1,0},{2,3},{3,2},{4,5},{5,4},{6,7},{7,6},{8,9},{9,8},{10,11... | collective-permute-start | bytes 786440 | tf_op jit(solution)/shard_map/ppermute | solution.py:125
  2.6 0.3 collective-permute-start
  2.8 2.9 %collective-permute-done.2.refs_1_ = bf16[256,512]{1,0:T(8,128)(2,1)S(1)} collective-permute-done((bf16[256,512]{1,0:T(8,128)(2,1)}, bf16[256,512]{1,0:T(8,128)(2,1)S(1)}, u32[]{:S(2)}, u32[]{:S(2)}) %collective-permute-start.2) | collective-permute-done | bytes 262176 | tf_op jit(solution)/shard_map/ppermute | solution.py:125
  5.7 0.2 collective-permute-start.3
  6.0 1.2 %collective-permute-start.13 = (bf16[256,512]{1,0:T(8,128)(2,1)S(1)}, bf16[256,512]{1,0:T(8,128)(2,1)S(1)}, u32[]{:S(2)}, u32[]{:S(2)}) collective-permute-start(bf16[256,512]{1,0:T(8,128)(2,1)S(1)} %copy-done), channel_id=1, source_target_pairs={{0,8},{1,5},{2,10},{3,7},{4,12},{5,1},{6,14},{7,3},{8,0},{9,13},{1... | collective-permute-start | bytes 786440 | tf_op jit(solution)/shard_map/ppermute | solution.py:125
  7.2 2.1 %collective-permute-start.14 = (bf16[256,512]{1,0:T(8,128)(2,1)S(1)}, bf16[256,512]{1,0:T(8,128)(2,1)S(1)}, u32[]{:S(2)}, u32[]{:S(2)}) collective-permute-start(bf16[256,512]{1,0:T(8,128)(2,1)S(1)} %copy-done), channel_id=1, source_target_pairs={{0,1},{1,0},{2,3},{3,2},{4,5},{5,4},{6,7},{7,6},{8,9},{9,8},{10,11... | collective-permute-start | bytes 786440 | tf_op jit(solution)/shard_map/ppermute | solution.py:125
  9.3 0.3 collective-permute-start.11
  9.5 0.9 %collective-permute-done.refs_0_ = bf16[256,512]{1,0:T(8,128)(2,1)S(1)} collective-permute-done((bf16[256,512]{1,0:T(8,128)(2,1)S(1)}, bf16[256,512]{1,0:T(8,128)(2,1)S(1)}, u32[]{:S(2)}, u32[]{:S(2)}) %collective-permute-start) | collective-permute-done | bytes 262176 | tf_op jit(solution)/shard_map/ppermute | solution.py:125
  10.4 0.8 %collective-permute-done.3.refs_3_ = bf16[256,512]{1,0:T(8,128)(2,1)S(1)} collective-permute-done((bf16[256,512]{1,0:T(8,128)(2,1)S(1)}, bf16[256,512]{1,0:T(8,128)(2,1)S(1)}, u32[]{:S(2)}, u32[]{:S(2)}) %collective-permute-start.3) | collective-permute-done | bytes 262176 | tf_op jit(solution)/shard_map/ppermute | solution.py:125
  11.2 2.5 %collective-permute-start.12 = (bf16[512,256]{1,0:T(8,128)(2,1)S(1)}, bf16[512,256]{1,0:T(8,128)(2,1)S(1)}, u32[]{:S(2)}, u32[]{:S(2)}) collective-permute-start(bf16[512,256]{1,0:T(8,128)(2,1)S(1)} %get-tuple-element.10), channel_id=1, source_target_pairs={{0,3},{1,2},{2,1},{3,0},{4,7},{5,6},{6,5},{7,4},{8,11},{9,10},{10,... | collective-permute-start | bytes 786440 | tf_op jit(solution)/shard_map/ppermute | solution.py:125
  13.8 0.3 collective-permute-done.13.refs_2_
  14.1 5.2 %collective-permute-start.15 = (bf16[256,512]{1,0:T(8,128)(2,1)S(1)}, bf16[256,512]{1,0:T(8,128)(2,1)S(1)}, u32[]{:S(2)}, u32[]{:S(2)}) collective-permute-start(bf16[256,512]{1,0:T(8,128)(2,1)S(1)} %collective-permute-done.2.refs_1_), channel_id=1, source_target_pairs={{0,1},{1,0},{2,3},{3,2},{4,5},{5,4},{6,7},{7,6},{8,9},{9,8},{10,11... | collective-permute-start | bytes 786440 | tf_op jit(solution)/shard_map/ppermute | solution.py:125
  19.3 0.1 collective-permute-start.4
  19.4 1.4 %collective-permute-start.5 = (bf16[256,512]{1,0:T(8,128)(2,1)S(1)}, bf16[256,512]{1,0:T(8,128)(2,1)S(1)}, u32[]{:S(2)}, u32[]{:S(2)}) collective-permute-start(bf16[256,512]{1,0:T(8,128)(2,1)S(1)} %collective-permute-done.1.refs_1_), channel_id=1, source_target_pairs={{0,8},{1,5},{2,10},{3,7},{4,12},{5,1},{6,14},{7,3},{8,0},{9,13},{1... | collective-permute-start | bytes 786440 | tf_op jit(solution)/shard_map/ppermute | solution.py:125
  20.8 2.4 %collective-permute-done.12.refs_11_ = bf16[512,256]{1,0:T(8,128)(2,1)S(1)} collective-permute-done((bf16[512,256]{1,0:T(8,128)(2,1)S(1)}, bf16[512,256]{1,0:T(8,128)(2,1)S(1)}, u32[]{:S(2)}, u32[]{:S(2)}) %collective-permute-start.12) | collective-permute-done | bytes 262176 | tf_op jit(solution)/shard_map/ppermute | solution.py:125
  23.2 0.5 %collective-permute-start.6 = (bf16[256,512]{1,0:T(8,128)(2,1)S(1)}, bf16[256,512]{1,0:T(8,128)(2,1)S(1)}, u32[]{:S(2)}, u32[]{:S(2)}) collective-permute-start(bf16[256,512]{1,0:T(8,128)(2,1)S(1)} %collective-permute-done.refs_0_), channel_id=1, source_target_pairs={{0,1},{1,0},{2,3},{3,2},{4,5},{5,4},{6,7},{7,6},{8,9},{9,8},{10,11... | collective-permute-start | bytes 786440 | tf_op jit(solution)/shard_map/ppermute | solution.py:125
  23.8 1.0 %collective-permute-done.4.refs_2_ = bf16[256,512]{1,0:T(8,128)(2,1)S(1)} collective-permute-done((bf16[256,512]{1,0:T(8,128)(2,1)S(1)}, bf16[256,512]{1,0:T(8,128)(2,1)S(1)}, u32[]{:S(2)}, u32[]{:S(2)}) %collective-permute-start.4) | collective-permute-done | bytes 262176 | tf_op jit(solution)/shard_map/ppermute | solution.py:125
  24.8 1.3 %collective-permute-start.8 = (bf16[256,512]{1,0:T(8,128)(2,1)S(1)}, bf16[256,512]{1,0:T(8,128)(2,1)S(1)}, u32[]{:S(2)}, u32[]{:S(2)}) collective-permute-start(bf16[256,512]{1,0:T(8,128)(2,1)S(1)} %collective-permute-done.4.refs_2_), channel_id=1, source_target_pairs={{0,1},{1,0},{2,3},{3,2},{4,5},{5,4},{6,7},{7,6},{8,9},{9,8},{10,11... | collective-permute-start | bytes 786440 | tf_op jit(solution)/shard_map/ppermute | solution.py:125
  26.1 1.5 %collective-permute-done.5.refs_3_ = bf16[256,512]{1,0:T(8,128)(2,1)S(1)} collective-permute-done((bf16[256,512]{1,0:T(8,128)(2,1)S(1)}, bf16[256,512]{1,0:T(8,128)(2,1)S(1)}, u32[]{:S(2)}, u32[]{:S(2)}) %collective-permute-start.5) | collective-permute-done | bytes 262176 | tf_op jit(solution)/shard_map/ppermute | solution.py:125
  27.7 1.3 %collective-permute-start.9 = (bf16[256,512]{1,0:T(8,128)(2,1)S(1)}, bf16[256,512]{1,0:T(8,128)(2,1)S(1)}, u32[]{:S(2)}, u32[]{:S(2)}) collective-permute-start(bf16[256,512]{1,0:T(8,128)(2,1)S(1)} %collective-permute-done.5.refs_3_), channel_id=1, source_target_pairs={{0,1},{1,0},{2,3},{3,2},{4,5},{5,4},{6,7},{7,6},{8,9},{9,8},{10,11... | collective-permute-start | bytes 786440 | tf_op jit(solution)/shard_map/ppermute | solution.py:125
  29.0 2.3 %multiply.2.refs_12_ = f32[256,1024]{1,0:T(8,128)} custom-call(s32[4,4]{1,0:T(4,128)S(1)} %copy-done.1, bf16[256,512]{1,0:T(8,128)(2,1)S(1)} %copy-done, bf16[256,512]{1,0:T(8,128)(2,1)S(1)} %collective-permute-done.2.refs_1_, bf16[256,512]{1,0:T(8,128)(2,1)S(1)} %collective-permute-done.13.refs_2_, bf16[256,512]{1,0:T(8,128)(2,1)S(1)} %collective-permute-done.3.refs_3_, ...), custom_call_target="tpu_custom_call" | custom-call | flops 268435456 | bytes 1048576 | tf_op jit(solution)/shard_map/multiply/pallas_call | solution.py:92
  31.3 2.4 %multiply.3 = f32[256,1024]{1,0:T(8,128)} custom-call(s32[4,4]{1,0:T(4,128)S(1)} %copy-done.1, bf16[256,512]{1,0:T(8,128)(2,1)S(1)} %collective-permute-done.refs_0_, bf16[256,512]{1,0:T(8,128)(2,1)S(1)} %collective-permute-done.1.refs_1_, bf16[256,512]{1,0:T(8,128)(2,1)S(1)} %collective-permute-done.4.refs_2_, ...), custom_call_target="tpu_custom_call", output_to_operand_aliasing={{}: (13, {})} | custom-call | flops 268435456 | bytes 1048576 | tf_op jit(solution)/shard_map/multiply/pallas_call | solution.py:92
  (19 shorter events, 0.1 us)
Async XLA Ops:
  0.0 5.7 %collective-permute-start.2 = (bf16[256,512]{1,0:T(8,128)(2,1)}, bf16[256,512]{1,0:T(8,128)(2,1)S(1)}, u32[]{:S(2)}, u32[]{:S(2)}) collective-permute-start(bf16[256,512]{1,0:T(8,128)(2,1)} %refs_0_.1), channel_id=1, source_target_pairs={{0,4},{1,9},{2,6},{3,11},{4,0},{5,13},{6,2},{7,15},{8,12},{9,1},{1... | collective-permute-start | bytes 786440 | tf_op jit(solution)/shard_map/ppermute | solution.py:125
  0.2 2.4 %copy-start = (bf16[256,512]{1,0:T(8,128)(2,1)S(1)}, bf16[256,512]{1,0:T(8,128)(2,1)}, u32[]{:S(2)}) copy-start(bf16[256,512]{1,0:T(8,128)(2,1)} %refs_0_.1) | copy-start | bytes 786436
  1.5 7.8 %collective-permute-start.10 = (bf16[512,256]{1,0:T(8,128)(2,1)S(1)}, bf16[512,256]{1,0:T(8,128)(2,1)S(1)}, u32[]{:S(2)}, u32[]{:S(2)}) collective-permute-start(bf16[512,256]{1,0:T(8,128)(2,1)S(1)} %get-tuple-element.12), channel_id=1, source_target_pairs={{0,1},{1,0},{2,3},{3,2},{4,5},{5,4},{6,7},{7,6},{8,9},{9,8},{10,11... | collective-permute-start | bytes 786440 | tf_op jit(solution)/shard_map/ppermute | solution.py:125
  2.6 7.9 %collective-permute-start = (bf16[256,512]{1,0:T(8,128)(2,1)S(1)}, bf16[256,512]{1,0:T(8,128)(2,1)S(1)}, u32[]{:S(2)}, u32[]{:S(2)}) collective-permute-start(bf16[256,512]{1,0:T(8,128)(2,1)S(1)} %copy-done), channel_id=1, source_target_pairs={{0,2},{1,3},{2,0},{3,1},{4,6},{5,7},{6,4},{7,5},{8,10},{9,11},{10,... | collective-permute-start | bytes 786440 | tf_op jit(solution)/shard_map/ppermute | solution.py:125
  5.7 5.5 %collective-permute-start.3 = (bf16[256,512]{1,0:T(8,128)(2,1)S(1)}, bf16[256,512]{1,0:T(8,128)(2,1)S(1)}, u32[]{:S(2)}, u32[]{:S(2)}) collective-permute-start(bf16[256,512]{1,0:T(8,128)(2,1)S(1)} %collective-permute-done.2.refs_1_), channel_id=1, source_target_pairs={{0,8},{1,5},{2,10},{3,7},{4,12},{5,1},{6,14},{7,3},{8,0},{9,13},{1... | collective-permute-start | bytes 786440 | tf_op jit(solution)/shard_map/ppermute | solution.py:125
  6.0 8.1 %collective-permute-start.13 = (bf16[256,512]{1,0:T(8,128)(2,1)S(1)}, bf16[256,512]{1,0:T(8,128)(2,1)S(1)}, u32[]{:S(2)}, u32[]{:S(2)}) collective-permute-start(bf16[256,512]{1,0:T(8,128)(2,1)S(1)} %copy-done), channel_id=1, source_target_pairs={{0,8},{1,5},{2,10},{3,7},{4,12},{5,1},{6,14},{7,3},{8,0},{9,13},{1... | collective-permute-start | bytes 786440 | tf_op jit(solution)/shard_map/ppermute | solution.py:125
  7.2 12.1 %collective-permute-start.14 = (bf16[256,512]{1,0:T(8,128)(2,1)S(1)}, bf16[256,512]{1,0:T(8,128)(2,1)S(1)}, u32[]{:S(2)}, u32[]{:S(2)}) collective-permute-start(bf16[256,512]{1,0:T(8,128)(2,1)S(1)} %copy-done), channel_id=1, source_target_pairs={{0,1},{1,0},{2,3},{3,2},{4,5},{5,4},{6,7},{7,6},{8,9},{9,8},{10,11... | collective-permute-start | bytes 786440 | tf_op jit(solution)/shard_map/ppermute | solution.py:125
  9.3 19.7 %copy-start.1 = (s32[4,4]{1,0:T(4,128)S(1)}, s32[4,4]{1,0:T(4,128)}, u32[]{:S(2)}) copy-start(s32[4,4]{1,0:T(4,128)} %pairs.3) | copy-start | bytes 196
  9.3 10.0 %collective-permute-start.11 = (bf16[512,256]{1,0:T(8,128)(2,1)S(1)}, bf16[512,256]{1,0:T(8,128)(2,1)S(1)}, u32[]{:S(2)}, u32[]{:S(2)}) collective-permute-start(bf16[512,256]{1,0:T(8,128)(2,1)S(1)} %get-tuple-element.9), channel_id=1, source_target_pairs={{0,2},{1,3},{2,0},{3,1},{4,6},{5,7},{6,4},{7,5},{8,10},{9,11},{10,... | collective-permute-start | bytes 786440 | tf_op jit(solution)/shard_map/ppermute | solution.py:125
  10.4 8.9 %collective-permute-start.1 = (bf16[256,512]{1,0:T(8,128)(2,1)S(1)}, bf16[256,512]{1,0:T(8,128)(2,1)S(1)}, u32[]{:S(2)}, u32[]{:S(2)}) collective-permute-start(bf16[256,512]{1,0:T(8,128)(2,1)S(1)} %collective-permute-done.refs_0_), channel_id=1, source_target_pairs={{0,4},{1,9},{2,6},{3,11},{4,0},{5,13},{6,2},{7,15},{8,12},{9,1},{1... | collective-permute-start | bytes 786440 | tf_op jit(solution)/shard_map/ppermute | solution.py:125
  11.2 12.0 %collective-permute-start.12 = (bf16[512,256]{1,0:T(8,128)(2,1)S(1)}, bf16[512,256]{1,0:T(8,128)(2,1)S(1)}, u32[]{:S(2)}, u32[]{:S(2)}) collective-permute-start(bf16[512,256]{1,0:T(8,128)(2,1)S(1)} %get-tuple-element.10), channel_id=1, source_target_pairs={{0,3},{1,2},{2,1},{3,0},{4,7},{5,6},{6,5},{7,4},{8,11},{9,10},{10,... | collective-permute-start | bytes 786440 | tf_op jit(solution)/shard_map/ppermute | solution.py:125
  14.1 9.2 %collective-permute-start.15 = (bf16[256,512]{1,0:T(8,128)(2,1)S(1)}, bf16[256,512]{1,0:T(8,128)(2,1)S(1)}, u32[]{:S(2)}, u32[]{:S(2)}) collective-permute-start(bf16[256,512]{1,0:T(8,128)(2,1)S(1)} %collective-permute-done.2.refs_1_), channel_id=1, source_target_pairs={{0,1},{1,0},{2,3},{3,2},{4,5},{5,4},{6,7},{7,6},{8,9},{9,8},{10,11... | collective-permute-start | bytes 786440 | tf_op jit(solution)/shard_map/ppermute | solution.py:125
  19.3 4.5 %collective-permute-start.16 = (bf16[256,512]{1,0:T(8,128)(2,1)S(1)}, bf16[256,512]{1,0:T(8,128)(2,1)S(1)}, u32[]{:S(2)}, u32[]{:S(2)}) collective-permute-start(bf16[256,512]{1,0:T(8,128)(2,1)S(1)} %collective-permute-done.13.refs_2_), channel_id=1, source_target_pairs={{0,1},{1,0},{2,3},{3,2},{4,5},{5,4},{6,7},{7,6},{8,9},{9,8},{10,11... | collective-permute-start | bytes 786440 | tf_op jit(solution)/shard_map/ppermute | solution.py:125
  19.3 5.6 %collective-permute-start.4 = (bf16[256,512]{1,0:T(8,128)(2,1)S(1)}, bf16[256,512]{1,0:T(8,128)(2,1)S(1)}, u32[]{:S(2)}, u32[]{:S(2)}) collective-permute-start(bf16[256,512]{1,0:T(8,128)(2,1)S(1)} %collective-permute-done.refs_0_), channel_id=1, source_target_pairs={{0,8},{1,5},{2,10},{3,7},{4,12},{5,1},{6,14},{7,3},{8,0},{9,13},{1... | collective-permute-start | bytes 786440 | tf_op jit(solution)/shard_map/ppermute | solution.py:125
  19.4 8.3 %collective-permute-start.5 = (bf16[256,512]{1,0:T(8,128)(2,1)S(1)}, bf16[256,512]{1,0:T(8,128)(2,1)S(1)}, u32[]{:S(2)}, u32[]{:S(2)}) collective-permute-start(bf16[256,512]{1,0:T(8,128)(2,1)S(1)} %collective-permute-done.1.refs_1_), channel_id=1, source_target_pairs={{0,8},{1,5},{2,10},{3,7},{4,12},{5,1},{6,14},{7,3},{8,0},{9,13},{1... | collective-permute-start | bytes 786440 | tf_op jit(solution)/shard_map/ppermute | solution.py:125
  23.2 5.7 %collective-permute-start.17 = (bf16[256,512]{1,0:T(8,128)(2,1)S(1)}, bf16[256,512]{1,0:T(8,128)(2,1)S(1)}, u32[]{:S(2)}, u32[]{:S(2)}) collective-permute-start(bf16[256,512]{1,0:T(8,128)(2,1)S(1)} %collective-permute-done.3.refs_3_), channel_id=1, source_target_pairs={{0,1},{1,0},{2,3},{3,2},{4,5},{5,4},{6,7},{7,6},{8,9},{9,8},{10,11... | collective-permute-start | bytes 786440 | tf_op jit(solution)/shard_map/ppermute | solution.py:125
  23.2 8.1 %collective-permute-start.6 = (bf16[256,512]{1,0:T(8,128)(2,1)S(1)}, bf16[256,512]{1,0:T(8,128)(2,1)S(1)}, u32[]{:S(2)}, u32[]{:S(2)}) collective-permute-start(bf16[256,512]{1,0:T(8,128)(2,1)S(1)} %collective-permute-done.refs_0_), channel_id=1, source_target_pairs={{0,1},{1,0},{2,3},{3,2},{4,5},{5,4},{6,7},{7,6},{8,9},{9,8},{10,11... | collective-permute-start | bytes 786440 | tf_op jit(solution)/shard_map/ppermute | solution.py:125
  23.8 7.6 %collective-permute-start.7 = (bf16[256,512]{1,0:T(8,128)(2,1)S(1)}, bf16[256,512]{1,0:T(8,128)(2,1)S(1)}, u32[]{:S(2)}, u32[]{:S(2)}) collective-permute-start(bf16[256,512]{1,0:T(8,128)(2,1)S(1)} %collective-permute-done.1.refs_1_), channel_id=1, source_target_pairs={{0,1},{1,0},{2,3},{3,2},{4,5},{5,4},{6,7},{7,6},{8,9},{9,8},{10,11... | collective-permute-start | bytes 786440 | tf_op jit(solution)/shard_map/ppermute | solution.py:125
  24.8 6.5 %collective-permute-start.8 = (bf16[256,512]{1,0:T(8,128)(2,1)S(1)}, bf16[256,512]{1,0:T(8,128)(2,1)S(1)}, u32[]{:S(2)}, u32[]{:S(2)}) collective-permute-start(bf16[256,512]{1,0:T(8,128)(2,1)S(1)} %collective-permute-done.4.refs_2_), channel_id=1, source_target_pairs={{0,1},{1,0},{2,3},{3,2},{4,5},{5,4},{6,7},{7,6},{8,9},{9,8},{10,11... | collective-permute-start | bytes 786440 | tf_op jit(solution)/shard_map/ppermute | solution.py:125
  27.7 3.7 %collective-permute-start.9 = (bf16[256,512]{1,0:T(8,128)(2,1)S(1)}, bf16[256,512]{1,0:T(8,128)(2,1)S(1)}, u32[]{:S(2)}, u32[]{:S(2)}) collective-permute-start(bf16[256,512]{1,0:T(8,128)(2,1)S(1)} %collective-permute-done.5.refs_3_), channel_id=1, source_target_pairs={{0,1},{1,0},{2,3},{3,2},{4,5},{5,4},{6,7},{7,6},{8,9},{9,8},{10,11... | collective-permute-start | bytes 786440 | tf_op jit(solution)/shard_map/ppermute | solution.py:125

commit v3 on v0

--- a/solution.py
+++ b/solution.py
@@ -1,7 +1,13 @@
+import functools
+
 import jax
 import jax.numpy as jnp
 from jax import lax
+from jax.experimental import pallas as pl
+from jax.experimental.pallas import tpu as pltpu
 from jax.sharding import PartitionSpec as P
+
+GRID = ("row", "col")
 
 
 def shifted(block, axis, distance):
@@ -10,7 +16,7 @@
     return lax.ppermute(block, axis, route)
 
 
-def shards(amps, ints, block_list):
+def shift_shards(amps, ints, block_list):
     row_pos = lax.axis_index("row")
     col_pos = lax.axis_index("col")
     col_count = lax.axis_size("col")
@@ -30,8 +36,135 @@
     return owned.reshape(1, owned.shape[0], owned.shape[1])
 
 
+def multiply_kernel(pairs, *refs, parts, width):
+    blocks, pieces, keep, send, sums = refs[:4], refs[4:6], refs[6], refs[7], refs[8]
+    row, col = lax.axis_index("row"), lax.axis_index("col")
+    mine = pl.multiple_of((col & 1) * width, width)
+    other = pl.multiple_of(width - mine, width)
+    for index, part in enumerate(parts):
+        owner = col ^ part
+        sums[...] = jnp.zeros(sums.shape, sums.dtype)
+        for slot in range(2):
+            kind = ((row ^ (2 * slot + (part & 1))) + owner) & 3
+            listed = pairs[owner, kind] != 0
+            here = kind == ((row + col) & 3)
+            for source in range(2):
+                if part & 1 == 0 and source != (slot ^ (part >> 1)):
+                    continue
+
+                @pl.when(listed & (here == (source == 0)))
+                def _(slot=slot, source=source, index=index):
+                    sums[...] += jnp.dot(
+                        blocks[2 * index + slot][...],
+                        pieces[source][...],
+                        preferred_element_type=jnp.float32,
+                    )
+
+        keep[index] = sums[:, pl.ds(mine, width)]
+        send[index] = sums[:, pl.ds(other, width)]
+
+
+def multiply(block_list, blocks, pieces, parts, cost):
+    vmem = pl.BlockSpec(memory_space=pltpu.VMEM)
+    rows, width = blocks[0].shape[0], pieces[0].shape[1] // 2
+    half = jax.ShapeDtypeStruct((2, rows, width), jnp.float32)
+    return pl.pallas_call(
+        functools.partial(multiply_kernel, parts=parts, width=width),
+        out_shape=(half, half),
+        in_specs=[pl.BlockSpec(memory_space=pltpu.SMEM)] + [vmem] * 6,
+        out_specs=(vmem, vmem),
+        scratch_shapes=[pltpu.VMEM((rows, 2 * width), jnp.float32)],
+        cost_estimate=pl.CostEstimate(flops=cost, transcendentals=0, bytes_accessed=2**20),
+        compiler_params=pltpu.CompilerParams(vmem_limit_bytes=8 * 2**20),
+        name="multiply",
+    )(block_list, *blocks, *pieces)
+
+
+def add_kernel(keep, received, *refs, parts):
+    out, held, sems = refs[-3:]
+    col = lax.axis_index("col")
+    copies = []
+    for index, part in enumerate(parts):
+        held[index] = keep[index] + received[1 - index]
+        start = pl.multiple_of((col ^ part) * held.shape[2], held.shape[2])
+        copy = pltpu.make_async_copy(
+            held.at[index], out.at[:, pl.ds(start, held.shape[2])], sems.at[index]
+        )
+        copy.start()
+        copies.append(copy)
+    for copy in copies:
+        copy.wait()
+
+
+def add(keep, received, parts, earlier, shape):
+    anywhere = pl.BlockSpec(memory_space=pl.ANY)
+    vmem = pl.BlockSpec(memory_space=pltpu.VMEM)
+    operands = [keep, received] + ([] if earlier is None else [earlier])
+    return pl.pallas_call(
+        functools.partial(add_kernel, parts=parts),
+        out_shape=jax.ShapeDtypeStruct(shape, jnp.float32),
+        in_specs=[vmem, vmem] + ([] if earlier is None else [anywhere]),
+        out_specs=anywhere,
+        scratch_shapes=[pltpu.VMEM(keep.shape, jnp.float32), pltpu.SemaphoreType.DMA((2,))],
+        input_output_aliases={} if earlier is None else {2: 0},
+        compiler_params=pltpu.CompilerParams(vmem_limit_bytes=8 * 2**20),
+        name="add",
+    )(*operands)
+
+
+def gather_shards(amps, ints, block_list):
+    rows, cols = lax.axis_size("row"), lax.axis_size("col")
+    row_pos, col_pos = lax.axis_index("row"), lax.axis_index("col")
+    width = ints.shape[1] // cols
+
+    def moved(block, target):
+        route = [
+            (r * cols + c, target(r, c)[0] * cols + target(r, c)[1])
+            for r in range(rows)
+            for c in range(cols)
+        ]
+        return lax.ppermute(block, GRID, route)
+
+    def turn(r, c):
+        return (r ^ 1, c ^ 1) if (r >> 1 ^ c) & 1 else (r ^ 2, c)
+
+    pair = functools.partial(moved, target=lambda r, c: (r ^ 2, c))
+    cross = functools.partial(moved, target=lambda r, c: (r ^ 1, c ^ 1))
+    across = functools.partial(moved, target=lambda r, c: (r, c ^ 2))
+    beside = functools.partial(moved, target=lambda r, c: (r, c ^ 1))
+    turns = ((row_pos >> 1) ^ col_pos) & 1 == 1
+
+    def last(by_pair, by_cross):
+        return moved(jnp.where(turns, by_pair, by_cross), turn)
+
+    def chip_columns(chip):
+        return lax.dynamic_slice_in_dim(ints, chip * 2 * width, 2 * width, 1)
+
+    chip = col_pos // 2
+    far0 = across(amps)
+    near1 = pair(amps)
+    near2 = cross(amps)
+    pieces = [chip_columns(chip), across(chip_columns(1 - chip))]
+    near3 = last(near1, near2)
+    far1 = pair(far0)
+    far2 = cross(far0)
+    far3 = last(far1, far2)
+    shape = (amps.shape[0], ints.shape[1])
+    cost = 4 * 2 * amps.shape[0] * amps.shape[1] * width
+    keep, send = multiply(block_list, [amps, near1, near2, near3], pieces, (0, 1), 30 * cost)
+    out = add(keep, beside(send), (0, 1), None, shape)
+    keep, send = multiply(block_list, [far0, far1, far2, far3], pieces, (2, 3), cost)
+    out = add(keep, beside(send), (2, 3), out, shape)
+    return out[None]
+
+
 def solution(mesh):
     placed = (P("col", "row"), P("col", "row"), P())
+    whole_gather = mesh.shape["col"] == 4 and mesh.shape["row"] % 4 == 0
     return jax.shard_map(
-        shards, mesh=mesh, in_specs=placed, out_specs=P(("row", "col"), None, None), check_vma=False
+        gather_shards if whole_gather else shift_shards,
+        mesh=mesh,
+        in_specs=placed,
+        out_specs=P(("row", "col"), None, None),
+        check_vma=False,
     )

time: 76.1 us -> 30.5 us (0.40)
  waiting for transfers between devices: 44.8 us -> 15.6 us
  blocking collectives: 17.1 us -> 0 us
  Pallas kernels: 0 us -> 4.32 us
  starting transfers between devices: 5.18 us -> 9.03 us
  matrix products: 3.08 us -> 0 us
  between operations: 2.66 us -> 0.08 us
  local copies, waits for them, and re-layouts: 3.07 us -> 1.28 us
    ppermute x6 -> x10, waiting for transfers between devices: 44.8 us -> 15.6 us  [moved(): return lax.ppermute(block, GRID, route)]
    all_to_all x1 -> x0, blocking collectives: 17.1 us -> none  [shards(): lax.all_to_all(running, 'col', split_axis=1, concat_axis=1, tiled=True)]
    pallas_call x0 -> x4, Pallas kernels: none -> 4.32 us  [the longest x2 2.65 us: multiply(): pl.pallas_call(functools.partial(multiply_kernel, parts=parts, width=widt...]
    ppermute x6 -> x10, starting transfers between devices: 5.18 us -> 9.03 us  [moved(): return lax.ppermute(block, GRID, route)]
    dot_general x4 -> x0, matrix products: 3.08 us -> none  [shards(): jnp.dot(held_amps, held_ints, preferred_element_type=jnp.float32)]
    reshape x1 -> x0, local copies, waits for them, and re-layouts: 1.31 us -> none  [shards(): return owned.reshape(1, owned.shape[0], owned.shape[1])]
  transfers between devices with their start and end apart: 6 -> 10, of which waited for: 4 -> 8; matrix products, arithmetic and copies ran while one was open for 4% -> 4% of each run, Pallas kernels for 0% -> 11%
where the time goes in v3:
time: 30.5 us; the launch traced here: 30.3 us
  waiting for transfers between devices  15.6 us (51%)
  starting transfers between devices  9.03 us (30%)
  Pallas kernels  4.32 us (14%)
  local copies, waits for them, and re-layouts  1.28 us (4%)
    ppermute x10, waiting for transfers between devices, moved(): return lax.ppermute(block, GRID, route)  15.6 us
    ppermute x10, starting transfers between devices, moved(): return lax.ppermute(block, GRID, route)  9.03 us
    pallas_call x2, Pallas kernels, multiply(): pl.pallas_call(functools.partial(multiply_kernel, parts=parts, width=widt...  2.65 us
    pallas_call x2, Pallas kernels, add(): pl.pallas_call(functools.partial(add_kernel, parts=parts), out_shape=jax....  1.67 us
    dynamic_slice x1, local copies, waits for them, and re-layouts, chip_columns(): return lax.dynamic_slice_in_dim(ints, chip * 2 * width, 2 * width, 1)  1.27 us
  transfers between devices with their start and end apart: 10, of which 8 were waited for; matrix products, arithmetic and copies ran while one was open for 4% of the time, Pallas kernels for 11%

profile of v3, /device:TPU:0, one launch (start us, length us, event | category | flops | bytes accessed | tf_op | source)
XLA Modules:
  0.0 30.3 jit_solution(5500565641750788358)
XLA Ops:
  0.0 2.9 %collective-permute-start = (bf16[256,512]{1,0:T(8,128)(2,1)}, bf16[256,512]{1,0:T(8,128)(2,1)S(1)}, u32[]{:S(2)}, u32[]{:S(2)}) collective-permute-start(bf16[256,512]{1,0:T(8,128)(2,1)} %refs_0_.1), channel_id=1, source_target_pairs={{0,2},{1,3},{2,0},{3,1},{4,6},{5,7},{6,4},{7,5},{8,10},{9,11},{10,... | collective-permute-start | bytes 786440 | tf_op jit(solution)/shard_map/ppermute | solution.py:126
  2.9 1.6 %collective-permute-start.6 = (bf16[256,512]{1,0:T(8,128)(2,1)}, bf16[256,512]{1,0:T(8,128)(2,1)S(1)}, u32[]{:S(2)}, u32[]{:S(2)}) collective-permute-start(bf16[256,512]{1,0:T(8,128)(2,1)} %refs_0_.1), channel_id=1, source_target_pairs={{0,8},{1,9},{2,10},{3,11},{4,12},{5,13},{6,14},{7,15},{8,0},{9,1},... | collective-permute-start | bytes 786440 | tf_op jit(solution)/shard_map/ppermute | solution.py:126
  4.5 0.4 %collective-permute-start.7 = (bf16[256,512]{1,0:T(8,128)(2,1)}, bf16[256,512]{1,0:T(8,128)(2,1)S(1)}, u32[]{:S(2)}, u32[]{:S(2)}) collective-permute-start(bf16[256,512]{1,0:T(8,128)(2,1)} %refs_0_.1), channel_id=1, source_target_pairs={{0,5},{1,4},{2,7},{3,6},{4,1},{5,0},{6,3},{7,2},{8,13},{9,12},{10,... | collective-permute-start | bytes 786440 | tf_op jit(solution)/shard_map/ppermute | solution.py:126
  4.9 1.3 %constant_dynamic-slice_fusion = (bf16[512,512]{1,0:T(8,128)(2,1)S(1)}, bf16[512,512]{1,0:T(8,128)(2,1)S(1)}) fusion(bf16[512,1024]{1,0:T(8,128)(2,1)} %param.4, s32[]{:T(128)S(6)} %select_n.27, s32[]{:T(128)S(6)} %select_n.26), kind=kLoop, calls=%fused_computation.2 | loop fusion | bytes 2097160 | tf_op jit(solution)/shard_map/dynamic_slice | solution.py:141
  6.2 0.6 %collective-permute-start.4 = (bf16[512,512]{1,0:T(8,128)(2,1)S(1)}, bf16[512,512]{1,0:T(8,128)(2,1)S(1)}, u32[]{:S(2)}, u32[]{:S(2)}) collective-permute-start(bf16[512,512]{1,0:T(8,128)(2,1)S(1)} %get-tuple-element.13), channel_id=1, source_target_pairs={{0,2},{1,3},{2,0},{3,1},{4,6},{5,7},{6,4},{7,5},{8,10},{9,11},{10,... | collective-permute-start | bytes 1572872 | tf_op jit(solution)/shard_map/ppermute | solution.py:126
  6.8 2.7 %collective-permute-done.refs_0_ = bf16[256,512]{1,0:T(8,128)(2,1)S(1)} collective-permute-done((bf16[256,512]{1,0:T(8,128)(2,1)}, bf16[256,512]{1,0:T(8,128)(2,1)S(1)}, u32[]{:S(2)}, u32[]{:S(2)}) %collective-permute-start) | collective-permute-done | bytes 262176 | tf_op jit(solution)/shard_map/ppermute | solution.py:126
  9.5 2.5 %collective-permute-start.1 = (bf16[256,512]{1,0:T(8,128)(2,1)S(1)}, bf16[256,512]{1,0:T(8,128)(2,1)S(1)}, u32[]{:S(2)}, u32[]{:S(2)}) collective-permute-start(bf16[256,512]{1,0:T(8,128)(2,1)S(1)} %collective-permute-done.refs_0_), channel_id=1, source_target_pairs={{0,8},{1,9},{2,10},{3,11},{4,12},{5,13},{6,14},{7,15},{8,0},{9,1},... | collective-permute-start | bytes 786440 | tf_op jit(solution)/shard_map/ppermute | solution.py:126
  12.0 1.3 %collective-permute-done.7.refs_2_ = bf16[256,512]{1,0:T(8,128)(2,1)S(1)} collective-permute-done((bf16[256,512]{1,0:T(8,128)(2,1)}, bf16[256,512]{1,0:T(8,128)(2,1)S(1)}, u32[]{:S(2)}, u32[]{:S(2)}) %collective-permute-start.7) | collective-permute-done | bytes 262176 | tf_op jit(solution)/shard_map/ppermute | solution.py:126
  13.3 0.0 copy-start
  13.3 0.0 copy-start.1
  13.3 0.5 %collective-permute-start.8 = (bf16[256,512]{1,0:T(8,128)(2,1)S(1)}, bf16[256,512]{1,0:T(8,128)(2,1)S(1)}, u32[]{:S(2)}, u32[]{:S(2)}) collective-permute-start(bf16[256,512]{1,0:T(8,128)(2,1)S(1)} %broadcast_select_fusion), channel_id=1, source_target_pairs={{0,8},{1,4},{2,10},{3,6},{4,12},{5,0},{6,14},{7,2},{8,13},{9,1},{1... | collective-permute-start | bytes 786440 | tf_op jit(solution)/shard_map/ppermute | solution.py:126
  13.8 3.2 %collective-permute-done.1.refs_1_ = bf16[256,512]{1,0:T(8,128)(2,1)S(1)} collective-permute-done((bf16[256,512]{1,0:T(8,128)(2,1)S(1)}, bf16[256,512]{1,0:T(8,128)(2,1)S(1)}, u32[]{:S(2)}, u32[]{:S(2)}) %collective-permute-start.1) | collective-permute-done | bytes 262176 | tf_op jit(solution)/shard_map/ppermute | solution.py:126
  17.0 3.1 %collective-permute-done.2.refs_2_ = bf16[256,512]{1,0:T(8,128)(2,1)S(1)} collective-permute-done((bf16[256,512]{1,0:T(8,128)(2,1)S(1)}, bf16[256,512]{1,0:T(8,128)(2,1)S(1)}, u32[]{:S(2)}, u32[]{:S(2)}) %collective-permute-start.2) | collective-permute-done | bytes 262176 | tf_op jit(solution)/shard_map/ppermute | solution.py:126
  20.1 0.1 collective-permute-start.3
  20.2 0.6 %collective-permute-done.4.refs_5_ = bf16[512,512]{1,0:T(8,128)(2,1)S(1)} collective-permute-done((bf16[512,512]{1,0:T(8,128)(2,1)S(1)}, bf16[512,512]{1,0:T(8,128)(2,1)S(1)}, u32[]{:S(2)}, u32[]{:S(2)}) %collective-permute-start.4) | collective-permute-done | bytes 524320 | tf_op jit(solution)/shard_map/ppermute | solution.py:126
  20.8 2.6 %collective-permute-done.8.refs_3_ = bf16[256,512]{1,0:T(8,128)(2,1)S(1)} collective-permute-done((bf16[256,512]{1,0:T(8,128)(2,1)S(1)}, bf16[256,512]{1,0:T(8,128)(2,1)S(1)}, u32[]{:S(2)}, u32[]{:S(2)}) %collective-permute-start.8) | collective-permute-done | bytes 262176 | tf_op jit(solution)/shard_map/ppermute | solution.py:126
  23.4 1.3 %multiply.7 = (f32[2,256,256]{2,1,0:T(8,128)S(1)}, f32[2,256,256]{2,1,0:T(8,128)S(1)}) custom-call(s32[4,4]{1,0:T(4,128)S(1)} %copy-done, bf16[256,512]{1,0:T(8,128)(2,1)S(1)} %copy-done.1, bf16[256,512]{1,0:T(8,128)(2,1)S(1)} %collective-permute-done.6.refs_1_, bf16[256,512]{1,0:T(8,128)(2,1)S(1)} %collective-permute-done.7.refs_2_, ...), custom_call_target="tpu_custom_call" | custom-call | flops 8053063680 | bytes 1048576 | tf_op jit(solution)/shard_map/multiply/pallas_call | solution.py:71
  24.7 0.1 collective-permute-start.9
  24.8 1.4 %collective-permute-done.3.refs_3_ = bf16[256,512]{1,0:T(8,128)(2,1)S(1)} collective-permute-done((bf16[256,512]{1,0:T(8,128)(2,1)S(1)}, bf16[256,512]{1,0:T(8,128)(2,1)S(1)}, u32[]{:S(2)}, u32[]{:S(2)}) %collective-permute-start.3) | collective-permute-done | bytes 262176 | tf_op jit(solution)/shard_map/ppermute | solution.py:126
  26.2 1.3 %multiply.6 = (f32[2,256,256]{2,1,0:T(8,128)S(1)}, f32[2,256,256]{2,1,0:T(8,128)S(1)}) custom-call(s32[4,4]{1,0:T(4,128)S(1)} %copy-done, bf16[256,512]{1,0:T(8,128)(2,1)S(1)} %collective-permute-done.refs_0_, bf16[256,512]{1,0:T(8,128)(2,1)S(1)} %collective-permute-done.1.refs_1_, bf16[256,512]{1,0:T(8,128)(2,1)S(1)} %collective-permute-done.2.refs_2_, ...), custom_call_target="tpu_custom_call" | custom-call | flops 268435456 | bytes 1048576 | tf_op jit(solution)/shard_map/multiply/pallas_call | solution.py:71
  27.5 0.4 %collective-permute-start.5 = (f32[2,256,256]{2,1,0:T(8,128)S(1)}, f32[2,256,256]{2,1,0:T(8,128)S(1)}, u32[]{:S(2)}, u32[]{:S(2)}) collective-permute-start(f32[2,256,256]{2,1,0:T(8,128)S(1)} %get-tuple-element.10), channel_id=1, source_target_pairs={{0,1},{1,0},{2,3},{3,2},{4,5},{5,4},{6,7},{7,6},{8,9},{9,8},{10,11... | collective-permute-start | bytes 1572872 | tf_op jit(solution)/shard_map/ppermute | solution.py:126
  27.9 0.8 %add.11.refs_0_ = f32[256,1024]{1,0:T(8,128)} custom-call(f32[2,256,256]{2,1,0:T(8,128)S(1)} %get-tuple-element.11.keep, f32[2,256,256]{2,1,0:T(8,128)S(1)} %collective-permute-done.9.received), custom_call_target="tpu_custom_call" | custom-call | tf_op jit(solution)/shard_map/add/pallas_call | solution.py:103
  28.7 0.8 %collective-permute-done.5.received = f32[2,256,256]{2,1,0:T(8,128)S(1)} collective-permute-done((f32[2,256,256]{2,1,0:T(8,128)S(1)}, f32[2,256,256]{2,1,0:T(8,128)S(1)}, u32[]{:S(2)}, u32[]{:S(2)}) %collective-permute-start.5) | collective-permute-done | bytes 524320 | tf_op jit(solution)/shard_map/ppermute | solution.py:126
  29.5 0.8 %add.12 = f32[256,1024]{1,0:T(8,128)} custom-call(f32[2,256,256]{2,1,0:T(8,128)S(1)} %get-tuple-element.9.keep, f32[2,256,256]{2,1,0:T(8,128)S(1)} %collective-permute-done.5.received, f32[256,1024]{1,0:T(8,128)} %add.11.refs_0_), custom_call_target="tpu_custom_call", output_to_operand_aliasing={{}: (2, {})} | custom-call | tf_op jit(solution)/shard_map/add/pallas_call | solution.py:103
  (7 shorter events, 0.1 us)
Async XLA Ops:
  0.0 9.5 %collective-permute-start = (bf16[256,512]{1,0:T(8,128)(2,1)}, bf16[256,512]{1,0:T(8,128)(2,1)S(1)}, u32[]{:S(2)}, u32[]{:S(2)}) collective-permute-start(bf16[256,512]{1,0:T(8,128)(2,1)} %refs_0_.1), channel_id=1, source_target_pairs={{0,2},{1,3},{2,0},{3,1},{4,6},{5,7},{6,4},{7,5},{8,10},{9,11},{10,... | collective-permute-start | bytes 786440 | tf_op jit(solution)/shard_map/ppermute | solution.py:126
  2.9 9.0 %collective-permute-start.6 = (bf16[256,512]{1,0:T(8,128)(2,1)}, bf16[256,512]{1,0:T(8,128)(2,1)S(1)}, u32[]{:S(2)}, u32[]{:S(2)}) collective-permute-start(bf16[256,512]{1,0:T(8,128)(2,1)} %refs_0_.1), channel_id=1, source_target_pairs={{0,8},{1,9},{2,10},{3,11},{4,12},{5,13},{6,14},{7,15},{8,0},{9,1},... | collective-permute-start | bytes 786440 | tf_op jit(solution)/shard_map/ppermute | solution.py:126
  4.5 8.7 %collective-permute-start.7 = (bf16[256,512]{1,0:T(8,128)(2,1)}, bf16[256,512]{1,0:T(8,128)(2,1)S(1)}, u32[]{:S(2)}, u32[]{:S(2)}) collective-permute-start(bf16[256,512]{1,0:T(8,128)(2,1)} %refs_0_.1), channel_id=1, source_target_pairs={{0,5},{1,4},{2,7},{3,6},{4,1},{5,0},{6,3},{7,2},{8,13},{9,12},{10,... | collective-permute-start | bytes 786440 | tf_op jit(solution)/shard_map/ppermute | solution.py:126
  6.2 14.6 %collective-permute-start.4 = (bf16[512,512]{1,0:T(8,128)(2,1)S(1)}, bf16[512,512]{1,0:T(8,128)(2,1)S(1)}, u32[]{:S(2)}, u32[]{:S(2)}) collective-permute-start(bf16[512,512]{1,0:T(8,128)(2,1)S(1)} %get-tuple-element.13), channel_id=1, source_target_pairs={{0,2},{1,3},{2,0},{3,1},{4,6},{5,7},{6,4},{7,5},{8,10},{9,11},{10,... | collective-permute-start | bytes 1572872 | tf_op jit(solution)/shard_map/ppermute | solution.py:126
  9.5 7.6 %collective-permute-start.1 = (bf16[256,512]{1,0:T(8,128)(2,1)S(1)}, bf16[256,512]{1,0:T(8,128)(2,1)S(1)}, u32[]{:S(2)}, u32[]{:S(2)}) collective-permute-start(bf16[256,512]{1,0:T(8,128)(2,1)S(1)} %collective-permute-done.refs_0_), channel_id=1, source_target_pairs={{0,8},{1,9},{2,10},{3,11},{4,12},{5,13},{6,14},{7,15},{8,0},{9,1},... | collective-permute-start | bytes 786440 | tf_op jit(solution)/shard_map/ppermute | solution.py:126
  12.0 8.1 %collective-permute-start.2 = (bf16[256,512]{1,0:T(8,128)(2,1)S(1)}, bf16[256,512]{1,0:T(8,128)(2,1)S(1)}, u32[]{:S(2)}, u32[]{:S(2)}) collective-permute-start(bf16[256,512]{1,0:T(8,128)(2,1)S(1)} %collective-permute-done.refs_0_), channel_id=1, source_target_pairs={{0,5},{1,4},{2,7},{3,6},{4,1},{5,0},{6,3},{7,2},{8,13},{9,12},{10,... | collective-permute-start | bytes 786440 | tf_op jit(solution)/shard_map/ppermute | solution.py:126
  13.3 10.1 %copy-start = (s32[4,4]{1,0:T(4,128)S(1)}, s32[4,4]{1,0:T(4,128)}, u32[]{:S(2)}) copy-start(s32[4,4]{1,0:T(4,128)} %pairs.3) | copy-start | bytes 196
  13.3 10.1 %copy-start.1 = (bf16[256,512]{1,0:T(8,128)(2,1)S(1)}, bf16[256,512]{1,0:T(8,128)(2,1)}, u32[]{:S(2)}) copy-start(bf16[256,512]{1,0:T(8,128)(2,1)} %refs_0_.1) | copy-start | bytes 786436
  13.3 10.1 %collective-permute-start.8 = (bf16[256,512]{1,0:T(8,128)(2,1)S(1)}, bf16[256,512]{1,0:T(8,128)(2,1)S(1)}, u32[]{:S(2)}, u32[]{:S(2)}) collective-permute-start(bf16[256,512]{1,0:T(8,128)(2,1)S(1)} %broadcast_select_fusion), channel_id=1, source_target_pairs={{0,8},{1,4},{2,10},{3,6},{4,12},{5,0},{6,14},{7,2},{8,13},{9,1},{1... | collective-permute-start | bytes 786440 | tf_op jit(solution)/shard_map/ppermute | solution.py:126
  20.1 6.1 %collective-permute-start.3 = (bf16[256,512]{1,0:T(8,128)(2,1)S(1)}, bf16[256,512]{1,0:T(8,128)(2,1)S(1)}, u32[]{:S(2)}, u32[]{:S(2)}) collective-permute-start(bf16[256,512]{1,0:T(8,128)(2,1)S(1)} %broadcast_select_fusion.1), channel_id=1, source_target_pairs={{0,8},{1,4},{2,10},{3,6},{4,12},{5,0},{6,14},{7,2},{8,13},{9,1},{1... | collective-permute-start | bytes 786440 | tf_op jit(solution)/shard_map/ppermute | solution.py:126
  24.7 3.2 %collective-permute-start.9 = (f32[2,256,256]{2,1,0:T(8,128)S(1)}, f32[2,256,256]{2,1,0:T(8,128)S(1)}, u32[]{:S(2)}, u32[]{:S(2)}) collective-permute-start(f32[2,256,256]{2,1,0:T(8,128)S(1)} %get-tuple-element.12), channel_id=1, source_target_pairs={{0,1},{1,0},{2,3},{3,2},{4,5},{5,4},{6,7},{7,6},{8,9},{9,8},{10,11... | collective-permute-start | bytes 1572872 | tf_op jit(solution)/shard_map/ppermute | solution.py:126
  27.5 2.0 %collective-permute-start.5 = (f32[2,256,256]{2,1,0:T(8,128)S(1)}, f32[2,256,256]{2,1,0:T(8,128)S(1)}, u32[]{:S(2)}, u32[]{:S(2)}) collective-permute-start(f32[2,256,256]{2,1,0:T(8,128)S(1)} %get-tuple-element.10), channel_id=1, source_target_pairs={{0,1},{1,0},{2,3},{3,2},{4,5},{5,4},{6,7},{7,6},{8,9},{9,8},{10,11... | collective-permute-start | bytes 1572872 | tf_op jit(solution)/shard_map/ppermute | solution.py:126

commit v4 on v3

--- a/solution.py
+++ b/solution.py
@@ -37,7 +37,9 @@
 
 
 def multiply_kernel(pairs, *refs, parts, width):
-    blocks, pieces, keep, send, sums = refs[:4], refs[4:6], refs[6], refs[7], refs[8]
+    keep, *sends, sums = refs[-2 - len(parts) :]
+    blocks = refs[: 2 * len(parts)]
+    pieces = refs[2 * len(parts) : 2 * len(parts) + 2]
     row, col = lax.axis_index("row"), lax.axis_index("col")
     mine = pl.multiple_of((col & 1) * width, width)
     other = pl.multiple_of(width - mine, width)
@@ -61,34 +63,37 @@
                     )
 
         keep[index] = sums[:, pl.ds(mine, width)]
-        send[index] = sums[:, pl.ds(other, width)]
+        sends[index][...] = sums[:, pl.ds(other, width)]
 
 
-def multiply(block_list, blocks, pieces, parts, cost):
+def multiply(block_list, blocks, pieces, parts, cost, ahead=()):
     vmem = pl.BlockSpec(memory_space=pltpu.VMEM)
     rows, width = blocks[0].shape[0], pieces[0].shape[1] // 2
-    half = jax.ShapeDtypeStruct((2, rows, width), jnp.float32)
+    keep = jax.ShapeDtypeStruct((len(parts), rows, width), jnp.float32)
+    send = jax.ShapeDtypeStruct((rows, width), jnp.float32)
     return pl.pallas_call(
         functools.partial(multiply_kernel, parts=parts, width=width),
-        out_shape=(half, half),
-        in_specs=[pl.BlockSpec(memory_space=pltpu.SMEM)] + [vmem] * 6,
-        out_specs=(vmem, vmem),
+        out_shape=(keep,) + (send,) * len(parts),
+        in_specs=[pl.BlockSpec(memory_space=pltpu.SMEM)] + [vmem] * (len(blocks) + 2)
+        + [pl.BlockSpec(memory_space=pl.ANY)] * len(ahead),
+        out_specs=(vmem,) * (1 + len(parts)),
         scratch_shapes=[pltpu.VMEM((rows, 2 * width), jnp.float32)],
         cost_estimate=pl.CostEstimate(flops=cost, transcendentals=0, bytes_accessed=2**20),
         compiler_params=pltpu.CompilerParams(vmem_limit_bytes=8 * 2**20),
         name="multiply",
-    )(block_list, *blocks, *pieces)
+    )(block_list, *blocks, *pieces, *ahead)
 
 
-def add_kernel(keep, received, *refs, parts):
+def add_kernel(*refs, terms):
     out, held, sems = refs[-3:]
     col = lax.axis_index("col")
+    width = held.shape[2]
     copies = []
-    for index, part in enumerate(parts):
-        held[index] = keep[index] + received[1 - index]
-        start = pl.multiple_of((col ^ part) * held.shape[2], held.shape[2])
+    for place, (part, kept, received) in enumerate(terms):
+        held[place] = refs[kept[0]][kept[1]] + refs[received][...]
+        start = pl.multiple_of((col ^ part) * width, width)
         copy = pltpu.make_async_copy(
-            held.at[index], out.at[:, pl.ds(start, held.shape[2])], sems.at[index]
+            held.at[place], out.at[:, pl.ds(start, width)], sems.at[place]
         )
         copy.start()
         copies.append(copy)
@@ -96,20 +101,24 @@
         copy.wait()
 
 
-def add(keep, received, parts, earlier, shape):
+def add(sums, terms, earlier=None):
     anywhere = pl.BlockSpec(memory_space=pl.ANY)
     vmem = pl.BlockSpec(memory_space=pltpu.VMEM)
-    operands = [keep, received] + ([] if earlier is None else [earlier])
+    rows, width = sums[0].shape[1:]
+    aliased = [] if earlier is None else [earlier]
     return pl.pallas_call(
-        functools.partial(add_kernel, parts=parts),
-        out_shape=jax.ShapeDtypeStruct(shape, jnp.float32),
-        in_specs=[vmem, vmem] + ([] if earlier is None else [anywhere]),
+        functools.partial(add_kernel, terms=terms),
+        out_shape=jax.ShapeDtypeStruct((rows, 4 * width), jnp.float32),
+        in_specs=[vmem] * len(sums) + [anywhere] * len(aliased),
         out_specs=anywhere,
-        scratch_shapes=[pltpu.VMEM(keep.shape, jnp.float32), pltpu.SemaphoreType.DMA((2,))],
-        input_output_aliases={} if earlier is None else {2: 0},
+        scratch_shapes=[
+            pltpu.VMEM((len(terms), rows, width), jnp.float32),
+            pltpu.SemaphoreType.DMA((len(terms),)),
+        ],
+        input_output_aliases={len(sums): 0} if aliased else {},
         compiler_params=pltpu.CompilerParams(vmem_limit_bytes=8 * 2**20),
         name="add",
-    )(*operands)
+    )(*sums, *aliased)
 
 
 def gather_shards(amps, ints, block_list):
@@ -134,8 +143,8 @@
     beside = functools.partial(moved, target=lambda r, c: (r, c ^ 1))
     turns = ((row_pos >> 1) ^ col_pos) & 1 == 1
 
-    def last(by_pair, by_cross):
-        return moved(jnp.where(turns, by_pair, by_cross), turn)
+    def chosen(by_pair, by_cross):
+        return jnp.where(turns, by_pair, by_cross)
 
     def chip_columns(chip):
         return lax.dynamic_slice_in_dim(ints, chip * 2 * width, 2 * width, 1)
@@ -145,16 +154,20 @@
     near1 = pair(amps)
     near2 = cross(amps)
     pieces = [chip_columns(chip), across(chip_columns(1 - chip))]
-    near3 = last(near1, near2)
+    near3 = moved(chosen(near1, near2), turn)
     far1 = pair(far0)
     far2 = cross(far0)
-    far3 = last(far1, far2)
-    shape = (amps.shape[0], ints.shape[1])
-    cost = 4 * 2 * amps.shape[0] * amps.shape[1] * width
-    keep, send = multiply(block_list, [amps, near1, near2, near3], pieces, (0, 1), 30 * cost)
-    out = add(keep, beside(send), (0, 1), None, shape)
-    keep, send = multiply(block_list, [far0, far1, far2, far3], pieces, (2, 3), cost)
-    out = add(keep, beside(send), (2, 3), out, shape)
+    onward = chosen(far1, far2)
+    far3 = moved(onward, turn)
+    cost = 2 * 2 * amps.shape[0] * amps.shape[1] * width
+    blocks = [amps, near1, near2, near3, far0, far1]
+    keep, *sends = multiply(block_list, blocks, pieces, (0, 1, 2), 30 * cost, (onward,))
+    received = [beside(send) for send in sends]
+    last_keep, last_send = multiply(block_list, [far2, far3], pieces, (3,), cost)
+    last_received = beside(last_send)
+    out = add([keep, *received[:2]], ((0, (0, 0), 2), (1, (0, 1), 1)))
+    sums = [keep, last_keep, received[2], last_received]
+    out = add(sums, ((2, (0, 2), 3), (3, (1, 0), 2)), out)
     return out[None]
 
 

time: 30.5 us -> 29.7 us (0.974)
  waiting for transfers between devices: 15.6 us -> 14.2 us
  starting transfers between devices: 9.03 us -> 9.61 us
    ppermute x10 -> x12, waiting for transfers between devices: 15.6 us -> 14.2 us  [moved(): return lax.ppermute(block, GRID, route)]
    ppermute x10 -> x12, starting transfers between devices: 9.03 us -> 9.61 us  [moved(): return lax.ppermute(block, GRID, route)]
  transfers between devices with their start and end apart: 10 -> 12, of which waited for: 8 -> 8; matrix products, arithmetic and copies ran while one was open for 4% -> 4% of each run, Pallas kernels for 11% -> 12%
where the time goes in v4:
time: 29.7 us; the launch traced here: 29.6 us
  waiting for transfers between devices  14.2 us (48%)
  starting transfers between devices  9.61 us (32%)
  Pallas kernels  4.32 us (15%)
  local copies, waits for them, and re-layouts  1.28 us (4%)
    ppermute x12, waiting for transfers between devices, moved(): return lax.ppermute(block, GRID, route)  14.2 us
    ppermute x12, starting transfers between devices, moved(): return lax.ppermute(block, GRID, route)  9.61 us
    pallas_call x2, Pallas kernels, multiply(): pl.pallas_call(functools.partial(multiply_kernel, parts=parts, width=widt...  2.65 us
    pallas_call x2, Pallas kernels, add(): pl.pallas_call(functools.partial(add_kernel, terms=terms), out_shape=jax....  1.67 us
    dynamic_slice x1, local copies, waits for them, and re-layouts, chip_columns(): return lax.dynamic_slice_in_dim(ints, chip * 2 * width, 2 * width, 1)  1.27 us
  transfers between devices with their start and end apart: 12, of which 8 were waited for; matrix products, arithmetic and copies ran while one was open for 4% of the time, Pallas kernels for 12%

profile of v4, /device:TPU:0, one launch (start us, length us, event | category | flops | bytes accessed | tf_op | source)
XLA Modules:
  0.0 29.6 jit_solution(11793430909860971173)
XLA Ops:
  0.0 2.9 %collective-permute-start.3 = (bf16[256,512]{1,0:T(8,128)(2,1)}, bf16[256,512]{1,0:T(8,128)(2,1)S(1)}, u32[]{:S(2)}, u32[]{:S(2)}) collective-permute-start(bf16[256,512]{1,0:T(8,128)(2,1)} %refs_0_.1), channel_id=1, source_target_pairs={{0,2},{1,3},{2,0},{3,1},{4,6},{5,7},{6,4},{7,5},{8,10},{9,11},{10,... | collective-permute-start | bytes 786440 | tf_op jit(solution)/shard_map/ppermute | solution.py:135
  2.9 1.6 %collective-permute-start = (bf16[256,512]{1,0:T(8,128)(2,1)}, bf16[256,512]{1,0:T(8,128)(2,1)S(1)}, u32[]{:S(2)}, u32[]{:S(2)}) collective-permute-start(bf16[256,512]{1,0:T(8,128)(2,1)} %refs_0_.1), channel_id=1, source_target_pairs={{0,8},{1,9},{2,10},{3,11},{4,12},{5,13},{6,14},{7,15},{8,0},{9,1},... | collective-permute-start | bytes 786440 | tf_op jit(solution)/shard_map/ppermute | solution.py:135
  4.5 0.4 %collective-permute-start.1 = (bf16[256,512]{1,0:T(8,128)(2,1)}, bf16[256,512]{1,0:T(8,128)(2,1)S(1)}, u32[]{:S(2)}, u32[]{:S(2)}) collective-permute-start(bf16[256,512]{1,0:T(8,128)(2,1)} %refs_0_.1), channel_id=1, source_target_pairs={{0,5},{1,4},{2,7},{3,6},{4,1},{5,0},{6,3},{7,2},{8,13},{9,12},{10,... | collective-permute-start | bytes 786440 | tf_op jit(solution)/shard_map/ppermute | solution.py:135
  4.9 1.3 %constant_dynamic-slice_fusion = (bf16[512,512]{1,0:T(8,128)(2,1)S(1)}, bf16[512,512]{1,0:T(8,128)(2,1)S(1)}) fusion(bf16[512,1024]{1,0:T(8,128)(2,1)} %param.4, s32[]{:T(128)S(6)} %select_n.27, s32[]{:T(128)S(6)} %select_n.26), kind=kLoop, calls=%fused_computation.2 | loop fusion | bytes 2097160 | tf_op jit(solution)/shard_map/dynamic_slice | solution.py:150
  6.2 0.6 %collective-permute-start.5 = (bf16[512,512]{1,0:T(8,128)(2,1)S(1)}, bf16[512,512]{1,0:T(8,128)(2,1)S(1)}, u32[]{:S(2)}, u32[]{:S(2)}) collective-permute-start(bf16[512,512]{1,0:T(8,128)(2,1)S(1)} %get-tuple-element.17), channel_id=1, source_target_pairs={{0,2},{1,3},{2,0},{3,1},{4,6},{5,7},{6,4},{7,5},{8,10},{9,11},{10,... | collective-permute-start | bytes 1572872 | tf_op jit(solution)/shard_map/ppermute | solution.py:135
  6.8 2.7 %collective-permute-done.3.refs_4_ = bf16[256,512]{1,0:T(8,128)(2,1)S(1)} collective-permute-done((bf16[256,512]{1,0:T(8,128)(2,1)}, bf16[256,512]{1,0:T(8,128)(2,1)S(1)}, u32[]{:S(2)}, u32[]{:S(2)}) %collective-permute-start.3) | collective-permute-done | bytes 262176 | tf_op jit(solution)/shard_map/ppermute | solution.py:135
  9.5 2.5 %collective-permute-start.4 = (bf16[256,512]{1,0:T(8,128)(2,1)S(1)}, bf16[256,512]{1,0:T(8,128)(2,1)S(1)}, u32[]{:S(2)}, u32[]{:S(2)}) collective-permute-start(bf16[256,512]{1,0:T(8,128)(2,1)S(1)} %collective-permute-done.3.refs_4_), channel_id=1, source_target_pairs={{0,8},{1,9},{2,10},{3,11},{4,12},{5,13},{6,14},{7,15},{8,0},{9,1},... | collective-permute-start | bytes 786440 | tf_op jit(solution)/shard_map/ppermute | solution.py:135
  12.0 1.3 %collective-permute-done.1.refs_2_ = bf16[256,512]{1,0:T(8,128)(2,1)S(1)} collective-permute-done((bf16[256,512]{1,0:T(8,128)(2,1)}, bf16[256,512]{1,0:T(8,128)(2,1)S(1)}, u32[]{:S(2)}, u32[]{:S(2)}) %collective-permute-start.1) | collective-permute-done | bytes 262176 | tf_op jit(solution)/shard_map/ppermute | solution.py:135
  13.3 0.5 %collective-permute-start.2 = (bf16[256,512]{1,0:T(8,128)(2,1)S(1)}, bf16[256,512]{1,0:T(8,128)(2,1)S(1)}, u32[]{:S(2)}, u32[]{:S(2)}) collective-permute-start(bf16[256,512]{1,0:T(8,128)(2,1)S(1)} %broadcast_select_fusion.1), channel_id=1, source_target_pairs={{0,8},{1,4},{2,10},{3,6},{4,12},{5,0},{6,14},{7,2},{8,13},{9,1},{1... | collective-permute-start | bytes 786440 | tf_op jit(solution)/shard_map/ppermute | solution.py:135
  13.8 3.2 %collective-permute-done.4.refs_5_ = bf16[256,512]{1,0:T(8,128)(2,1)S(1)} collective-permute-done((bf16[256,512]{1,0:T(8,128)(2,1)S(1)}, bf16[256,512]{1,0:T(8,128)(2,1)S(1)}, u32[]{:S(2)}, u32[]{:S(2)}) %collective-permute-start.4) | collective-permute-done | bytes 262176 | tf_op jit(solution)/shard_map/ppermute | solution.py:135
  17.0 3.1 %collective-permute-done.6.refs_0_ = bf16[256,512]{1,0:T(8,128)(2,1)S(1)} collective-permute-done((bf16[256,512]{1,0:T(8,128)(2,1)S(1)}, bf16[256,512]{1,0:T(8,128)(2,1)S(1)}, u32[]{:S(2)}, u32[]{:S(2)}) %collective-permute-start.6) | collective-permute-done | bytes 262176 | tf_op jit(solution)/shard_map/ppermute | solution.py:135
  20.1 0.1 collective-permute-start.7
  20.2 0.6 %collective-permute-done.5.refs_7_.refs_3_ = bf16[512,512]{1,0:T(8,128)(2,1)S(1)} collective-permute-done((bf16[512,512]{1,0:T(8,128)(2,1)S(1)}, bf16[512,512]{1,0:T(8,128)(2,1)S(1)}, u32[]{:S(2)}, u32[]{:S(2)}) %collective-permute-start.5) | collective-permute-done | bytes 524320 | tf_op jit(solution)/shard_map/ppermute | solution.py:135
  20.8 2.6 %collective-permute-done.2.refs_3_ = bf16[256,512]{1,0:T(8,128)(2,1)S(1)} collective-permute-done((bf16[256,512]{1,0:T(8,128)(2,1)S(1)}, bf16[256,512]{1,0:T(8,128)(2,1)S(1)}, u32[]{:S(2)}, u32[]{:S(2)}) %collective-permute-start.2) | collective-permute-done | bytes 262176 | tf_op jit(solution)/shard_map/ppermute | solution.py:135
  23.4 1.7 %multiply.6 = (f32[3,256,256]{2,1,0:T(8,128)S(1)}, f32[256,256]{1,0:T(8,128)S(1)}, f32[256,256]{1,0:T(8,128)S(1)}, f32[256,256]{1,0:T(8,128)S(1)}) custom-call(s32[4,4]{1,0:T(4,128)S(1)} %copy-done, bf16[256,512]{1,0:T(8,128)(2,1)S(1)} %copy-done.1, bf16[256,512]{1,0:T(8,128)(2,1)S(1)} %collective-permute-done.refs_1_, ...), custom_call_target="tpu_custom_call" | custom-call | flops 4026531840 | bytes 1048576 | tf_op jit(solution)/shard_map/multiply/pallas_call | solution.py:74
  25.1 0.1 collective-permute-start.10
  25.2 0.5 %collective-permute-start.11 = (f32[256,256]{1,0:T(8,128)S(1)}, f32[256,256]{1,0:T(8,128)S(1)}, u32[]{:S(2)}, u32[]{:S(2)}) collective-permute-start(f32[256,256]{1,0:T(8,128)S(1)} %get-tuple-element.16), channel_id=1, source_target_pairs={{0,1},{1,0},{2,3},{3,2},{4,5},{5,4},{6,7},{7,6},{8,9},{9,8},{10,11... | collective-permute-start | bytes 786440 | tf_op jit(solution)/shard_map/ppermute | solution.py:135
  25.7 0.1 collective-permute-start.8
  25.8 0.4 %collective-permute-done.7.refs_1_ = bf16[256,512]{1,0:T(8,128)(2,1)S(1)} collective-permute-done((bf16[256,512]{1,0:T(8,128)(2,1)S(1)}, bf16[256,512]{1,0:T(8,128)(2,1)S(1)}, u32[]{:S(2)}, u32[]{:S(2)}) %collective-permute-start.7) | collective-permute-done | bytes 262176 | tf_op jit(solution)/shard_map/ppermute | solution.py:135
  26.2 0.9 %multiply.7 = (f32[1,256,256]{2,1,0:T(8,128)S(1)}, f32[256,256]{1,0:T(8,128)S(1)}) custom-call(s32[4,4]{1,0:T(4,128)S(1)} %copy-done, bf16[256,512]{1,0:T(8,128)(2,1)S(1)} %collective-permute-done.6.refs_0_, bf16[256,512]{1,0:T(8,128)(2,1)S(1)} %collective-permute-done.7.refs_1_, bf16[512,512]{1,0:T(8,128)(2,1)S(1)} %get-tuple-element.18.refs_6_.refs_2_, ...), custom_call_target="tpu_custom_call" | custom-call | flops 134217728 | bytes 1048576 | tf_op jit(solution)/shard_map/multiply/pallas_call | solution.py:74
  27.1 0.4 %collective-permute-start.9 = (f32[256,256]{1,0:T(8,128)S(1)}, f32[256,256]{1,0:T(8,128)S(1)}, u32[]{:S(2)}, u32[]{:S(2)}) collective-permute-start(f32[256,256]{1,0:T(8,128)S(1)} %get-tuple-element.14), channel_id=1, source_target_pairs={{0,1},{1,0},{2,3},{3,2},{4,5},{5,4},{6,7},{7,6},{8,9},{9,8},{10,11... | collective-permute-start | bytes 786440 | tf_op jit(solution)/shard_map/ppermute | solution.py:135
  27.5 0.8 %add.11.refs_4_ = f32[256,1024]{1,0:T(8,128)} custom-call(f32[3,256,256]{2,1,0:T(8,128)S(1)} %get-tuple-element.11.refs_0_, f32[256,256]{1,0:T(8,128)S(1)} %collective-permute-done.10.refs_1_, f32[256,256]{1,0:T(8,128)S(1)} %collective-permute-done.11.refs_2_), custom_call_target="tpu_custom_call" | custom-call | tf_op jit(solution)/shard_map/add/pallas_call | solution.py:109
  28.4 0.4 %collective-permute-done.9.refs_3_ = f32[256,256]{1,0:T(8,128)S(1)} collective-permute-done((f32[256,256]{1,0:T(8,128)S(1)}, f32[256,256]{1,0:T(8,128)S(1)}, u32[]{:S(2)}, u32[]{:S(2)}) %collective-permute-start.9) | collective-permute-done | bytes 262176 | tf_op jit(solution)/shard_map/ppermute | solution.py:135
  28.7 0.8 %add.12 = f32[256,1024]{1,0:T(8,128)} custom-call(f32[3,256,256]{2,1,0:T(8,128)S(1)} %get-tuple-element.11.refs_0_, f32[1,256,256]{2,1,0:T(8,128)S(1)} %get-tuple-element.12.refs_1_, f32[256,256]{1,0:T(8,128)S(1)} %collective-permute-done.8.refs_2_, f32[256,256]{1,0:T(8,128)S(1)} %collective-permute-done.9.refs_3_, ...), custom_call_target="tpu_custom_call", output_to_operand_aliasing={{}: (4, {})} | custom-call | tf_op jit(solution)/shard_map/add/pallas_call | solution.py:109
  (11 shorter events, 0.1 us)
Async XLA Ops:
  0.0 9.5 %collective-permute-start.3 = (bf16[256,512]{1,0:T(8,128)(2,1)}, bf16[256,512]{1,0:T(8,128)(2,1)S(1)}, u32[]{:S(2)}, u32[]{:S(2)}) collective-permute-start(bf16[256,512]{1,0:T(8,128)(2,1)} %refs_0_.1), channel_id=1, source_target_pairs={{0,2},{1,3},{2,0},{3,1},{4,6},{5,7},{6,4},{7,5},{8,10},{9,11},{10,... | collective-permute-start | bytes 786440 | tf_op jit(solution)/shard_map/ppermute | solution.py:135
  2.9 9.0 %collective-permute-start = (bf16[256,512]{1,0:T(8,128)(2,1)}, bf16[256,512]{1,0:T(8,128)(2,1)S(1)}, u32[]{:S(2)}, u32[]{:S(2)}) collective-permute-start(bf16[256,512]{1,0:T(8,128)(2,1)} %refs_0_.1), channel_id=1, source_target_pairs={{0,8},{1,9},{2,10},{3,11},{4,12},{5,13},{6,14},{7,15},{8,0},{9,1},... | collective-permute-start | bytes 786440 | tf_op jit(solution)/shard_map/ppermute | solution.py:135
  4.5 8.7 %collective-permute-start.1 = (bf16[256,512]{1,0:T(8,128)(2,1)}, bf16[256,512]{1,0:T(8,128)(2,1)S(1)}, u32[]{:S(2)}, u32[]{:S(2)}) collective-permute-start(bf16[256,512]{1,0:T(8,128)(2,1)} %refs_0_.1), channel_id=1, source_target_pairs={{0,5},{1,4},{2,7},{3,6},{4,1},{5,0},{6,3},{7,2},{8,13},{9,12},{10,... | collective-permute-start | bytes 786440 | tf_op jit(solution)/shard_map/ppermute | solution.py:135
  6.2 14.6 %collective-permute-start.5 = (bf16[512,512]{1,0:T(8,128)(2,1)S(1)}, bf16[512,512]{1,0:T(8,128)(2,1)S(1)}, u32[]{:S(2)}, u32[]{:S(2)}) collective-permute-start(bf16[512,512]{1,0:T(8,128)(2,1)S(1)} %get-tuple-element.17), channel_id=1, source_target_pairs={{0,2},{1,3},{2,0},{3,1},{4,6},{5,7},{6,4},{7,5},{8,10},{9,11},{10,... | collective-permute-start | bytes 1572872 | tf_op jit(solution)/shard_map/ppermute | solution.py:135
  9.5 7.6 %collective-permute-start.4 = (bf16[256,512]{1,0:T(8,128)(2,1)S(1)}, bf16[256,512]{1,0:T(8,128)(2,1)S(1)}, u32[]{:S(2)}, u32[]{:S(2)}) collective-permute-start(bf16[256,512]{1,0:T(8,128)(2,1)S(1)} %collective-permute-done.3.refs_4_), channel_id=1, source_target_pairs={{0,8},{1,9},{2,10},{3,11},{4,12},{5,13},{6,14},{7,15},{8,0},{9,1},... | collective-permute-start | bytes 786440 | tf_op jit(solution)/shard_map/ppermute | solution.py:135
  12.0 8.1 %collective-permute-start.6 = (bf16[256,512]{1,0:T(8,128)(2,1)S(1)}, bf16[256,512]{1,0:T(8,128)(2,1)S(1)}, u32[]{:S(2)}, u32[]{:S(2)}) collective-permute-start(bf16[256,512]{1,0:T(8,128)(2,1)S(1)} %collective-permute-done.3.refs_4_), channel_id=1, source_target_pairs={{0,5},{1,4},{2,7},{3,6},{4,1},{5,0},{6,3},{7,2},{8,13},{9,12},{10,... | collective-permute-start | bytes 786440 | tf_op jit(solution)/shard_map/ppermute | solution.py:135
  13.3 10.1 %copy-start = (s32[4,4]{1,0:T(4,128)S(1)}, s32[4,4]{1,0:T(4,128)}, u32[]{:S(2)}) copy-start(s32[4,4]{1,0:T(4,128)} %pairs.3) | copy-start | bytes 196
  13.3 10.1 %copy-start.1 = (bf16[256,512]{1,0:T(8,128)(2,1)S(1)}, bf16[256,512]{1,0:T(8,128)(2,1)}, u32[]{:S(2)}) copy-start(bf16[256,512]{1,0:T(8,128)(2,1)} %refs_0_.1) | copy-start | bytes 786436
  13.3 10.1 %collective-permute-start.2 = (bf16[256,512]{1,0:T(8,128)(2,1)S(1)}, bf16[256,512]{1,0:T(8,128)(2,1)S(1)}, u32[]{:S(2)}, u32[]{:S(2)}) collective-permute-start(bf16[256,512]{1,0:T(8,128)(2,1)S(1)} %broadcast_select_fusion.1), channel_id=1, source_target_pairs={{0,8},{1,4},{2,10},{3,6},{4,12},{5,0},{6,14},{7,2},{8,13},{9,1},{1... | collective-permute-start | bytes 786440 | tf_op jit(solution)/shard_map/ppermute | solution.py:135
  20.1 6.1 %collective-permute-start.7 = (bf16[256,512]{1,0:T(8,128)(2,1)S(1)}, bf16[256,512]{1,0:T(8,128)(2,1)S(1)}, u32[]{:S(2)}, u32[]{:S(2)}) collective-permute-start(bf16[256,512]{1,0:T(8,128)(2,1)S(1)} %broadcast_select_fusion.refs_8_), channel_id=1, source_target_pairs={{0,8},{1,4},{2,10},{3,6},{4,12},{5,0},{6,14},{7,2},{8,13},{9,1},{1... | collective-permute-start | bytes 786440 | tf_op jit(solution)/shard_map/ppermute | solution.py:135
  25.1 2.4 %collective-permute-start.10 = (f32[256,256]{1,0:T(8,128)S(1)}, f32[256,256]{1,0:T(8,128)S(1)}, u32[]{:S(2)}, u32[]{:S(2)}) collective-permute-start(f32[256,256]{1,0:T(8,128)S(1)} %get-tuple-element.15), channel_id=1, source_target_pairs={{0,1},{1,0},{2,3},{3,2},{4,5},{5,4},{6,7},{7,6},{8,9},{9,8},{10,11... | collective-permute-start | bytes 786440 | tf_op jit(solution)/shard_map/ppermute | solution.py:135
  25.2 2.3 %collective-permute-start.11 = (f32[256,256]{1,0:T(8,128)S(1)}, f32[256,256]{1,0:T(8,128)S(1)}, u32[]{:S(2)}, u32[]{:S(2)}) collective-permute-start(f32[256,256]{1,0:T(8,128)S(1)} %get-tuple-element.16), channel_id=1, source_target_pairs={{0,1},{1,0},{2,3},{3,2},{4,5},{5,4},{6,7},{7,6},{8,9},{9,8},{10,11... | collective-permute-start | bytes 786440 | tf_op jit(solution)/shard_map/ppermute | solution.py:135
  25.7 2.7 %collective-permute-start.8 = (f32[256,256]{1,0:T(8,128)S(1)}, f32[256,256]{1,0:T(8,128)S(1)}, u32[]{:S(2)}, u32[]{:S(2)}) collective-permute-start(f32[256,256]{1,0:T(8,128)S(1)} %get-tuple-element.13), channel_id=1, source_target_pairs={{0,1},{1,0},{2,3},{3,2},{4,5},{5,4},{6,7},{7,6},{8,9},{9,8},{10,11... | collective-permute-start | bytes 786440 | tf_op jit(solution)/shard_map/ppermute | solution.py:135
  27.1 1.6 %collective-permute-start.9 = (f32[256,256]{1,0:T(8,128)S(1)}, f32[256,256]{1,0:T(8,128)S(1)}, u32[]{:S(2)}, u32[]{:S(2)}) collective-permute-start(f32[256,256]{1,0:T(8,128)S(1)} %get-tuple-element.14), channel_id=1, source_target_pairs={{0,1},{1,0},{2,3},{3,2},{4,5},{5,4},{6,7},{7,6},{8,9},{9,8},{10,11... | collective-permute-start | bytes 786440 | tf_op jit(solution)/shard_map/ppermute | solution.py:135

commit v5 on v4

--- a/solution.py
+++ b/solution.py
@@ -36,52 +36,60 @@
     return owned.reshape(1, owned.shape[0], owned.shape[1])
 
 
-def multiply_kernel(pairs, *refs, parts, width):
+def multiply_kernel(pairs, *refs, groups, parts, width):
     keep, *sends, sums = refs[-2 - len(parts) :]
-    blocks = refs[: 2 * len(parts)]
-    pieces = refs[2 * len(parts) : 2 * len(parts) + 2]
+    refs = list(refs)
+    blocks = [[refs.pop(0) if used else None for used in group] for group in groups]
+    pieces = refs[:2]
     row, col = lax.axis_index("row"), lax.axis_index("col")
     mine = pl.multiple_of((col & 1) * width, width)
     other = pl.multiple_of(width - mine, width)
+    turned = (((row >> 1) ^ col) & 1) == 1
     for index, part in enumerate(parts):
         owner = col ^ part
         sums[...] = jnp.zeros(sums.shape, sums.dtype)
-        for slot in range(2):
+        if part & 1 == 0:
+            choices = ((0, 0, None), (1, 1, True), (1, 2, False))
+        else:
+            choices = ((0, 1, False), (0, 2, True), (1, 3, None))
+        for slot, label, when_turned in choices:
+            block = blocks[index][label]
             kind = ((row ^ (2 * slot + (part & 1))) + owner) & 3
             listed = pairs[owner, kind] != 0
+            if when_turned is not None:
+                listed = listed & (turned if when_turned else ~turned)
             here = kind == ((row + col) & 3)
             for source in range(2):
                 if part & 1 == 0 and source != (slot ^ (part >> 1)):
                     continue
 
                 @pl.when(listed & (here == (source == 0)))
-                def _(slot=slot, source=source, index=index):
+                def _(block=block, source=source):
                     sums[...] += jnp.dot(
-                        blocks[2 * index + slot][...],
-                        pieces[source][...],
-                        preferred_element_type=jnp.float32,
+                        block[...], pieces[source][...], preferred_element_type=jnp.float32
                     )
 
         keep[index] = sums[:, pl.ds(mine, width)]
         sends[index][...] = sums[:, pl.ds(other, width)]
 
 
-def multiply(block_list, blocks, pieces, parts, cost, ahead=()):
+def multiply(block_list, groups, pieces, parts, cost):
     vmem = pl.BlockSpec(memory_space=pltpu.VMEM)
+    blocks = [block for group in groups for block in group if block is not None]
     rows, width = blocks[0].shape[0], pieces[0].shape[1] // 2
     keep = jax.ShapeDtypeStruct((len(parts), rows, width), jnp.float32)
     send = jax.ShapeDtypeStruct((rows, width), jnp.float32)
+    used = tuple(tuple(block is not None for block in group) for group in groups)
     return pl.pallas_call(
-        functools.partial(multiply_kernel, parts=parts, width=width),
+        functools.partial(multiply_kernel, groups=used, parts=parts, width=width),
         out_shape=(keep,) + (send,) * len(parts),
-        in_specs=[pl.BlockSpec(memory_space=pltpu.SMEM)] + [vmem] * (len(blocks) + 2)
-        + [pl.BlockSpec(memory_space=pl.ANY)] * len(ahead),
+        in_specs=[pl.BlockSpec(memory_space=pltpu.SMEM)] + [vmem] * (len(blocks) + 2),
         out_specs=(vmem,) * (1 + len(parts)),
         scratch_shapes=[pltpu.VMEM((rows, 2 * width), jnp.float32)],
         cost_estimate=pl.CostEstimate(flops=cost, transcendentals=0, bytes_accessed=2**20),
         compiler_params=pltpu.CompilerParams(vmem_limit_bytes=8 * 2**20),
         name="multiply",
-    )(block_list, *blocks, *pieces, *ahead)
+    )(block_list, *blocks, *pieces)
 
 
 def add_kernel(*refs, terms):
@@ -123,7 +131,7 @@
 
 def gather_shards(amps, ints, block_list):
     rows, cols = lax.axis_size("row"), lax.axis_size("col")
-    row_pos, col_pos = lax.axis_index("row"), lax.axis_index("col")
+    col_pos = lax.axis_index("col")
     width = ints.shape[1] // cols
 
     def moved(block, target):
@@ -134,40 +142,38 @@
         ]
         return lax.ppermute(block, GRID, route)
 
-    def turn(r, c):
-        return (r ^ 1, c ^ 1) if (r >> 1 ^ c) & 1 else (r ^ 2, c)
+    def either(flip):
+        return lambda r, c: (r ^ 1, c ^ 1) if (r >> 1 ^ c ^ flip) & 1 else (r ^ 2, c)
 
-    pair = functools.partial(moved, target=lambda r, c: (r ^ 2, c))
-    cross = functools.partial(moved, target=lambda r, c: (r ^ 1, c ^ 1))
+    first = functools.partial(moved, target=either(0))
+    second = functools.partial(moved, target=either(1))
     across = functools.partial(moved, target=lambda r, c: (r, c ^ 2))
     beside = functools.partial(moved, target=lambda r, c: (r, c ^ 1))
-    turns = ((row_pos >> 1) ^ col_pos) & 1 == 1
-
-    def chosen(by_pair, by_cross):
-        return jnp.where(turns, by_pair, by_cross)
 
     def chip_columns(chip):
         return lax.dynamic_slice_in_dim(ints, chip * 2 * width, 2 * width, 1)
 
     chip = col_pos // 2
     far0 = across(amps)
-    near1 = pair(amps)
-    near2 = cross(amps)
+    near1 = first(amps)
+    near2 = second(amps)
     pieces = [chip_columns(chip), across(chip_columns(1 - chip))]
-    near3 = moved(chosen(near1, near2), turn)
-    far1 = pair(far0)
-    far2 = cross(far0)
-    onward = chosen(far1, far2)
-    far3 = moved(onward, turn)
+    far0, near2 = lax.optimization_barrier((far0, near2))
+    near3 = first(near1)
+    far1 = first(far0)
+    far2 = second(far0)
+    far3 = first(far1)
     cost = 2 * 2 * amps.shape[0] * amps.shape[1] * width
-    blocks = [amps, near1, near2, near3, far0, far1]
-    keep, *sends = multiply(block_list, blocks, pieces, (0, 1, 2), 30 * cost, (onward,))
-    received = [beside(send) for send in sends]
-    last_keep, last_send = multiply(block_list, [far2, far3], pieces, (3,), cost)
-    last_received = beside(last_send)
-    out = add([keep, *received[:2]], ((0, (0, 0), 2), (1, (0, 1), 1)))
-    sums = [keep, last_keep, received[2], last_received]
-    out = add(sums, ((2, (0, 2), 3), (3, (1, 0), 2)), out)
+    run = functools.partial(multiply, block_list, pieces=pieces)
+    groups = [[amps, near1, near2, None], [far0, far1, far2, None]]
+    keep, *sends = run(groups=groups, parts=(0, 2), cost=15 * cost)
+    received0, received2 = [beside(send) for send in sends]
+    keep1, send1 = run(groups=[[None, near1, near2, near3]], parts=(1,), cost=15 * cost)
+    received1 = beside(send1)
+    keep3, send3 = run(groups=[[None, far1, far2, far3]], parts=(3,), cost=cost)
+    received3 = beside(send3)
+    out = add([keep, keep1, received0, received1], ((0, (0, 0), 3), (1, (1, 0), 2)))
+    out = add([keep, keep3, received2, received3], ((2, (0, 1), 3), (3, (1, 0), 2)), out)
     return out[None]
 
 

time: 29.7 us -> 28.5 us (0.960)
  waiting for transfers between devices: 14.2 us -> 9.2 us
  starting transfers between devices: 9.61 us -> 12.8 us
  Pallas kernels: 4.32 us -> 4.95 us
    ppermute x12, waiting for transfers between devices: 14.2 us -> 9.2 us  [moved(): return lax.ppermute(block, GRID, route)]
    ppermute x12, starting transfers between devices: 9.61 us -> 12.8 us  [moved(): return lax.ppermute(block, GRID, route)]
    pallas_call x2 -> x3, Pallas kernels: 2.65 us -> 3.28 us  [multiply(): pl.pallas_call(functools.partial(multiply_kernel, groups=used, parts=part...]
  transfers between devices with their start and end apart: 12 -> 12, of which waited for: 8 -> 4; matrix products, arithmetic and copies ran while one was open for 4% -> 5% of each run, Pallas kernels for 12% -> 14%
where the time goes in v5:
time: 28.5 us; the launch traced here: 28.4 us
  starting transfers between devices  12.8 us (45%)
  waiting for transfers between devices  9.2 us (32%)
  Pallas kernels  4.95 us (17%)
  local copies, waits for them, and re-layouts  1.32 us (5%)
    ppermute x12, starting transfers between devices, moved(): return lax.ppermute(block, GRID, route)  12.8 us
    ppermute x12, waiting for transfers between devices, moved(): return lax.ppermute(block, GRID, route)  9.2 us
    pallas_call x3, Pallas kernels, multiply(): pl.pallas_call(functools.partial(multiply_kernel, groups=used, parts=part...  3.28 us
    pallas_call x2, Pallas kernels, add(): pl.pallas_call(functools.partial(add_kernel, terms=terms), out_shape=jax....  1.67 us
    dynamic_slice x1, local copies, waits for them, and re-layouts, chip_columns(): return lax.dynamic_slice_in_dim(ints, chip * 2 * width, 2 * width, 1)  1.31 us
  transfers between devices with their start and end apart: 12, of which 4 were waited for; matrix products, arithmetic and copies ran while one was open for 5% of the time, Pallas kernels for 14%

profile of v5, /device:TPU:0, one launch (start us, length us, event | category | flops | bytes accessed | tf_op | source)
XLA Modules:
  0.0 28.4 jit_solution(7813405826666630373)
XLA Ops:
  0.0 2.9 %collective-permute-start.1 = (bf16[256,512]{1,0:T(8,128)(2,1)}, bf16[256,512]{1,0:T(8,128)(2,1)S(1)}, u32[]{:S(2)}, u32[]{:S(2)}) collective-permute-start(bf16[256,512]{1,0:T(8,128)(2,1)} %refs_0_.1), channel_id=1, source_target_pairs={{0,2},{1,3},{2,0},{3,1},{4,6},{5,7},{6,4},{7,5},{8,10},{9,11},{10,... | collective-permute-start | bytes 786440 | tf_op jit(solution)/shard_map/ppermute | solution.py:143
  2.9 0.7 %collective-permute-start.2 = (bf16[256,512]{1,0:T(8,128)(2,1)}, bf16[256,512]{1,0:T(8,128)(2,1)S(1)}, u32[]{:S(2)}, u32[]{:S(2)}) collective-permute-start(bf16[256,512]{1,0:T(8,128)(2,1)} %refs_0_.1), channel_id=1, source_target_pairs={{0,5},{1,9},{2,7},{3,11},{4,1},{5,13},{6,3},{7,15},{8,0},{9,12},{1... | collective-permute-start | bytes 786440 | tf_op jit(solution)/shard_map/ppermute | solution.py:143
  3.6 1.3 %constant_dynamic-slice_fusion = (bf16[512,512]{1,0:T(8,128)(2,1)S(1)}, bf16[512,512]{1,0:T(8,128)(2,1)S(1)}) fusion(bf16[512,1024]{1,0:T(8,128)(2,1)} %param.4, s32[]{:T(128)S(6)} %select_n.13, s32[]{:T(128)S(6)} %select_n.12), kind=kLoop, calls=%fused_computation | loop fusion | bytes 2097160 | tf_op jit(solution)/shard_map/dynamic_slice | solution.py:154
  4.9 0.0 copy-start
  4.9 0.6 %collective-permute-start.5 = (bf16[512,512]{1,0:T(8,128)(2,1)S(1)}, bf16[512,512]{1,0:T(8,128)(2,1)S(1)}, u32[]{:S(2)}, u32[]{:S(2)}) collective-permute-start(bf16[512,512]{1,0:T(8,128)(2,1)S(1)} %get-tuple-element.23), channel_id=1, source_target_pairs={{0,2},{1,3},{2,0},{3,1},{4,6},{5,7},{6,4},{7,5},{8,10},{9,11},{10,... | collective-permute-start | bytes 1572872 | tf_op jit(solution)/shard_map/ppermute | solution.py:143
  5.5 0.9 %collective-permute-start = (bf16[256,512]{1,0:T(8,128)(2,1)S(1)}, bf16[256,512]{1,0:T(8,128)(2,1)S(1)}, u32[]{:S(2)}, u32[]{:S(2)}) collective-permute-start(bf16[256,512]{1,0:T(8,128)(2,1)S(1)} %copy-done.1), channel_id=1, source_target_pairs={{0,8},{1,4},{2,10},{3,6},{4,12},{5,0},{6,14},{7,2},{8,13},{9,1},{1... | collective-permute-start | bytes 786440 | tf_op jit(solution)/shard_map/ppermute | solution.py:143
  6.5 3.8 %collective-permute-done.1.refs_3_ = bf16[256,512]{1,0:T(8,128)(2,1)S(1)} collective-permute-done((bf16[256,512]{1,0:T(8,128)(2,1)}, bf16[256,512]{1,0:T(8,128)(2,1)S(1)}, u32[]{:S(2)}, u32[]{:S(2)}) %collective-permute-start.1) | collective-permute-done | bytes 262176 | tf_op jit(solution)/shard_map/ppermute | solution.py:143
  10.3 0.0 collective-permute-done.2.refs_2_.refs_1_
  10.3 2.0 %collective-permute-start.3 = (bf16[256,512]{1,0:T(8,128)(2,1)S(1)}, bf16[256,512]{1,0:T(8,128)(2,1)S(1)}, u32[]{:S(2)}, u32[]{:S(2)}) collective-permute-start(bf16[256,512]{1,0:T(8,128)(2,1)S(1)} %collective-permute-done.1.refs_3_), channel_id=1, source_target_pairs={{0,8},{1,4},{2,10},{3,6},{4,12},{5,0},{6,14},{7,2},{8,13},{9,1},{1... | collective-permute-start | bytes 786440 | tf_op jit(solution)/shard_map/ppermute | solution.py:143
  12.4 0.0 collective-permute-start.4
  12.4 2.0 %collective-permute-start.9 = (bf16[256,512]{1,0:T(8,128)(2,1)S(1)}, bf16[256,512]{1,0:T(8,128)(2,1)S(1)}, u32[]{:S(2)}, u32[]{:S(2)}) collective-permute-start(bf16[256,512]{1,0:T(8,128)(2,1)S(1)} %collective-permute-done.refs_1_.refs_0_), channel_id=1, source_target_pairs={{0,8},{1,4},{2,10},{3,6},{4,12},{5,0},{6,14},{7,2},{8,13},{9,1},{1... | collective-permute-start | bytes 786440 | tf_op jit(solution)/shard_map/ppermute | solution.py:143
  14.4 4.2 %collective-permute-done.3.refs_4_.refs_0_ = bf16[256,512]{1,0:T(8,128)(2,1)S(1)} collective-permute-done((bf16[256,512]{1,0:T(8,128)(2,1)S(1)}, bf16[256,512]{1,0:T(8,128)(2,1)S(1)}, u32[]{:S(2)}, u32[]{:S(2)}) %collective-permute-start.3) | collective-permute-done | bytes 262176 | tf_op jit(solution)/shard_map/ppermute | solution.py:143
  18.6 2.5 %collective-permute-start.6 = (bf16[256,512]{1,0:T(8,128)(2,1)S(1)}, bf16[256,512]{1,0:T(8,128)(2,1)S(1)}, u32[]{:S(2)}, u32[]{:S(2)}) collective-permute-start(bf16[256,512]{1,0:T(8,128)(2,1)S(1)} %collective-permute-done.3.refs_4_.refs_0_), channel_id=1, source_target_pairs={{0,8},{1,4},{2,10},{3,6},{4,12},{5,0},{6,14},{7,2},{8,13},{9,1},{1... | collective-permute-start | bytes 786440 | tf_op jit(solution)/shard_map/ppermute | solution.py:143
  21.1 1.4 %multiply.7 = (f32[2,256,256]{2,1,0:T(8,128)S(1)}, f32[256,256]{1,0:T(8,128)S(1)}, f32[256,256]{1,0:T(8,128)S(1)}) custom-call(s32[4,4]{1,0:T(4,128)S(1)} %copy-done, bf16[256,512]{1,0:T(8,128)(2,1)S(1)} %copy-done.1, bf16[256,512]{1,0:T(8,128)(2,1)S(1)} %collective-permute-done.refs_1_.refs_0_, bf16[256,512]{1,0:T(8,128)(2,1)S(1)} %collective-permute-done.2.refs_2_.refs_1_, ...), custom_call_target="tpu_custom_call" | custom-call | flops 2013265920 | bytes 1048576 | tf_op jit(solution)/shard_map/multiply/pallas_call | solution.py:83
  22.5 0.5 %collective-permute-start.7 = (f32[256,256]{1,0:T(8,128)S(1)}, f32[256,256]{1,0:T(8,128)S(1)}, u32[]{:S(2)}, u32[]{:S(2)}) collective-permute-start(f32[256,256]{1,0:T(8,128)S(1)} %get-tuple-element.18), channel_id=1, source_target_pairs={{0,1},{1,0},{2,3},{3,2},{4,5},{5,4},{6,7},{7,6},{8,9},{9,8},{10,11... | collective-permute-start | bytes 786440 | tf_op jit(solution)/shard_map/ppermute | solution.py:143
  23.0 0.1 collective-permute-start.10
  23.1 1.0 %multiply.9 = (f32[1,256,256]{2,1,0:T(8,128)S(1)}, f32[256,256]{1,0:T(8,128)S(1)}) custom-call(s32[4,4]{1,0:T(4,128)S(1)} %copy-done, bf16[256,512]{1,0:T(8,128)(2,1)S(1)} %collective-permute-done.refs_1_.refs_0_, bf16[256,512]{1,0:T(8,128)(2,1)S(1)} %collective-permute-done.2.refs_2_.refs_1_, bf16[256,512]{1,0:T(8,128)(2,1)S(1)} %collective-permute-done.9.refs_2_, ...), custom_call_target="tpu_custom_call" | custom-call | flops 2013265920 | bytes 1048576 | tf_op jit(solution)/shard_map/multiply/pallas_call | solution.py:83
  24.1 0.5 %collective-permute-start.11 = (f32[256,256]{1,0:T(8,128)S(1)}, f32[256,256]{1,0:T(8,128)S(1)}, u32[]{:S(2)}, u32[]{:S(2)}) collective-permute-start(f32[256,256]{1,0:T(8,128)S(1)} %get-tuple-element.22), channel_id=1, source_target_pairs={{0,1},{1,0},{2,3},{3,2},{4,5},{5,4},{6,7},{7,6},{8,9},{9,8},{10,11... | collective-permute-start | bytes 786440 | tf_op jit(solution)/shard_map/ppermute | solution.py:143
  24.5 0.4 %collective-permute-done.6.refs_2_ = bf16[256,512]{1,0:T(8,128)(2,1)S(1)} collective-permute-done((bf16[256,512]{1,0:T(8,128)(2,1)S(1)}, bf16[256,512]{1,0:T(8,128)(2,1)S(1)}, u32[]{:S(2)}, u32[]{:S(2)}) %collective-permute-start.6) | collective-permute-done | bytes 262176 | tf_op jit(solution)/shard_map/ppermute | solution.py:143
  25.0 1.0 %multiply.8 = (f32[1,256,256]{2,1,0:T(8,128)S(1)}, f32[256,256]{1,0:T(8,128)S(1)}) custom-call(s32[4,4]{1,0:T(4,128)S(1)} %copy-done, bf16[256,512]{1,0:T(8,128)(2,1)S(1)} %collective-permute-done.3.refs_4_.refs_0_, bf16[256,512]{1,0:T(8,128)(2,1)S(1)} %collective-permute-done.4.refs_5_.refs_1_, bf16[256,512]{1,0:T(8,128)(2,1)S(1)} %collective-permute-done.6.refs_2_, ...), custom_call_target="tpu_custom_call" | custom-call | flops 134217728 | bytes 1048576 | tf_op jit(solution)/shard_map/multiply/pallas_call | solution.py:83
  25.9 0.1 collective-permute-start.8
  26.1 0.8 %add.11.refs_4_ = f32[256,1024]{1,0:T(8,128)} custom-call(f32[2,256,256]{2,1,0:T(8,128)S(1)} %get-tuple-element.16.refs_0_, f32[1,256,256]{2,1,0:T(8,128)S(1)} %get-tuple-element.20.refs_1_, f32[256,256]{1,0:T(8,128)S(1)} %collective-permute-done.10.refs_2_, f32[256,256]{1,0:T(8,128)S(1)} %collective-permute-done.11.refs_3_), custom_call_target="tpu_custom_call" | custom-call | tf_op jit(solution)/shard_map/add/pallas_call | solution.py:117
  26.9 0.6 %collective-permute-done.8.refs_3_ = f32[256,256]{1,0:T(8,128)S(1)} collective-permute-done((f32[256,256]{1,0:T(8,128)S(1)}, f32[256,256]{1,0:T(8,128)S(1)}, u32[]{:S(2)}, u32[]{:S(2)}) %collective-permute-start.8) | collective-permute-done | bytes 262176 | tf_op jit(solution)/shard_map/ppermute | solution.py:143
  27.6 0.8 %add.12 = f32[256,1024]{1,0:T(8,128)} custom-call(f32[2,256,256]{2,1,0:T(8,128)S(1)} %get-tuple-element.16.refs_0_, f32[1,256,256]{2,1,0:T(8,128)S(1)} %get-tuple-element.17.refs_1_, f32[256,256]{1,0:T(8,128)S(1)} %collective-permute-done.7.refs_2_, f32[256,256]{1,0:T(8,128)S(1)} %collective-permute-done.8.refs_3_, ...), custom_call_target="tpu_custom_call", output_to_operand_aliasing={{}: (4, {})} | custom-call | tf_op jit(solution)/shard_map/add/pallas_call | solution.py:117
  (10 shorter events, 0.0 us)
Async XLA Ops:
  0.0 10.3 %collective-permute-start.1 = (bf16[256,512]{1,0:T(8,128)(2,1)}, bf16[256,512]{1,0:T(8,128)(2,1)S(1)}, u32[]{:S(2)}, u32[]{:S(2)}) collective-permute-start(bf16[256,512]{1,0:T(8,128)(2,1)} %refs_0_.1), channel_id=1, source_target_pairs={{0,2},{1,3},{2,0},{3,1},{4,6},{5,7},{6,4},{7,5},{8,10},{9,11},{10,... | collective-permute-start | bytes 786440 | tf_op jit(solution)/shard_map/ppermute | solution.py:143
  2.9 7.4 %collective-permute-start.2 = (bf16[256,512]{1,0:T(8,128)(2,1)}, bf16[256,512]{1,0:T(8,128)(2,1)S(1)}, u32[]{:S(2)}, u32[]{:S(2)}) collective-permute-start(bf16[256,512]{1,0:T(8,128)(2,1)} %refs_0_.1), channel_id=1, source_target_pairs={{0,5},{1,9},{2,7},{3,11},{4,1},{5,13},{6,3},{7,15},{8,0},{9,12},{1... | collective-permute-start | bytes 786440 | tf_op jit(solution)/shard_map/ppermute | solution.py:143
  3.6 1.9 %copy-start.1 = (bf16[256,512]{1,0:T(8,128)(2,1)S(1)}, bf16[256,512]{1,0:T(8,128)(2,1)}, u32[]{:S(2)}) copy-start(bf16[256,512]{1,0:T(8,128)(2,1)} %refs_0_.1) | copy-start | bytes 786436
  4.9 16.2 %copy-start = (s32[4,4]{1,0:T(4,128)S(1)}, s32[4,4]{1,0:T(4,128)}, u32[]{:S(2)}) copy-start(s32[4,4]{1,0:T(4,128)} %pairs.5) | copy-start | bytes 196
  4.9 16.2 %collective-permute-start.5 = (bf16[512,512]{1,0:T(8,128)(2,1)S(1)}, bf16[512,512]{1,0:T(8,128)(2,1)S(1)}, u32[]{:S(2)}, u32[]{:S(2)}) collective-permute-start(bf16[512,512]{1,0:T(8,128)(2,1)S(1)} %get-tuple-element.23), channel_id=1, source_target_pairs={{0,2},{1,3},{2,0},{3,1},{4,6},{5,7},{6,4},{7,5},{8,10},{9,11},{10,... | collective-permute-start | bytes 1572872 | tf_op jit(solution)/shard_map/ppermute | solution.py:143
  5.5 6.8 %collective-permute-start = (bf16[256,512]{1,0:T(8,128)(2,1)S(1)}, bf16[256,512]{1,0:T(8,128)(2,1)S(1)}, u32[]{:S(2)}, u32[]{:S(2)}) collective-permute-start(bf16[256,512]{1,0:T(8,128)(2,1)S(1)} %copy-done.1), channel_id=1, source_target_pairs={{0,8},{1,4},{2,10},{3,6},{4,12},{5,0},{6,14},{7,2},{8,13},{9,1},{1... | collective-permute-start | bytes 786440 | tf_op jit(solution)/shard_map/ppermute | solution.py:143
  10.3 8.3 %collective-permute-start.3 = (bf16[256,512]{1,0:T(8,128)(2,1)S(1)}, bf16[256,512]{1,0:T(8,128)(2,1)S(1)}, u32[]{:S(2)}, u32[]{:S(2)}) collective-permute-start(bf16[256,512]{1,0:T(8,128)(2,1)S(1)} %collective-permute-done.1.refs_3_), channel_id=1, source_target_pairs={{0,8},{1,4},{2,10},{3,6},{4,12},{5,0},{6,14},{7,2},{8,13},{9,1},{1... | collective-permute-start | bytes 786440 | tf_op jit(solution)/shard_map/ppermute | solution.py:143
  12.4 8.7 %collective-permute-start.4 = (bf16[256,512]{1,0:T(8,128)(2,1)S(1)}, bf16[256,512]{1,0:T(8,128)(2,1)S(1)}, u32[]{:S(2)}, u32[]{:S(2)}) collective-permute-start(bf16[256,512]{1,0:T(8,128)(2,1)S(1)} %collective-permute-done.1.refs_3_), channel_id=1, source_target_pairs={{0,5},{1,9},{2,7},{3,11},{4,1},{5,13},{6,3},{7,15},{8,0},{9,12},{1... | collective-permute-start | bytes 786440 | tf_op jit(solution)/shard_map/ppermute | solution.py:143
  12.4 10.7 %collective-permute-start.9 = (bf16[256,512]{1,0:T(8,128)(2,1)S(1)}, bf16[256,512]{1,0:T(8,128)(2,1)S(1)}, u32[]{:S(2)}, u32[]{:S(2)}) collective-permute-start(bf16[256,512]{1,0:T(8,128)(2,1)S(1)} %collective-permute-done.refs_1_.refs_0_), channel_id=1, source_target_pairs={{0,8},{1,4},{2,10},{3,6},{4,12},{5,0},{6,14},{7,2},{8,13},{9,1},{1... | collective-permute-start | bytes 786440 | tf_op jit(solution)/shard_map/ppermute | solution.py:143
  18.6 6.4 %collective-permute-start.6 = (bf16[256,512]{1,0:T(8,128)(2,1)S(1)}, bf16[256,512]{1,0:T(8,128)(2,1)S(1)}, u32[]{:S(2)}, u32[]{:S(2)}) collective-permute-start(bf16[256,512]{1,0:T(8,128)(2,1)S(1)} %collective-permute-done.3.refs_4_.refs_0_), channel_id=1, source_target_pairs={{0,8},{1,4},{2,10},{3,6},{4,12},{5,0},{6,14},{7,2},{8,13},{9,1},{1... | collective-permute-start | bytes 786440 | tf_op jit(solution)/shard_map/ppermute | solution.py:143
  22.5 4.4 %collective-permute-start.7 = (f32[256,256]{1,0:T(8,128)S(1)}, f32[256,256]{1,0:T(8,128)S(1)}, u32[]{:S(2)}, u32[]{:S(2)}) collective-permute-start(f32[256,256]{1,0:T(8,128)S(1)} %get-tuple-element.18), channel_id=1, source_target_pairs={{0,1},{1,0},{2,3},{3,2},{4,5},{5,4},{6,7},{7,6},{8,9},{9,8},{10,11... | collective-permute-start | bytes 786440 | tf_op jit(solution)/shard_map/ppermute | solution.py:143
  23.0 3.0 %collective-permute-start.10 = (f32[256,256]{1,0:T(8,128)S(1)}, f32[256,256]{1,0:T(8,128)S(1)}, u32[]{:S(2)}, u32[]{:S(2)}) collective-permute-start(f32[256,256]{1,0:T(8,128)S(1)} %get-tuple-element.21), channel_id=1, source_target_pairs={{0,1},{1,0},{2,3},{3,2},{4,5},{5,4},{6,7},{7,6},{8,9},{9,8},{10,11... | collective-permute-start | bytes 786440 | tf_op jit(solution)/shard_map/ppermute | solution.py:143
  24.1 2.0 %collective-permute-start.11 = (f32[256,256]{1,0:T(8,128)S(1)}, f32[256,256]{1,0:T(8,128)S(1)}, u32[]{:S(2)}, u32[]{:S(2)}) collective-permute-start(f32[256,256]{1,0:T(8,128)S(1)} %get-tuple-element.22), channel_id=1, source_target_pairs={{0,1},{1,0},{2,3},{3,2},{4,5},{5,4},{6,7},{7,6},{8,9},{9,8},{10,11... | collective-permute-start | bytes 786440 | tf_op jit(solution)/shard_map/ppermute | solution.py:143
  25.9 1.6 %collective-permute-start.8 = (f32[256,256]{1,0:T(8,128)S(1)}, f32[256,256]{1,0:T(8,128)S(1)}, u32[]{:S(2)}, u32[]{:S(2)}) collective-permute-start(f32[256,256]{1,0:T(8,128)S(1)} %get-tuple-element.19), channel_id=1, source_target_pairs={{0,1},{1,0},{2,3},{3,2},{4,5},{5,4},{6,7},{7,6},{8,9},{9,8},{10,11... | collective-permute-start | bytes 786440 | tf_op jit(solution)/shard_map/ppermute | solution.py:143

commit v6 on v5

--- a/solution.py
+++ b/solution.py
@@ -37,11 +37,15 @@
 
 
 def multiply_kernel(pairs, *refs, groups, parts, width):
-    keep, *sends, sums = refs[-2 - len(parts) :]
+    keep, send, sums = refs[-3:]
     refs = list(refs)
     blocks = [[refs.pop(0) if used else None for used in group] for group in groups]
     pieces = refs[:2]
     row, col = lax.axis_index("row"), lax.axis_index("col")
+    bit = lax.broadcasted_iota(jnp.int32, pairs.shape, 0) * 4
+    bit = bit + lax.broadcasted_iota(jnp.int32, pairs.shape, 1)
+    table = jnp.where(pairs[...] != 0, jnp.left_shift(1, bit), 0)
+    table = jnp.sum(table.astype(jnp.float32)).astype(jnp.int32)
     mine = pl.multiple_of((col & 1) * width, width)
     other = pl.multiple_of(width - mine, width)
     turned = (((row >> 1) ^ col) & 1) == 1
@@ -55,7 +59,7 @@
         for slot, label, when_turned in choices:
             block = blocks[index][label]
             kind = ((row ^ (2 * slot + (part & 1))) + owner) & 3
-            listed = pairs[owner, kind] != 0
+            listed = (lax.shift_right_logical(table, owner * 4 + kind) & 1) == 1
             if when_turned is not None:
                 listed = listed & (turned if when_turned else ~turned)
             here = kind == ((row + col) & 3)
@@ -70,7 +74,7 @@
                     )
 
         keep[index] = sums[:, pl.ds(mine, width)]
-        sends[index][...] = sums[:, pl.ds(other, width)]
+        send[index] = sums[:, pl.ds(other, width)]
 
 
 def multiply(block_list, groups, pieces, parts, cost):
@@ -78,13 +82,12 @@
     blocks = [block for group in groups for block in group if block is not None]
     rows, width = blocks[0].shape[0], pieces[0].shape[1] // 2
     keep = jax.ShapeDtypeStruct((len(parts), rows, width), jnp.float32)
-    send = jax.ShapeDtypeStruct((rows, width), jnp.float32)
     used = tuple(tuple(block is not None for block in group) for group in groups)
     return pl.pallas_call(
         functools.partial(multiply_kernel, groups=used, parts=parts, width=width),
-        out_shape=(keep,) + (send,) * len(parts),
-        in_specs=[pl.BlockSpec(memory_space=pltpu.SMEM)] + [vmem] * (len(blocks) + 2),
-        out_specs=(vmem,) * (1 + len(parts)),
+        out_shape=(keep, keep),
+        in_specs=[vmem] * (len(blocks) + 3),
+        out_specs=(vmem, vmem),
         scratch_shapes=[pltpu.VMEM((rows, 2 * width), jnp.float32)],
         cost_estimate=pl.CostEstimate(flops=cost, transcendentals=0, bytes_accessed=2**20),
         compiler_params=pltpu.CompilerParams(vmem_limit_bytes=8 * 2**20),
@@ -98,7 +101,7 @@
     width = held.shape[2]
     copies = []
     for place, (part, kept, received) in enumerate(terms):
-        held[place] = refs[kept[0]][kept[1]] + refs[received][...]
+        held[place] = refs[kept[0]][kept[1]] + refs[received[0]][received[1]]
         start = pl.multiple_of((col ^ part) * width, width)
         copy = pltpu.make_async_copy(
             held.at[place], out.at[:, pl.ds(start, width)], sems.at[place]
@@ -166,14 +169,14 @@
     cost = 2 * 2 * amps.shape[0] * amps.shape[1] * width
     run = functools.partial(multiply, block_list, pieces=pieces)
     groups = [[amps, near1, near2, None], [far0, far1, far2, None]]
-    keep, *sends = run(groups=groups, parts=(0, 2), cost=15 * cost)
-    received0, received2 = [beside(send) for send in sends]
+    keep, send = run(groups=groups, parts=(0, 2), cost=15 * cost)
+    received = beside(send)
     keep1, send1 = run(groups=[[None, near1, near2, near3]], parts=(1,), cost=15 * cost)
     received1 = beside(send1)
     keep3, send3 = run(groups=[[None, far1, far2, far3]], parts=(3,), cost=cost)
     received3 = beside(send3)
-    out = add([keep, keep1, received0, received1], ((0, (0, 0), 3), (1, (1, 0), 2)))
-    out = add([keep, keep3, received2, received3], ((2, (0, 1), 3), (3, (1, 0), 2)), out)
+    out = add([keep, keep1, received, received1], ((0, (0, 0), (3, 0)), (1, (1, 0), (2, 0))))
+    out = add([keep, keep3, received, received3], ((2, (0, 1), (3, 0)), (3, (1, 0), (2, 1))), out)
     return out[None]
 
 

time: 28.5 us -> 28.1 us (0.986)
  Pallas kernels: 4.95 us -> 3.52 us
  waiting for transfers between devices: 9.2 us -> 10.6 us
  starting transfers between devices: 12.8 us -> 12.4 us
    pallas_call x3, Pallas kernels: 3.28 us -> 1.86 us  [multiply(): pl.pallas_call(functools.partial(multiply_kernel, groups=used, parts=part...]
    ppermute x12 -> x11, waiting for transfers between devices: 9.2 us -> 10.6 us  [moved(): return lax.ppermute(block, GRID, route)]
    ppermute x12 -> x11, starting transfers between devices: 12.8 us -> 12.4 us  [moved(): return lax.ppermute(block, GRID, route)]
  transfers between devices with their start and end apart: 12 -> 11, of which waited for: 4 -> 4; matrix products, arithmetic and copies ran while one was open for 5% -> 5% of each run, Pallas kernels for 14% -> 10%
where the time goes in v6:
time: 28.1 us; the launch traced here: 27.9 us
  starting transfers between devices  12.4 us (44%)
  waiting for transfers between devices  10.6 us (38%)
  Pallas kernels  3.52 us (13%)
  local copies, waits for them, and re-layouts  1.32 us (5%)
    ppermute x11, starting transfers between devices, moved(): return lax.ppermute(block, GRID, route)  12.4 us
    ppermute x11, waiting for transfers between devices, moved(): return lax.ppermute(block, GRID, route)  10.6 us
    pallas_call x3, Pallas kernels, multiply(): pl.pallas_call(functools.partial(multiply_kernel, groups=used, parts=part...  1.86 us
    pallas_call x2, Pallas kernels, add(): pl.pallas_call(functools.partial(add_kernel, terms=terms), out_shape=jax....  1.67 us
    dynamic_slice x1, local copies, waits for them, and re-layouts, chip_columns(): return lax.dynamic_slice_in_dim(ints, chip * 2 * width, 2 * width, 1)  1.31 us
  transfers between devices with their start and end apart: 11, of which 4 were waited for; matrix products, arithmetic and copies ran while one was open for 5% of the time, Pallas kernels for 10%

profile of v6, /device:TPU:0, one launch (start us, length us, event | category | flops | bytes accessed | tf_op | source)
XLA Modules:
  0.0 27.9 jit_solution(4674680404449604419)
XLA Ops:
  0.0 2.9 %collective-permute-start.1 = (bf16[256,512]{1,0:T(8,128)(2,1)}, bf16[256,512]{1,0:T(8,128)(2,1)S(1)}, u32[]{:S(2)}, u32[]{:S(2)}) collective-permute-start(bf16[256,512]{1,0:T(8,128)(2,1)} %refs_0_.1), channel_id=1, source_target_pairs={{0,2},{1,3},{2,0},{3,1},{4,6},{5,7},{6,4},{7,5},{8,10},{9,11},{10,... | collective-permute-start | bytes 786440 | tf_op jit(solution)/shard_map/ppermute | solution.py:146
  2.9 0.7 %collective-permute-start.2 = (bf16[256,512]{1,0:T(8,128)(2,1)}, bf16[256,512]{1,0:T(8,128)(2,1)S(1)}, u32[]{:S(2)}, u32[]{:S(2)}) collective-permute-start(bf16[256,512]{1,0:T(8,128)(2,1)} %refs_0_.1), channel_id=1, source_target_pairs={{0,5},{1,9},{2,7},{3,11},{4,1},{5,13},{6,3},{7,15},{8,0},{9,12},{1... | collective-permute-start | bytes 786440 | tf_op jit(solution)/shard_map/ppermute | solution.py:146
  3.6 1.3 %constant_dynamic-slice_fusion = (bf16[512,512]{1,0:T(8,128)(2,1)S(1)}, bf16[512,512]{1,0:T(8,128)(2,1)S(1)}) fusion(bf16[512,1024]{1,0:T(8,128)(2,1)} %param.4, s32[]{:T(128)S(6)} %select_n.13, s32[]{:T(128)S(6)} %select_n.12), kind=kLoop, calls=%fused_computation | loop fusion | bytes 2097160 | tf_op jit(solution)/shard_map/dynamic_slice | solution.py:157
  4.9 0.0 copy-start
  4.9 0.6 %collective-permute-start.5 = (bf16[512,512]{1,0:T(8,128)(2,1)S(1)}, bf16[512,512]{1,0:T(8,128)(2,1)S(1)}, u32[]{:S(2)}, u32[]{:S(2)}) collective-permute-start(bf16[512,512]{1,0:T(8,128)(2,1)S(1)} %get-tuple-element.21), channel_id=1, source_target_pairs={{0,2},{1,3},{2,0},{3,1},{4,6},{5,7},{6,4},{7,5},{8,10},{9,11},{10,... | collective-permute-start | bytes 1572872 | tf_op jit(solution)/shard_map/ppermute | solution.py:146
  5.5 0.9 %collective-permute-start = (bf16[256,512]{1,0:T(8,128)(2,1)S(1)}, bf16[256,512]{1,0:T(8,128)(2,1)S(1)}, u32[]{:S(2)}, u32[]{:S(2)}) collective-permute-start(bf16[256,512]{1,0:T(8,128)(2,1)S(1)} %copy-done.1), channel_id=1, source_target_pairs={{0,8},{1,4},{2,10},{3,6},{4,12},{5,0},{6,14},{7,2},{8,13},{9,1},{1... | collective-permute-start | bytes 786440 | tf_op jit(solution)/shard_map/ppermute | solution.py:146
  6.5 3.8 %collective-permute-done.1.refs_3_ = bf16[256,512]{1,0:T(8,128)(2,1)S(1)} collective-permute-done((bf16[256,512]{1,0:T(8,128)(2,1)}, bf16[256,512]{1,0:T(8,128)(2,1)S(1)}, u32[]{:S(2)}, u32[]{:S(2)}) %collective-permute-start.1) | collective-permute-done | bytes 262176 | tf_op jit(solution)/shard_map/ppermute | solution.py:146
  10.3 0.0 collective-permute-done.2.refs_2_.refs_1_
  10.3 2.0 %collective-permute-start.3 = (bf16[256,512]{1,0:T(8,128)(2,1)S(1)}, bf16[256,512]{1,0:T(8,128)(2,1)S(1)}, u32[]{:S(2)}, u32[]{:S(2)}) collective-permute-start(bf16[256,512]{1,0:T(8,128)(2,1)S(1)} %collective-permute-done.1.refs_3_), channel_id=1, source_target_pairs={{0,8},{1,4},{2,10},{3,6},{4,12},{5,0},{6,14},{7,2},{8,13},{9,1},{1... | collective-permute-start | bytes 786440 | tf_op jit(solution)/shard_map/ppermute | solution.py:146
  12.4 0.0 collective-permute-start.4
  12.4 0.0 collective-permute-done.refs_1_.refs_0_
  12.4 2.0 %collective-permute-start.9 = (bf16[256,512]{1,0:T(8,128)(2,1)S(1)}, bf16[256,512]{1,0:T(8,128)(2,1)S(1)}, u32[]{:S(2)}, u32[]{:S(2)}) collective-permute-start(bf16[256,512]{1,0:T(8,128)(2,1)S(1)} %collective-permute-done.refs_1_.refs_0_), channel_id=1, source_target_pairs={{0,8},{1,4},{2,10},{3,6},{4,12},{5,0},{6,14},{7,2},{8,13},{9,1},{1... | collective-permute-start | bytes 786440 | tf_op jit(solution)/shard_map/ppermute | solution.py:146
  14.4 4.2 %collective-permute-done.3.refs_4_.refs_0_ = bf16[256,512]{1,0:T(8,128)(2,1)S(1)} collective-permute-done((bf16[256,512]{1,0:T(8,128)(2,1)S(1)}, bf16[256,512]{1,0:T(8,128)(2,1)S(1)}, u32[]{:S(2)}, u32[]{:S(2)}) %collective-permute-start.3) | collective-permute-done | bytes 262176 | tf_op jit(solution)/shard_map/ppermute | solution.py:146
  18.6 2.5 %collective-permute-start.6 = (bf16[256,512]{1,0:T(8,128)(2,1)S(1)}, bf16[256,512]{1,0:T(8,128)(2,1)S(1)}, u32[]{:S(2)}, u32[]{:S(2)}) collective-permute-start(bf16[256,512]{1,0:T(8,128)(2,1)S(1)} %collective-permute-done.3.refs_4_.refs_0_), channel_id=1, source_target_pairs={{0,8},{1,4},{2,10},{3,6},{4,12},{5,0},{6,14},{7,2},{8,13},{9,1},{1... | collective-permute-start | bytes 786440 | tf_op jit(solution)/shard_map/ppermute | solution.py:146
  21.1 0.9 %multiply.7 = (f32[2,256,256]{2,1,0:T(8,128)S(1)}, f32[2,256,256]{2,1,0:T(8,128)S(1)}) custom-call(s32[4,4]{1,0:T(4,128)S(1)} %copy-done, bf16[256,512]{1,0:T(8,128)(2,1)S(1)} %copy-done.1, bf16[256,512]{1,0:T(8,128)(2,1)S(1)} %collective-permute-done.refs_1_.refs_0_, bf16[256,512]{1,0:T(8,128)(2,1)S(1)} %collective-permute-done.2.refs_2_.refs_1_, ...), custom_call_target="tpu_custom_call" | custom-call | flops 2013265920 | bytes 1048576 | tf_op jit(solution)/shard_map/multiply/pallas_call | solution.py:86
  22.0 0.5 %collective-permute-start.7 = (f32[2,256,256]{2,1,0:T(8,128)S(1)}, f32[2,256,256]{2,1,0:T(8,128)S(1)}, u32[]{:S(2)}, u32[]{:S(2)}) collective-permute-start(f32[2,256,256]{2,1,0:T(8,128)S(1)} %get-tuple-element.17), channel_id=1, source_target_pairs={{0,1},{1,0},{2,3},{3,2},{4,5},{5,4},{6,7},{7,6},{8,9},{9,8},{10,11... | collective-permute-start | bytes 1572872 | tf_op jit(solution)/shard_map/ppermute | solution.py:146
  22.5 0.5 %multiply.9 = (f32[1,256,256]{2,1,0:T(8,128)S(1)}, f32[1,256,256]{2,1,0:T(8,128)S(1)}) custom-call(s32[4,4]{1,0:T(4,128)S(1)} %copy-done, bf16[256,512]{1,0:T(8,128)(2,1)S(1)} %collective-permute-done.refs_1_.refs_0_, bf16[256,512]{1,0:T(8,128)(2,1)S(1)} %collective-permute-done.2.refs_2_.refs_1_, bf16[256,512]{1,0:T(8,128)(2,1)S(1)} %collective-permute-done.9.refs_2_, ...), custom_call_target="tpu_custom_call" | custom-call | flops 2013265920 | bytes 1048576 | tf_op jit(solution)/shard_map/multiply/pallas_call | solution.py:86
  23.0 0.1 collective-permute-start.10
  23.1 1.9 %collective-permute-done.6.refs_2_ = bf16[256,512]{1,0:T(8,128)(2,1)S(1)} collective-permute-done((bf16[256,512]{1,0:T(8,128)(2,1)S(1)}, bf16[256,512]{1,0:T(8,128)(2,1)S(1)}, u32[]{:S(2)}, u32[]{:S(2)}) %collective-permute-start.6) | collective-permute-done | bytes 262176 | tf_op jit(solution)/shard_map/ppermute | solution.py:146
  25.0 0.5 %multiply.8 = (f32[1,256,256]{2,1,0:T(8,128)S(1)}, f32[1,256,256]{2,1,0:T(8,128)S(1)}) custom-call(s32[4,4]{1,0:T(4,128)S(1)} %copy-done, bf16[256,512]{1,0:T(8,128)(2,1)S(1)} %collective-permute-done.3.refs_4_.refs_0_, bf16[256,512]{1,0:T(8,128)(2,1)S(1)} %collective-permute-done.4.refs_5_.refs_1_, bf16[256,512]{1,0:T(8,128)(2,1)S(1)} %collective-permute-done.6.refs_2_, ...), custom_call_target="tpu_custom_call" | custom-call | flops 134217728 | bytes 1048576 | tf_op jit(solution)/shard_map/multiply/pallas_call | solution.py:86
  25.5 0.1 collective-permute-start.8
  25.6 0.8 %add.11.refs_4_ = f32[256,1024]{1,0:T(8,128)} custom-call(f32[2,256,256]{2,1,0:T(8,128)S(1)} %get-tuple-element.15.refs_0_, f32[1,256,256]{2,1,0:T(8,128)S(1)} %get-tuple-element.19.refs_1_, f32[2,256,256]{2,1,0:T(8,128)S(1)} %collective-permute-done.7.refs_2_, f32[1,256,256]{2,1,0:T(8,128)S(1)} %collective-permute-done.10.refs_3_), custom_call_target="tpu_custom_call" | custom-call | tf_op jit(solution)/shard_map/add/pallas_call | solution.py:120
  26.4 0.7 %collective-permute-done.8.refs_3_ = f32[1,256,256]{2,1,0:T(8,128)S(1)} collective-permute-done((f32[1,256,256]{2,1,0:T(8,128)S(1)}, f32[1,256,256]{2,1,0:T(8,128)S(1)}, u32[]{:S(2)}, u32[]{:S(2)}) %collective-permute-start.8) | collective-permute-done | bytes 262176 | tf_op jit(solution)/shard_map/ppermute | solution.py:146
  27.1 0.8 %add.12 = f32[256,1024]{1,0:T(8,128)} custom-call(f32[2,256,256]{2,1,0:T(8,128)S(1)} %get-tuple-element.15.refs_0_, f32[1,256,256]{2,1,0:T(8,128)S(1)} %get-tuple-element.16.refs_1_, f32[2,256,256]{2,1,0:T(8,128)S(1)} %collective-permute-done.7.refs_2_, f32[1,256,256]{2,1,0:T(8,128)S(1)} %collective-permute-done.8.refs_3_, ...), custom_call_target="tpu_custom_call", output_to_operand_aliasing={{}: (4, {})} | custom-call | tf_op jit(solution)/shard_map/add/pallas_call | solution.py:120
  (8 shorter events, 0.0 us)
Async XLA Ops:
  0.0 10.3 %collective-permute-start.1 = (bf16[256,512]{1,0:T(8,128)(2,1)}, bf16[256,512]{1,0:T(8,128)(2,1)S(1)}, u32[]{:S(2)}, u32[]{:S(2)}) collective-permute-start(bf16[256,512]{1,0:T(8,128)(2,1)} %refs_0_.1), channel_id=1, source_target_pairs={{0,2},{1,3},{2,0},{3,1},{4,6},{5,7},{6,4},{7,5},{8,10},{9,11},{10,... | collective-permute-start | bytes 786440 | tf_op jit(solution)/shard_map/ppermute | solution.py:146
  2.9 7.4 %collective-permute-start.2 = (bf16[256,512]{1,0:T(8,128)(2,1)}, bf16[256,512]{1,0:T(8,128)(2,1)S(1)}, u32[]{:S(2)}, u32[]{:S(2)}) collective-permute-start(bf16[256,512]{1,0:T(8,128)(2,1)} %refs_0_.1), channel_id=1, source_target_pairs={{0,5},{1,9},{2,7},{3,11},{4,1},{5,13},{6,3},{7,15},{8,0},{9,12},{1... | collective-permute-start | bytes 786440 | tf_op jit(solution)/shard_map/ppermute | solution.py:146
  3.6 1.9 %copy-start.1 = (bf16[256,512]{1,0:T(8,128)(2,1)S(1)}, bf16[256,512]{1,0:T(8,128)(2,1)}, u32[]{:S(2)}) copy-start(bf16[256,512]{1,0:T(8,128)(2,1)} %refs_0_.1) | copy-start | bytes 786436
  4.9 16.2 %copy-start = (s32[4,4]{1,0:T(4,128)S(1)}, s32[4,4]{1,0:T(4,128)}, u32[]{:S(2)}) copy-start(s32[4,4]{1,0:T(4,128)} %pairs.5) | copy-start | bytes 196
  4.9 16.2 %collective-permute-start.5 = (bf16[512,512]{1,0:T(8,128)(2,1)S(1)}, bf16[512,512]{1,0:T(8,128)(2,1)S(1)}, u32[]{:S(2)}, u32[]{:S(2)}) collective-permute-start(bf16[512,512]{1,0:T(8,128)(2,1)S(1)} %get-tuple-element.21), channel_id=1, source_target_pairs={{0,2},{1,3},{2,0},{3,1},{4,6},{5,7},{6,4},{7,5},{8,10},{9,11},{10,... | collective-permute-start | bytes 1572872 | tf_op jit(solution)/shard_map/ppermute | solution.py:146
  5.5 6.8 %collective-permute-start = (bf16[256,512]{1,0:T(8,128)(2,1)S(1)}, bf16[256,512]{1,0:T(8,128)(2,1)S(1)}, u32[]{:S(2)}, u32[]{:S(2)}) collective-permute-start(bf16[256,512]{1,0:T(8,128)(2,1)S(1)} %copy-done.1), channel_id=1, source_target_pairs={{0,8},{1,4},{2,10},{3,6},{4,12},{5,0},{6,14},{7,2},{8,13},{9,1},{1... | collective-permute-start | bytes 786440 | tf_op jit(solution)/shard_map/ppermute | solution.py:146
  10.3 8.3 %collective-permute-start.3 = (bf16[256,512]{1,0:T(8,128)(2,1)S(1)}, bf16[256,512]{1,0:T(8,128)(2,1)S(1)}, u32[]{:S(2)}, u32[]{:S(2)}) collective-permute-start(bf16[256,512]{1,0:T(8,128)(2,1)S(1)} %collective-permute-done.1.refs_3_), channel_id=1, source_target_pairs={{0,8},{1,4},{2,10},{3,6},{4,12},{5,0},{6,14},{7,2},{8,13},{9,1},{1... | collective-permute-start | bytes 786440 | tf_op jit(solution)/shard_map/ppermute | solution.py:146
  12.4 8.7 %collective-permute-start.4 = (bf16[256,512]{1,0:T(8,128)(2,1)S(1)}, bf16[256,512]{1,0:T(8,128)(2,1)S(1)}, u32[]{:S(2)}, u32[]{:S(2)}) collective-permute-start(bf16[256,512]{1,0:T(8,128)(2,1)S(1)} %collective-permute-done.1.refs_3_), channel_id=1, source_target_pairs={{0,5},{1,9},{2,7},{3,11},{4,1},{5,13},{6,3},{7,15},{8,0},{9,12},{1... | collective-permute-start | bytes 786440 | tf_op jit(solution)/shard_map/ppermute | solution.py:146
  12.4 10.2 %collective-permute-start.9 = (bf16[256,512]{1,0:T(8,128)(2,1)S(1)}, bf16[256,512]{1,0:T(8,128)(2,1)S(1)}, u32[]{:S(2)}, u32[]{:S(2)}) collective-permute-start(bf16[256,512]{1,0:T(8,128)(2,1)S(1)} %collective-permute-done.refs_1_.refs_0_), channel_id=1, source_target_pairs={{0,8},{1,4},{2,10},{3,6},{4,12},{5,0},{6,14},{7,2},{8,13},{9,1},{1... | collective-permute-start | bytes 786440 | tf_op jit(solution)/shard_map/ppermute | solution.py:146
  18.6 6.4 %collective-permute-start.6 = (bf16[256,512]{1,0:T(8,128)(2,1)S(1)}, bf16[256,512]{1,0:T(8,128)(2,1)S(1)}, u32[]{:S(2)}, u32[]{:S(2)}) collective-permute-start(bf16[256,512]{1,0:T(8,128)(2,1)S(1)} %collective-permute-done.3.refs_4_.refs_0_), channel_id=1, source_target_pairs={{0,8},{1,4},{2,10},{3,6},{4,12},{5,0},{6,14},{7,2},{8,13},{9,1},{1... | collective-permute-start | bytes 786440 | tf_op jit(solution)/shard_map/ppermute | solution.py:146
  22.0 3.6 %collective-permute-start.7 = (f32[2,256,256]{2,1,0:T(8,128)S(1)}, f32[2,256,256]{2,1,0:T(8,128)S(1)}, u32[]{:S(2)}, u32[]{:S(2)}) collective-permute-start(f32[2,256,256]{2,1,0:T(8,128)S(1)} %get-tuple-element.17), channel_id=1, source_target_pairs={{0,1},{1,0},{2,3},{3,2},{4,5},{5,4},{6,7},{7,6},{8,9},{9,8},{10,11... | collective-permute-start | bytes 1572872 | tf_op jit(solution)/shard_map/ppermute | solution.py:146
  23.0 2.5 %collective-permute-start.10 = (f32[1,256,256]{2,1,0:T(8,128)S(1)}, f32[1,256,256]{2,1,0:T(8,128)S(1)}, u32[]{:S(2)}, u32[]{:S(2)}) collective-permute-start(f32[1,256,256]{2,1,0:T(8,128)S(1)} %get-tuple-element.20), channel_id=1, source_target_pairs={{0,1},{1,0},{2,3},{3,2},{4,5},{5,4},{6,7},{7,6},{8,9},{9,8},{10,11... | collective-permute-start | bytes 786440 | tf_op jit(solution)/shard_map/ppermute | solution.py:146
  25.5 1.6 %collective-permute-start.8 = (f32[1,256,256]{2,1,0:T(8,128)S(1)}, f32[1,256,256]{2,1,0:T(8,128)S(1)}, u32[]{:S(2)}, u32[]{:S(2)}) collective-permute-start(f32[1,256,256]{2,1,0:T(8,128)S(1)} %get-tuple-element.18), channel_id=1, source_target_pairs={{0,1},{1,0},{2,3},{3,2},{4,5},{5,4},{6,7},{7,6},{8,9},{9,8},{10,11... | collective-permute-start | bytes 786440 | tf_op jit(solution)/shard_map/ppermute | solution.py:146

commit v7 on v6

--- a/solution.py
+++ b/solution.py
@@ -36,11 +36,12 @@
     return owned.reshape(1, owned.shape[0], owned.shape[1])
 
 
-def multiply_kernel(pairs, *refs, groups, parts, width):
-    keep, send, sums = refs[-3:]
+def multiply_kernel(pairs, *refs, groups, parts, opening, begun, width):
     refs = list(refs)
     blocks = [[refs.pop(0) if used else None for used in group] for group in groups]
-    pieces = refs[:2]
+    pieces, refs = refs[:2], refs[2:]
+    started = refs.pop(0) if begun else None
+    keep, send, *opened, sums = refs
     row, col = lax.axis_index("row"), lax.axis_index("col")
     bit = lax.broadcasted_iota(jnp.int32, pairs.shape, 0) * 4
     bit = bit + lax.broadcasted_iota(jnp.int32, pairs.shape, 1)
@@ -49,15 +50,21 @@
     mine = pl.multiple_of((col & 1) * width, width)
     other = pl.multiple_of(width - mine, width)
     turned = (((row >> 1) ^ col) & 1) == 1
-    for index, part in enumerate(parts):
+    for index, part in enumerate(parts + opening):
         owner = col ^ part
-        sums[...] = jnp.zeros(sums.shape, sums.dtype)
+        total = sums if index < len(parts) else opened[0]
+        if begun and index == 0:
+            total[...] = started[...]
+        else:
+            total[...] = jnp.zeros(total.shape, total.dtype)
         if part & 1 == 0:
             choices = ((0, 0, None), (1, 1, True), (1, 2, False))
         else:
             choices = ((0, 1, False), (0, 2, True), (1, 3, None))
         for slot, label, when_turned in choices:
             block = blocks[index][label]
+            if block is None:
+                continue
             kind = ((row ^ (2 * slot + (part & 1))) + owner) & 3
             listed = (lax.shift_right_logical(table, owner * 4 + kind) & 1) == 1
             if when_turned is not None:
@@ -68,31 +75,41 @@
                     continue
 
                 @pl.when(listed & (here == (source == 0)))
-                def _(block=block, source=source):
-                    sums[...] += jnp.dot(
+                def _(block=block, source=source, total=total):
+                    total[...] += jnp.dot(
                         block[...], pieces[source][...], preferred_element_type=jnp.float32
                     )
 
-        keep[index] = sums[:, pl.ds(mine, width)]
-        send[index] = sums[:, pl.ds(other, width)]
-
-
-def multiply(block_list, groups, pieces, parts, cost):
+        if index < len(parts):
+            keep[index] = sums[:, pl.ds(mine, width)]
+            send[index] = sums[:, pl.ds(other, width)]
+
+
+def multiply(block_list, groups, pieces, parts, cost, opening=(), begun=None):
     vmem = pl.BlockSpec(memory_space=pltpu.VMEM)
     blocks = [block for group in groups for block in group if block is not None]
+    operands = [block_list, *blocks, *pieces] + ([] if begun is None else [begun])
     rows, width = blocks[0].shape[0], pieces[0].shape[1] // 2
     keep = jax.ShapeDtypeStruct((len(parts), rows, width), jnp.float32)
+    full = jax.ShapeDtypeStruct((rows, 2 * width), jnp.float32)
     used = tuple(tuple(block is not None for block in group) for group in groups)
     return pl.pallas_call(
-        functools.partial(multiply_kernel, groups=used, parts=parts, width=width),
-        out_shape=(keep, keep),
-        in_specs=[vmem] * (len(blocks) + 3),
-        out_specs=(vmem, vmem),
-        scratch_shapes=[pltpu.VMEM((rows, 2 * width), jnp.float32)],
+        functools.partial(
+            multiply_kernel,
+            groups=used,
+            parts=parts,
+            opening=opening,
+            begun=begun is not None,
+            width=width,
+        ),
+        out_shape=(keep, keep) + (full,) * len(opening),
+        in_specs=[vmem] * len(operands),
+        out_specs=(vmem,) * (2 + len(opening)),
+        scratch_shapes=[pltpu.VMEM(full.shape, full.dtype)],
         cost_estimate=pl.CostEstimate(flops=cost, transcendentals=0, bytes_accessed=2**20),
         compiler_params=pltpu.CompilerParams(vmem_limit_bytes=8 * 2**20),
         name="multiply",
-    )(block_list, *blocks, *pieces)
+    )(*operands)
 
 
 def add_kernel(*refs, terms):
@@ -171,12 +188,15 @@
     groups = [[amps, near1, near2, None], [far0, far1, far2, None]]
     keep, send = run(groups=groups, parts=(0, 2), cost=15 * cost)
     received = beside(send)
-    keep1, send1 = run(groups=[[None, near1, near2, near3]], parts=(1,), cost=15 * cost)
+    groups = [[None, near1, near2, near3], [None, far1, far2, None]]
+    keep1, send1, begun = run(groups=groups, parts=(1,), cost=15 * cost, opening=(3,))
     received1 = beside(send1)
-    keep3, send3 = run(groups=[[None, far1, far2, far3]], parts=(3,), cost=cost)
+    groups = [[None, None, None, far3]]
+    keep3, send3 = run(groups=groups, parts=(3,), cost=cost, begun=begun)
     received3 = beside(send3)
-    out = add([keep, keep1, received, received1], ((0, (0, 0), (3, 0)), (1, (1, 0), (2, 0))))
-    out = add([keep, keep3, received, received3], ((2, (0, 1), (3, 0)), (3, (1, 0), (2, 1))), out)
+    sums = [keep, keep1, keep3, received, received1]
+    out = add(sums, ((0, (0, 0), (4, 0)), (1, (1, 0), (3, 0)), (3, (2, 0), (3, 1))))
+    out = add([keep, received3], ((2, (0, 1), (1, 0)),), out)
     return out[None]
 
 

time: 28.1 us -> 27.9 us (level)
  waiting for transfers between devices: 10.6 us -> 10.2 us
  starting transfers between devices: 12.4 us -> 12.7 us
    ppermute x11, waiting for transfers between devices: 10.6 us -> 10.2 us  [moved(): return lax.ppermute(block, GRID, route)]
    ppermute x11, starting transfers between devices: 12.4 us -> 12.7 us  [moved(): return lax.ppermute(block, GRID, route)]
where the time goes in v7:
time: 27.9 us; the launch traced here: 27.8 us
  starting transfers between devices  12.7 us (46%)
  waiting for transfers between devices  10.2 us (37%)
  Pallas kernels  3.54 us (13%)
  local copies, waits for them, and re-layouts  1.32 us (5%)
    ppermute x11, starting transfers between devices, moved(): return lax.ppermute(block, GRID, route)  12.7 us
    ppermute x11, waiting for transfers between devices, moved(): return lax.ppermute(block, GRID, route)  10.2 us
    pallas_call x3, Pallas kernels, multiply(): pl.pallas_call(functools.partial(multiply_kernel, groups=used, parts=part...  1.87 us
    pallas_call x2, Pallas kernels, add(): pl.pallas_call(functools.partial(add_kernel, terms=terms), out_shape=jax....  1.67 us
    dynamic_slice x1, local copies, waits for them, and re-layouts, chip_columns(): return lax.dynamic_slice_in_dim(ints, chip * 2 * width, 2 * width, 1)  1.31 us
  transfers between devices with their start and end apart: 11, of which 4 were waited for; matrix products, arithmetic and copies ran while one was open for 5% of the time, Pallas kernels for 10%

profile of v7, /device:TPU:0, one launch (start us, length us, event | category | flops | bytes accessed | tf_op | source)
XLA Modules:
  0.0 27.8 jit_solution(1735415345768650762)
XLA Ops:
  0.0 2.9 %collective-permute-start.1 = (bf16[256,512]{1,0:T(8,128)(2,1)}, bf16[256,512]{1,0:T(8,128)(2,1)S(1)}, u32[]{:S(2)}, u32[]{:S(2)}) collective-permute-start(bf16[256,512]{1,0:T(8,128)(2,1)} %refs_0_.1), channel_id=1, source_target_pairs={{0,2},{1,3},{2,0},{3,1},{4,6},{5,7},{6,4},{7,5},{8,10},{9,11},{10,... | collective-permute-start | bytes 786440 | tf_op jit(solution)/shard_map/ppermute | solution.py:163
  2.9 0.7 %collective-permute-start.2 = (bf16[256,512]{1,0:T(8,128)(2,1)}, bf16[256,512]{1,0:T(8,128)(2,1)S(1)}, u32[]{:S(2)}, u32[]{:S(2)}) collective-permute-start(bf16[256,512]{1,0:T(8,128)(2,1)} %refs_0_.1), channel_id=1, source_target_pairs={{0,5},{1,9},{2,7},{3,11},{4,1},{5,13},{6,3},{7,15},{8,0},{9,12},{1... | collective-permute-start | bytes 786440 | tf_op jit(solution)/shard_map/ppermute | solution.py:163
  3.6 1.3 %constant_dynamic-slice_fusion = (bf16[512,512]{1,0:T(8,128)(2,1)S(1)}, bf16[512,512]{1,0:T(8,128)(2,1)S(1)}) fusion(bf16[512,1024]{1,0:T(8,128)(2,1)} %param.4, s32[]{:T(128)S(6)} %select_n.13, s32[]{:T(128)S(6)} %select_n.12), kind=kLoop, calls=%fused_computation | loop fusion | bytes 2097160 | tf_op jit(solution)/shard_map/dynamic_slice | solution.py:174
  4.9 0.0 copy-start
  4.9 0.6 %collective-permute-start.5 = (bf16[512,512]{1,0:T(8,128)(2,1)S(1)}, bf16[512,512]{1,0:T(8,128)(2,1)S(1)}, u32[]{:S(2)}, u32[]{:S(2)}) collective-permute-start(bf16[512,512]{1,0:T(8,128)(2,1)S(1)} %get-tuple-element.23), channel_id=1, source_target_pairs={{0,2},{1,3},{2,0},{3,1},{4,6},{5,7},{6,4},{7,5},{8,10},{9,11},{10,... | collective-permute-start | bytes 1572872 | tf_op jit(solution)/shard_map/ppermute | solution.py:163
  5.5 0.9 %collective-permute-start = (bf16[256,512]{1,0:T(8,128)(2,1)S(1)}, bf16[256,512]{1,0:T(8,128)(2,1)S(1)}, u32[]{:S(2)}, u32[]{:S(2)}) collective-permute-start(bf16[256,512]{1,0:T(8,128)(2,1)S(1)} %copy-done.1), channel_id=1, source_target_pairs={{0,8},{1,4},{2,10},{3,6},{4,12},{5,0},{6,14},{7,2},{8,13},{9,1},{1... | collective-permute-start | bytes 786440 | tf_op jit(solution)/shard_map/ppermute | solution.py:163
  6.5 3.8 %collective-permute-done.1.refs_3_ = bf16[256,512]{1,0:T(8,128)(2,1)S(1)} collective-permute-done((bf16[256,512]{1,0:T(8,128)(2,1)}, bf16[256,512]{1,0:T(8,128)(2,1)S(1)}, u32[]{:S(2)}, u32[]{:S(2)}) %collective-permute-start.1) | collective-permute-done | bytes 262176 | tf_op jit(solution)/shard_map/ppermute | solution.py:163
  10.3 0.0 collective-permute-done.2.refs_2_.refs_1_
  10.3 2.0 %collective-permute-start.3 = (bf16[256,512]{1,0:T(8,128)(2,1)S(1)}, bf16[256,512]{1,0:T(8,128)(2,1)S(1)}, u32[]{:S(2)}, u32[]{:S(2)}) collective-permute-start(bf16[256,512]{1,0:T(8,128)(2,1)S(1)} %collective-permute-done.1.refs_3_), channel_id=1, source_target_pairs={{0,8},{1,4},{2,10},{3,6},{4,12},{5,0},{6,14},{7,2},{8,13},{9,1},{1... | collective-permute-start | bytes 786440 | tf_op jit(solution)/shard_map/ppermute | solution.py:163
  12.4 0.0 collective-permute-start.4
  12.4 0.0 collective-permute-done.refs_1_.refs_0_
  12.4 2.0 %collective-permute-start.7 = (bf16[256,512]{1,0:T(8,128)(2,1)S(1)}, bf16[256,512]{1,0:T(8,128)(2,1)S(1)}, u32[]{:S(2)}, u32[]{:S(2)}) collective-permute-start(bf16[256,512]{1,0:T(8,128)(2,1)S(1)} %collective-permute-done.refs_1_.refs_0_), channel_id=1, source_target_pairs={{0,8},{1,4},{2,10},{3,6},{4,12},{5,0},{6,14},{7,2},{8,13},{9,1},{1... | collective-permute-start | bytes 786440 | tf_op jit(solution)/shard_map/ppermute | solution.py:163
  14.4 4.2 %collective-permute-done.3.refs_4_.refs_3_ = bf16[256,512]{1,0:T(8,128)(2,1)S(1)} collective-permute-done((bf16[256,512]{1,0:T(8,128)(2,1)S(1)}, bf16[256,512]{1,0:T(8,128)(2,1)S(1)}, u32[]{:S(2)}, u32[]{:S(2)}) %collective-permute-start.3) | collective-permute-done | bytes 262176 | tf_op jit(solution)/shard_map/ppermute | solution.py:163
  18.6 2.5 %collective-permute-start.6 = (bf16[256,512]{1,0:T(8,128)(2,1)S(1)}, bf16[256,512]{1,0:T(8,128)(2,1)S(1)}, u32[]{:S(2)}, u32[]{:S(2)}) collective-permute-start(bf16[256,512]{1,0:T(8,128)(2,1)S(1)} %collective-permute-done.3.refs_4_.refs_3_), channel_id=1, source_target_pairs={{0,8},{1,4},{2,10},{3,6},{4,12},{5,0},{6,14},{7,2},{8,13},{9,1},{1... | collective-permute-start | bytes 786440 | tf_op jit(solution)/shard_map/ppermute | solution.py:163
  21.1 0.9 %multiply.7 = (f32[2,256,256]{2,1,0:T(8,128)S(1)}, f32[2,256,256]{2,1,0:T(8,128)S(1)}) custom-call(s32[4,4]{1,0:T(4,128)S(1)} %copy-done, bf16[256,512]{1,0:T(8,128)(2,1)S(1)} %copy-done.1, bf16[256,512]{1,0:T(8,128)(2,1)S(1)} %collective-permute-done.refs_1_.refs_0_, bf16[256,512]{1,0:T(8,128)(2,1)S(1)} %collective-permute-done.2.refs_2_.refs_1_, ...), custom_call_target="tpu_custom_call" | custom-call | flops 2013265920 | bytes 1048576 | tf_op jit(solution)/shard_map/multiply/pallas_call | solution.py:96
  22.0 0.5 %collective-permute-start.9 = (f32[2,256,256]{2,1,0:T(8,128)S(1)}, f32[2,256,256]{2,1,0:T(8,128)S(1)}, u32[]{:S(2)}, u32[]{:S(2)}) collective-permute-start(f32[2,256,256]{2,1,0:T(8,128)S(1)} %get-tuple-element.21), channel_id=1, source_target_pairs={{0,1},{1,0},{2,3},{3,2},{4,5},{5,4},{6,7},{7,6},{8,9},{9,8},{10,11... | collective-permute-start | bytes 1572872 | tf_op jit(solution)/shard_map/ppermute | solution.py:163
  22.5 0.5 %multiply.8 = (f32[1,256,256]{2,1,0:T(8,128)S(1)}, f32[1,256,256]{2,1,0:T(8,128)S(1)}, f32[256,512]{1,0:T(8,128)S(1)}) custom-call(s32[4,4]{1,0:T(4,128)S(1)} %copy-done, bf16[256,512]{1,0:T(8,128)(2,1)S(1)} %collective-permute-done.refs_1_.refs_0_, bf16[256,512]{1,0:T(8,128)(2,1)S(1)} %collective-permute-done.2.refs_2_.refs_1_, ...), custom_call_target="tpu_custom_call" | custom-call | flops 2013265920 | bytes 1048576 | tf_op jit(solution)/shard_map/multiply/pallas_call | solution.py:96
  23.1 0.4 %collective-permute-start.10 = (f32[1,256,256]{2,1,0:T(8,128)S(1)}, f32[1,256,256]{2,1,0:T(8,128)S(1)}, u32[]{:S(2)}, u32[]{:S(2)}) collective-permute-start(f32[1,256,256]{2,1,0:T(8,128)S(1)} %get-tuple-element.22), channel_id=1, source_target_pairs={{0,1},{1,0},{2,3},{3,2},{4,5},{5,4},{6,7},{7,6},{8,9},{9,8},{10,11... | collective-permute-start | bytes 786440 | tf_op jit(solution)/shard_map/ppermute | solution.py:163
  23.5 1.5 %collective-permute-done.6.refs_0_ = bf16[256,512]{1,0:T(8,128)(2,1)S(1)} collective-permute-done((bf16[256,512]{1,0:T(8,128)(2,1)S(1)}, bf16[256,512]{1,0:T(8,128)(2,1)S(1)}, u32[]{:S(2)}, u32[]{:S(2)}) %collective-permute-start.6) | collective-permute-done | bytes 262176 | tf_op jit(solution)/shard_map/ppermute | solution.py:163
  25.0 0.5 %multiply.9 = (f32[1,256,256]{2,1,0:T(8,128)S(1)}, f32[1,256,256]{2,1,0:T(8,128)S(1)}) custom-call(s32[4,4]{1,0:T(4,128)S(1)} %copy-done, bf16[256,512]{1,0:T(8,128)(2,1)S(1)} %collective-permute-done.6.refs_0_, bf16[512,512]{1,0:T(8,128)(2,1)S(1)} %get-tuple-element.24.refs_6_.refs_5_.refs_1_, ...), custom_call_target="tpu_custom_call" | custom-call | flops 134217728 | bytes 1048576 | tf_op jit(solution)/shard_map/multiply/pallas_call | solution.py:96
  25.5 0.1 collective-permute-start.8
  25.6 0.9 %add.11.refs_2_ = f32[256,1024]{1,0:T(8,128)} custom-call(f32[2,256,256]{2,1,0:T(8,128)S(1)} %get-tuple-element.16.refs_0_, f32[1,256,256]{2,1,0:T(8,128)S(1)} %get-tuple-element.19.refs_1_, f32[1,256,256]{2,1,0:T(8,128)S(1)} %get-tuple-element.20.refs_2_, f32[2,256,256]{2,1,0:T(8,128)S(1)} %collective-permute-done.9.refs_3_, ...), custom_call_target="tpu_custom_call" | custom-call | tf_op jit(solution)/shard_map/add/pallas_call | solution.py:137
  26.5 0.6 %collective-permute-done.8.refs_1_ = f32[1,256,256]{2,1,0:T(8,128)S(1)} collective-permute-done((f32[1,256,256]{2,1,0:T(8,128)S(1)}, f32[1,256,256]{2,1,0:T(8,128)S(1)}, u32[]{:S(2)}, u32[]{:S(2)}) %collective-permute-start.8) | collective-permute-done | bytes 262176 | tf_op jit(solution)/shard_map/ppermute | solution.py:163
  27.1 0.7 %add.12 = f32[256,1024]{1,0:T(8,128)} custom-call(f32[2,256,256]{2,1,0:T(8,128)S(1)} %get-tuple-element.16.refs_0_, f32[1,256,256]{2,1,0:T(8,128)S(1)} %collective-permute-done.8.refs_1_, f32[256,1024]{1,0:T(8,128)} %add.11.refs_2_), custom_call_target="tpu_custom_call", output_to_operand_aliasing={{}: (2, {})} | custom-call | tf_op jit(solution)/shard_map/add/pallas_call | solution.py:137
  (8 shorter events, 0.0 us)
Async XLA Ops:
  0.0 10.3 %collective-permute-start.1 = (bf16[256,512]{1,0:T(8,128)(2,1)}, bf16[256,512]{1,0:T(8,128)(2,1)S(1)}, u32[]{:S(2)}, u32[]{:S(2)}) collective-permute-start(bf16[256,512]{1,0:T(8,128)(2,1)} %refs_0_.1), channel_id=1, source_target_pairs={{0,2},{1,3},{2,0},{3,1},{4,6},{5,7},{6,4},{7,5},{8,10},{9,11},{10,... | collective-permute-start | bytes 786440 | tf_op jit(solution)/shard_map/ppermute | solution.py:163
  2.9 7.4 %collective-permute-start.2 = (bf16[256,512]{1,0:T(8,128)(2,1)}, bf16[256,512]{1,0:T(8,128)(2,1)S(1)}, u32[]{:S(2)}, u32[]{:S(2)}) collective-permute-start(bf16[256,512]{1,0:T(8,128)(2,1)} %refs_0_.1), channel_id=1, source_target_pairs={{0,5},{1,9},{2,7},{3,11},{4,1},{5,13},{6,3},{7,15},{8,0},{9,12},{1... | collective-permute-start | bytes 786440 | tf_op jit(solution)/shard_map/ppermute | solution.py:163
  3.6 1.9 %copy-start.1 = (bf16[256,512]{1,0:T(8,128)(2,1)S(1)}, bf16[256,512]{1,0:T(8,128)(2,1)}, u32[]{:S(2)}) copy-start(bf16[256,512]{1,0:T(8,128)(2,1)} %refs_0_.1) | copy-start | bytes 786436
  4.9 16.2 %copy-start = (s32[4,4]{1,0:T(4,128)S(1)}, s32[4,4]{1,0:T(4,128)}, u32[]{:S(2)}) copy-start(s32[4,4]{1,0:T(4,128)} %pairs.5) | copy-start | bytes 196
  4.9 16.2 %collective-permute-start.5 = (bf16[512,512]{1,0:T(8,128)(2,1)S(1)}, bf16[512,512]{1,0:T(8,128)(2,1)S(1)}, u32[]{:S(2)}, u32[]{:S(2)}) collective-permute-start(bf16[512,512]{1,0:T(8,128)(2,1)S(1)} %get-tuple-element.23), channel_id=1, source_target_pairs={{0,2},{1,3},{2,0},{3,1},{4,6},{5,7},{6,4},{7,5},{8,10},{9,11},{10,... | collective-permute-start | bytes 1572872 | tf_op jit(solution)/shard_map/ppermute | solution.py:163
  5.5 6.8 %collective-permute-start = (bf16[256,512]{1,0:T(8,128)(2,1)S(1)}, bf16[256,512]{1,0:T(8,128)(2,1)S(1)}, u32[]{:S(2)}, u32[]{:S(2)}) collective-permute-start(bf16[256,512]{1,0:T(8,128)(2,1)S(1)} %copy-done.1), channel_id=1, source_target_pairs={{0,8},{1,4},{2,10},{3,6},{4,12},{5,0},{6,14},{7,2},{8,13},{9,1},{1... | collective-permute-start | bytes 786440 | tf_op jit(solution)/shard_map/ppermute | solution.py:163
  10.3 8.3 %collective-permute-start.3 = (bf16[256,512]{1,0:T(8,128)(2,1)S(1)}, bf16[256,512]{1,0:T(8,128)(2,1)S(1)}, u32[]{:S(2)}, u32[]{:S(2)}) collective-permute-start(bf16[256,512]{1,0:T(8,128)(2,1)S(1)} %collective-permute-done.1.refs_3_), channel_id=1, source_target_pairs={{0,8},{1,4},{2,10},{3,6},{4,12},{5,0},{6,14},{7,2},{8,13},{9,1},{1... | collective-permute-start | bytes 786440 | tf_op jit(solution)/shard_map/ppermute | solution.py:163
  12.4 8.7 %collective-permute-start.4 = (bf16[256,512]{1,0:T(8,128)(2,1)S(1)}, bf16[256,512]{1,0:T(8,128)(2,1)S(1)}, u32[]{:S(2)}, u32[]{:S(2)}) collective-permute-start(bf16[256,512]{1,0:T(8,128)(2,1)S(1)} %collective-permute-done.1.refs_3_), channel_id=1, source_target_pairs={{0,5},{1,9},{2,7},{3,11},{4,1},{5,13},{6,3},{7,15},{8,0},{9,12},{1... | collective-permute-start | bytes 786440 | tf_op jit(solution)/shard_map/ppermute | solution.py:163
  12.4 10.1 %collective-permute-start.7 = (bf16[256,512]{1,0:T(8,128)(2,1)S(1)}, bf16[256,512]{1,0:T(8,128)(2,1)S(1)}, u32[]{:S(2)}, u32[]{:S(2)}) collective-permute-start(bf16[256,512]{1,0:T(8,128)(2,1)S(1)} %collective-permute-done.refs_1_.refs_0_), channel_id=1, source_target_pairs={{0,8},{1,4},{2,10},{3,6},{4,12},{5,0},{6,14},{7,2},{8,13},{9,1},{1... | collective-permute-start | bytes 786440 | tf_op jit(solution)/shard_map/ppermute | solution.py:163
  18.6 6.4 %collective-permute-start.6 = (bf16[256,512]{1,0:T(8,128)(2,1)S(1)}, bf16[256,512]{1,0:T(8,128)(2,1)S(1)}, u32[]{:S(2)}, u32[]{:S(2)}) collective-permute-start(bf16[256,512]{1,0:T(8,128)(2,1)S(1)} %collective-permute-done.3.refs_4_.refs_3_), channel_id=1, source_target_pairs={{0,8},{1,4},{2,10},{3,6},{4,12},{5,0},{6,14},{7,2},{8,13},{9,1},{1... | collective-permute-start | bytes 786440 | tf_op jit(solution)/shard_map/ppermute | solution.py:163
  22.0 3.6 %collective-permute-start.9 = (f32[2,256,256]{2,1,0:T(8,128)S(1)}, f32[2,256,256]{2,1,0:T(8,128)S(1)}, u32[]{:S(2)}, u32[]{:S(2)}) collective-permute-start(f32[2,256,256]{2,1,0:T(8,128)S(1)} %get-tuple-element.21), channel_id=1, source_target_pairs={{0,1},{1,0},{2,3},{3,2},{4,5},{5,4},{6,7},{7,6},{8,9},{9,8},{10,11... | collective-permute-start | bytes 1572872 | tf_op jit(solution)/shard_map/ppermute | solution.py:163
  23.1 2.5 %collective-permute-start.10 = (f32[1,256,256]{2,1,0:T(8,128)S(1)}, f32[1,256,256]{2,1,0:T(8,128)S(1)}, u32[]{:S(2)}, u32[]{:S(2)}) collective-permute-start(f32[1,256,256]{2,1,0:T(8,128)S(1)} %get-tuple-element.22), channel_id=1, source_target_pairs={{0,1},{1,0},{2,3},{3,2},{4,5},{5,4},{6,7},{7,6},{8,9},{9,8},{10,11... | collective-permute-start | bytes 786440 | tf_op jit(solution)/shard_map/ppermute | solution.py:163
  25.5 1.6 %collective-permute-start.8 = (f32[1,256,256]{2,1,0:T(8,128)S(1)}, f32[1,256,256]{2,1,0:T(8,128)S(1)}, u32[]{:S(2)}, u32[]{:S(2)}) collective-permute-start(f32[1,256,256]{2,1,0:T(8,128)S(1)} %get-tuple-element.18), channel_id=1, source_target_pairs={{0,1},{1,0},{2,3},{3,2},{4,5},{5,4},{6,7},{7,6},{8,9},{9,8},{10,11... | collective-permute-start | bytes 786440 | tf_op jit(solution)/shard_map/ppermute | solution.py:163

commit v8 on v7

--- a/solution.py
+++ b/solution.py
@@ -186,10 +186,10 @@
     cost = 2 * 2 * amps.shape[0] * amps.shape[1] * width
     run = functools.partial(multiply, block_list, pieces=pieces)
     groups = [[amps, near1, near2, None], [far0, far1, far2, None]]
-    keep, send = run(groups=groups, parts=(0, 2), cost=15 * cost)
+    keep, send = run(groups=groups, parts=(0, 2), cost=2 * cost)
     received = beside(send)
     groups = [[None, near1, near2, near3], [None, far1, far2, None]]
-    keep1, send1, begun = run(groups=groups, parts=(1,), cost=15 * cost, opening=(3,))
+    keep1, send1, begun = run(groups=groups, parts=(1,), cost=cost, opening=(3,))
     received1 = beside(send1)
     groups = [[None, None, None, far3]]
     keep3, send3 = run(groups=groups, parts=(3,), cost=cost, begun=begun)

time: 27.9 us -> 27.9 us (level)
  waiting for transfers between devices: 10.2 us -> 10.5 us
  starting transfers between devices: 12.7 us -> 12.4 us
    ppermute x11, waiting for transfers between devices: 10.2 us -> 10.5 us  [moved(): return lax.ppermute(block, GRID, route)]
    ppermute x11, starting transfers between devices: 12.7 us -> 12.4 us  [moved(): return lax.ppermute(block, GRID, route)]
where the time goes in v8:
time: 27.9 us; the launch traced here: 27.8 us
  starting transfers between devices  12.4 us (44%)
  waiting for transfers between devices  10.5 us (38%)
  Pallas kernels  3.53 us (13%)
  local copies, waits for them, and re-layouts  1.32 us (5%)
    ppermute x11, starting transfers between devices, moved(): return lax.ppermute(block, GRID, route)  12.4 us
    ppermute x11, waiting for transfers between devices, moved(): return lax.ppermute(block, GRID, route)  10.5 us
    pallas_call x3, Pallas kernels, multiply(): pl.pallas_call(functools.partial(multiply_kernel, groups=used, parts=part...  1.87 us
    pallas_call x2, Pallas kernels, add(): pl.pallas_call(functools.partial(add_kernel, terms=terms), out_shape=jax....  1.67 us
    dynamic_slice x1, local copies, waits for them, and re-layouts, chip_columns(): return lax.dynamic_slice_in_dim(ints, chip * 2 * width, 2 * width, 1)  1.31 us
  transfers between devices with their start and end apart: 11, of which 4 were waited for; matrix products, arithmetic and copies ran while one was open for 5% of the time, Pallas kernels for 10%

profile of v8, /device:TPU:0, one launch (start us, length us, event | category | flops | bytes accessed | tf_op | source)
XLA Modules:
  0.0 27.8 jit_solution(1828618631680753009)
XLA Ops:
  0.0 2.9 %collective-permute-start.1 = (bf16[256,512]{1,0:T(8,128)(2,1)}, bf16[256,512]{1,0:T(8,128)(2,1)S(1)}, u32[]{:S(2)}, u32[]{:S(2)}) collective-permute-start(bf16[256,512]{1,0:T(8,128)(2,1)} %refs_0_.1), channel_id=1, source_target_pairs={{0,2},{1,3},{2,0},{3,1},{4,6},{5,7},{6,4},{7,5},{8,10},{9,11},{10,... | collective-permute-start | bytes 786440 | tf_op jit(solution)/shard_map/ppermute | solution.py:163
  2.9 0.7 %collective-permute-start.2 = (bf16[256,512]{1,0:T(8,128)(2,1)}, bf16[256,512]{1,0:T(8,128)(2,1)S(1)}, u32[]{:S(2)}, u32[]{:S(2)}) collective-permute-start(bf16[256,512]{1,0:T(8,128)(2,1)} %refs_0_.1), channel_id=1, source_target_pairs={{0,5},{1,9},{2,7},{3,11},{4,1},{5,13},{6,3},{7,15},{8,0},{9,12},{1... | collective-permute-start | bytes 786440 | tf_op jit(solution)/shard_map/ppermute | solution.py:163
  3.6 1.3 %constant_dynamic-slice_fusion = (bf16[512,512]{1,0:T(8,128)(2,1)S(1)}, bf16[512,512]{1,0:T(8,128)(2,1)S(1)}) fusion(bf16[512,1024]{1,0:T(8,128)(2,1)} %param.4, s32[]{:T(128)S(6)} %select_n.13, s32[]{:T(128)S(6)} %select_n.12), kind=kLoop, calls=%fused_computation | loop fusion | bytes 2097160 | tf_op jit(solution)/shard_map/dynamic_slice | solution.py:174
  4.9 0.0 copy-start.1
  4.9 0.6 %collective-permute-start.5 = (bf16[512,512]{1,0:T(8,128)(2,1)S(1)}, bf16[512,512]{1,0:T(8,128)(2,1)S(1)}, u32[]{:S(2)}, u32[]{:S(2)}) collective-permute-start(bf16[512,512]{1,0:T(8,128)(2,1)S(1)} %get-tuple-element.23), channel_id=1, source_target_pairs={{0,2},{1,3},{2,0},{3,1},{4,6},{5,7},{6,4},{7,5},{8,10},{9,11},{10,... | collective-permute-start | bytes 1572872 | tf_op jit(solution)/shard_map/ppermute | solution.py:163
  5.5 0.9 %collective-permute-start = (bf16[256,512]{1,0:T(8,128)(2,1)S(1)}, bf16[256,512]{1,0:T(8,128)(2,1)S(1)}, u32[]{:S(2)}, u32[]{:S(2)}) collective-permute-start(bf16[256,512]{1,0:T(8,128)(2,1)S(1)} %copy-done), channel_id=1, source_target_pairs={{0,8},{1,4},{2,10},{3,6},{4,12},{5,0},{6,14},{7,2},{8,13},{9,1},{1... | collective-permute-start | bytes 786440 | tf_op jit(solution)/shard_map/ppermute | solution.py:163
  6.5 3.8 %collective-permute-done.1.refs_3_ = bf16[256,512]{1,0:T(8,128)(2,1)S(1)} collective-permute-done((bf16[256,512]{1,0:T(8,128)(2,1)}, bf16[256,512]{1,0:T(8,128)(2,1)S(1)}, u32[]{:S(2)}, u32[]{:S(2)}) %collective-permute-start.1) | collective-permute-done | bytes 262176 | tf_op jit(solution)/shard_map/ppermute | solution.py:163
  10.3 0.0 collective-permute-done.2.refs_2_.refs_1_
  10.3 2.0 %collective-permute-start.3 = (bf16[256,512]{1,0:T(8,128)(2,1)S(1)}, bf16[256,512]{1,0:T(8,128)(2,1)S(1)}, u32[]{:S(2)}, u32[]{:S(2)}) collective-permute-start(bf16[256,512]{1,0:T(8,128)(2,1)S(1)} %collective-permute-done.1.refs_3_), channel_id=1, source_target_pairs={{0,8},{1,4},{2,10},{3,6},{4,12},{5,0},{6,14},{7,2},{8,13},{9,1},{1... | collective-permute-start | bytes 786440 | tf_op jit(solution)/shard_map/ppermute | solution.py:163
  12.4 0.0 collective-permute-start.4
  12.4 2.0 %collective-permute-start.7 = (bf16[256,512]{1,0:T(8,128)(2,1)S(1)}, bf16[256,512]{1,0:T(8,128)(2,1)S(1)}, u32[]{:S(2)}, u32[]{:S(2)}) collective-permute-start(bf16[256,512]{1,0:T(8,128)(2,1)S(1)} %collective-permute-done.refs_1_.refs_0_), channel_id=1, source_target_pairs={{0,8},{1,4},{2,10},{3,6},{4,12},{5,0},{6,14},{7,2},{8,13},{9,1},{1... | collective-permute-start | bytes 786440 | tf_op jit(solution)/shard_map/ppermute | solution.py:163
  14.4 4.2 %collective-permute-done.3.refs_4_.refs_3_ = bf16[256,512]{1,0:T(8,128)(2,1)S(1)} collective-permute-done((bf16[256,512]{1,0:T(8,128)(2,1)S(1)}, bf16[256,512]{1,0:T(8,128)(2,1)S(1)}, u32[]{:S(2)}, u32[]{:S(2)}) %collective-permute-start.3) | collective-permute-done | bytes 262176 | tf_op jit(solution)/shard_map/ppermute | solution.py:163
  18.6 2.5 %collective-permute-start.6 = (bf16[256,512]{1,0:T(8,128)(2,1)S(1)}, bf16[256,512]{1,0:T(8,128)(2,1)S(1)}, u32[]{:S(2)}, u32[]{:S(2)}) collective-permute-start(bf16[256,512]{1,0:T(8,128)(2,1)S(1)} %collective-permute-done.3.refs_4_.refs_3_), channel_id=1, source_target_pairs={{0,8},{1,4},{2,10},{3,6},{4,12},{5,0},{6,14},{7,2},{8,13},{9,1},{1... | collective-permute-start | bytes 786440 | tf_op jit(solution)/shard_map/ppermute | solution.py:163
  21.1 0.3 %multiply.7 = (f32[2,256,256]{2,1,0:T(8,128)S(1)}, f32[2,256,256]{2,1,0:T(8,128)S(1)}) custom-call(s32[4,4]{1,0:T(4,128)S(1)} %copy-done.1, bf16[256,512]{1,0:T(8,128)(2,1)S(1)} %copy-done, bf16[256,512]{1,0:T(8,128)(2,1)S(1)} %collective-permute-done.refs_1_.refs_0_, bf16[256,512]{1,0:T(8,128)(2,1)S(1)} %collective-permute-done.2.refs_2_.refs_1_, ...), custom_call_target="tpu_custom_call" | custom-call | flops 268435456 | bytes 1048576 | tf_op jit(solution)/shard_map/multiply/pallas_call | solution.py:96
  21.4 0.5 %collective-permute-start.9 = (f32[2,256,256]{2,1,0:T(8,128)S(1)}, f32[2,256,256]{2,1,0:T(8,128)S(1)}, u32[]{:S(2)}, u32[]{:S(2)}) collective-permute-start(f32[2,256,256]{2,1,0:T(8,128)S(1)} %get-tuple-element.21), channel_id=1, source_target_pairs={{0,1},{1,0},{2,3},{3,2},{4,5},{5,4},{6,7},{7,6},{8,9},{9,8},{10,11... | collective-permute-start | bytes 1572872 | tf_op jit(solution)/shard_map/ppermute | solution.py:163
  21.9 0.0 collective-permute-done.7.refs_2_
  21.9 1.1 %multiply.8 = (f32[1,256,256]{2,1,0:T(8,128)S(1)}, f32[1,256,256]{2,1,0:T(8,128)S(1)}, f32[256,512]{1,0:T(8,128)S(1)}) custom-call(s32[4,4]{1,0:T(4,128)S(1)} %copy-done.1, bf16[256,512]{1,0:T(8,128)(2,1)S(1)} %collective-permute-done.refs_1_.refs_0_, bf16[256,512]{1,0:T(8,128)(2,1)S(1)} %collective-permute-done.2.refs_2_.refs_1_, ...), custom_call_target="tpu_custom_call" | custom-call | flops 134217728 | bytes 1048576 | tf_op jit(solution)/shard_map/multiply/pallas_call | solution.py:96
  23.1 0.1 collective-permute-start.10
  23.2 1.8 %collective-permute-done.6.refs_0_ = bf16[256,512]{1,0:T(8,128)(2,1)S(1)} collective-permute-done((bf16[256,512]{1,0:T(8,128)(2,1)S(1)}, bf16[256,512]{1,0:T(8,128)(2,1)S(1)}, u32[]{:S(2)}, u32[]{:S(2)}) %collective-permute-start.6) | collective-permute-done | bytes 262176 | tf_op jit(solution)/shard_map/ppermute | solution.py:163
  25.0 0.5 %multiply.9 = (f32[1,256,256]{2,1,0:T(8,128)S(1)}, f32[1,256,256]{2,1,0:T(8,128)S(1)}) custom-call(s32[4,4]{1,0:T(4,128)S(1)} %copy-done.1, bf16[256,512]{1,0:T(8,128)(2,1)S(1)} %collective-permute-done.6.refs_0_, bf16[512,512]{1,0:T(8,128)(2,1)S(1)} %get-tuple-element.24.refs_6_.refs_5_.refs_1_, ...), custom_call_target="tpu_custom_call" | custom-call | flops 134217728 | bytes 1048576 | tf_op jit(solution)/shard_map/multiply/pallas_call | solution.py:96
  25.5 0.1 collective-permute-start.8
  25.6 0.9 %add.11.refs_2_ = f32[256,1024]{1,0:T(8,128)} custom-call(f32[2,256,256]{2,1,0:T(8,128)S(1)} %get-tuple-element.16.refs_0_, f32[1,256,256]{2,1,0:T(8,128)S(1)} %get-tuple-element.19.refs_1_, f32[1,256,256]{2,1,0:T(8,128)S(1)} %get-tuple-element.20.refs_2_, f32[2,256,256]{2,1,0:T(8,128)S(1)} %collective-permute-done.9.refs_3_, ...), custom_call_target="tpu_custom_call" | custom-call | tf_op jit(solution)/shard_map/add/pallas_call | solution.py:137
  26.5 0.6 %collective-permute-done.8.refs_1_ = f32[1,256,256]{2,1,0:T(8,128)S(1)} collective-permute-done((f32[1,256,256]{2,1,0:T(8,128)S(1)}, f32[1,256,256]{2,1,0:T(8,128)S(1)}, u32[]{:S(2)}, u32[]{:S(2)}) %collective-permute-start.8) | collective-permute-done | bytes 262176 | tf_op jit(solution)/shard_map/ppermute | solution.py:163
  27.1 0.7 %add.12 = f32[256,1024]{1,0:T(8,128)} custom-call(f32[2,256,256]{2,1,0:T(8,128)S(1)} %get-tuple-element.16.refs_0_, f32[1,256,256]{2,1,0:T(8,128)S(1)} %collective-permute-done.8.refs_1_, f32[256,1024]{1,0:T(8,128)} %add.11.refs_2_), custom_call_target="tpu_custom_call", output_to_operand_aliasing={{}: (2, {})} | custom-call | tf_op jit(solution)/shard_map/add/pallas_call | solution.py:137
  (8 shorter events, 0.0 us)
Async XLA Ops:
  0.0 10.3 %collective-permute-start.1 = (bf16[256,512]{1,0:T(8,128)(2,1)}, bf16[256,512]{1,0:T(8,128)(2,1)S(1)}, u32[]{:S(2)}, u32[]{:S(2)}) collective-permute-start(bf16[256,512]{1,0:T(8,128)(2,1)} %refs_0_.1), channel_id=1, source_target_pairs={{0,2},{1,3},{2,0},{3,1},{4,6},{5,7},{6,4},{7,5},{8,10},{9,11},{10,... | collective-permute-start | bytes 786440 | tf_op jit(solution)/shard_map/ppermute | solution.py:163
  2.9 7.4 %collective-permute-start.2 = (bf16[256,512]{1,0:T(8,128)(2,1)}, bf16[256,512]{1,0:T(8,128)(2,1)S(1)}, u32[]{:S(2)}, u32[]{:S(2)}) collective-permute-start(bf16[256,512]{1,0:T(8,128)(2,1)} %refs_0_.1), channel_id=1, source_target_pairs={{0,5},{1,9},{2,7},{3,11},{4,1},{5,13},{6,3},{7,15},{8,0},{9,12},{1... | collective-permute-start | bytes 786440 | tf_op jit(solution)/shard_map/ppermute | solution.py:163
  3.6 1.9 %copy-start = (bf16[256,512]{1,0:T(8,128)(2,1)S(1)}, bf16[256,512]{1,0:T(8,128)(2,1)}, u32[]{:S(2)}) copy-start(bf16[256,512]{1,0:T(8,128)(2,1)} %refs_0_.1) | copy-start | bytes 786436
  4.9 16.2 %copy-start.1 = (s32[4,4]{1,0:T(4,128)S(1)}, s32[4,4]{1,0:T(4,128)}, u32[]{:S(2)}) copy-start(s32[4,4]{1,0:T(4,128)} %pairs.5) | copy-start | bytes 196
  4.9 16.2 %collective-permute-start.5 = (bf16[512,512]{1,0:T(8,128)(2,1)S(1)}, bf16[512,512]{1,0:T(8,128)(2,1)S(1)}, u32[]{:S(2)}, u32[]{:S(2)}) collective-permute-start(bf16[512,512]{1,0:T(8,128)(2,1)S(1)} %get-tuple-element.23), channel_id=1, source_target_pairs={{0,2},{1,3},{2,0},{3,1},{4,6},{5,7},{6,4},{7,5},{8,10},{9,11},{10,... | collective-permute-start | bytes 1572872 | tf_op jit(solution)/shard_map/ppermute | solution.py:163
  5.5 6.8 %collective-permute-start = (bf16[256,512]{1,0:T(8,128)(2,1)S(1)}, bf16[256,512]{1,0:T(8,128)(2,1)S(1)}, u32[]{:S(2)}, u32[]{:S(2)}) collective-permute-start(bf16[256,512]{1,0:T(8,128)(2,1)S(1)} %copy-done), channel_id=1, source_target_pairs={{0,8},{1,4},{2,10},{3,6},{4,12},{5,0},{6,14},{7,2},{8,13},{9,1},{1... | collective-permute-start | bytes 786440 | tf_op jit(solution)/shard_map/ppermute | solution.py:163
  10.3 8.3 %collective-permute-start.3 = (bf16[256,512]{1,0:T(8,128)(2,1)S(1)}, bf16[256,512]{1,0:T(8,128)(2,1)S(1)}, u32[]{:S(2)}, u32[]{:S(2)}) collective-permute-start(bf16[256,512]{1,0:T(8,128)(2,1)S(1)} %collective-permute-done.1.refs_3_), channel_id=1, source_target_pairs={{0,8},{1,4},{2,10},{3,6},{4,12},{5,0},{6,14},{7,2},{8,13},{9,1},{1... | collective-permute-start | bytes 786440 | tf_op jit(solution)/shard_map/ppermute | solution.py:163
  12.4 8.7 %collective-permute-start.4 = (bf16[256,512]{1,0:T(8,128)(2,1)S(1)}, bf16[256,512]{1,0:T(8,128)(2,1)S(1)}, u32[]{:S(2)}, u32[]{:S(2)}) collective-permute-start(bf16[256,512]{1,0:T(8,128)(2,1)S(1)} %collective-permute-done.1.refs_3_), channel_id=1, source_target_pairs={{0,5},{1,9},{2,7},{3,11},{4,1},{5,13},{6,3},{7,15},{8,0},{9,12},{1... | collective-permute-start | bytes 786440 | tf_op jit(solution)/shard_map/ppermute | solution.py:163
  12.4 9.6 %collective-permute-start.7 = (bf16[256,512]{1,0:T(8,128)(2,1)S(1)}, bf16[256,512]{1,0:T(8,128)(2,1)S(1)}, u32[]{:S(2)}, u32[]{:S(2)}) collective-permute-start(bf16[256,512]{1,0:T(8,128)(2,1)S(1)} %collective-permute-done.refs_1_.refs_0_), channel_id=1, source_target_pairs={{0,8},{1,4},{2,10},{3,6},{4,12},{5,0},{6,14},{7,2},{8,13},{9,1},{1... | collective-permute-start | bytes 786440 | tf_op jit(solution)/shard_map/ppermute | solution.py:163
  18.6 6.4 %collective-permute-start.6 = (bf16[256,512]{1,0:T(8,128)(2,1)S(1)}, bf16[256,512]{1,0:T(8,128)(2,1)S(1)}, u32[]{:S(2)}, u32[]{:S(2)}) collective-permute-start(bf16[256,512]{1,0:T(8,128)(2,1)S(1)} %collective-permute-done.3.refs_4_.refs_3_), channel_id=1, source_target_pairs={{0,8},{1,4},{2,10},{3,6},{4,12},{5,0},{6,14},{7,2},{8,13},{9,1},{1... | collective-permute-start | bytes 786440 | tf_op jit(solution)/shard_map/ppermute | solution.py:163
  21.4 4.1 %collective-permute-start.9 = (f32[2,256,256]{2,1,0:T(8,128)S(1)}, f32[2,256,256]{2,1,0:T(8,128)S(1)}, u32[]{:S(2)}, u32[]{:S(2)}) collective-permute-start(f32[2,256,256]{2,1,0:T(8,128)S(1)} %get-tuple-element.21), channel_id=1, source_target_pairs={{0,1},{1,0},{2,3},{3,2},{4,5},{5,4},{6,7},{7,6},{8,9},{9,8},{10,11... | collective-permute-start | bytes 1572872 | tf_op jit(solution)/shard_map/ppermute | solution.py:163
  23.1 2.5 %collective-permute-start.10 = (f32[1,256,256]{2,1,0:T(8,128)S(1)}, f32[1,256,256]{2,1,0:T(8,128)S(1)}, u32[]{:S(2)}, u32[]{:S(2)}) collective-permute-start(f32[1,256,256]{2,1,0:T(8,128)S(1)} %get-tuple-element.22), channel_id=1, source_target_pairs={{0,1},{1,0},{2,3},{3,2},{4,5},{5,4},{6,7},{7,6},{8,9},{9,8},{10,11... | collective-permute-start | bytes 786440 | tf_op jit(solution)/shard_map/ppermute | solution.py:163
  25.5 1.6 %collective-permute-start.8 = (f32[1,256,256]{2,1,0:T(8,128)S(1)}, f32[1,256,256]{2,1,0:T(8,128)S(1)}, u32[]{:S(2)}, u32[]{:S(2)}) collective-permute-start(f32[1,256,256]{2,1,0:T(8,128)S(1)} %get-tuple-element.18), channel_id=1, source_target_pairs={{0,1},{1,0},{2,3},{3,2},{4,5},{5,4},{6,7},{7,6},{8,9},{9,8},{10,11... | collective-permute-start | bytes 786440 | tf_op jit(solution)/shard_map/ppermute | solution.py:163

commit v9 on v8

--- a/solution.py
+++ b/solution.py
@@ -178,9 +178,9 @@
     near1 = first(amps)
     near2 = second(amps)
     pieces = [chip_columns(chip), across(chip_columns(1 - chip))]
-    far0, near2 = lax.optimization_barrier((far0, near2))
     near3 = first(near1)
     far1 = first(far0)
+    far0, near2 = lax.optimization_barrier((far0, near2))
     far2 = second(far0)
     far3 = first(far1)
     cost = 2 * 2 * amps.shape[0] * amps.shape[1] * width

time: 27.9 us -> 27.7 us (level)
  waiting for transfers between devices: 10.5 us -> 10 us
  starting transfers between devices: 12.4 us -> 12.7 us
    ppermute x11, waiting for transfers between devices: 10.5 us -> 10 us  [moved(): return lax.ppermute(block, GRID, route)]
    ppermute x11, starting transfers between devices: 12.4 us -> 12.7 us  [moved(): return lax.ppermute(block, GRID, route)]
where the time goes in v9:
time: 27.7 us
  starting transfers between devices  12.7 us (46%)
  waiting for transfers between devices  10 us (36%)
  Pallas kernels  3.55 us (13%)
  local copies, waits for them, and re-layouts  1.32 us (5%)
    ppermute x11, starting transfers between devices, moved(): return lax.ppermute(block, GRID, route)  12.7 us
    ppermute x11, waiting for transfers between devices, moved(): return lax.ppermute(block, GRID, route)  10 us
    pallas_call x3, Pallas kernels, multiply(): pl.pallas_call(functools.partial(multiply_kernel, groups=used, parts=part...  1.88 us
    pallas_call x2, Pallas kernels, add(): pl.pallas_call(functools.partial(add_kernel, terms=terms), out_shape=jax....  1.67 us
    dynamic_slice x1, local copies, waits for them, and re-layouts, chip_columns(): return lax.dynamic_slice_in_dim(ints, chip * 2 * width, 2 * width, 1)  1.31 us
  transfers between devices with their start and end apart: 11, of which 4 were waited for; matrix products, arithmetic and copies ran while one was open for 5% of the time, Pallas kernels for 10%

profile of v9, /device:TPU:0, one launch (start us, length us, event | category | flops | bytes accessed | tf_op | source)
XLA Modules:
  0.0 27.7 jit_solution(5090825393992014639)
XLA Ops:
  0.0 2.9 %collective-permute-start.1 = (bf16[256,512]{1,0:T(8,128)(2,1)}, bf16[256,512]{1,0:T(8,128)(2,1)S(1)}, u32[]{:S(2)}, u32[]{:S(2)}) collective-permute-start(bf16[256,512]{1,0:T(8,128)(2,1)} %refs_0_.1), channel_id=1, source_target_pairs={{0,2},{1,3},{2,0},{3,1},{4,6},{5,7},{6,4},{7,5},{8,10},{9,11},{10,... | collective-permute-start | bytes 786440 | tf_op jit(solution)/shard_map/ppermute | solution.py:163
  2.9 0.7 %collective-permute-start.2 = (bf16[256,512]{1,0:T(8,128)(2,1)}, bf16[256,512]{1,0:T(8,128)(2,1)S(1)}, u32[]{:S(2)}, u32[]{:S(2)}) collective-permute-start(bf16[256,512]{1,0:T(8,128)(2,1)} %refs_0_.1), channel_id=1, source_target_pairs={{0,5},{1,9},{2,7},{3,11},{4,1},{5,13},{6,3},{7,15},{8,0},{9,12},{1... | collective-permute-start | bytes 786440 | tf_op jit(solution)/shard_map/ppermute | solution.py:163
  3.6 1.3 %constant_dynamic-slice_fusion = (bf16[512,512]{1,0:T(8,128)(2,1)S(1)}, bf16[512,512]{1,0:T(8,128)(2,1)S(1)}) fusion(bf16[512,1024]{1,0:T(8,128)(2,1)} %param.4, s32[]{:T(128)S(6)} %select_n.13, s32[]{:T(128)S(6)} %select_n.12), kind=kLoop, calls=%fused_computation | loop fusion | bytes 2097160 | tf_op jit(solution)/shard_map/dynamic_slice | solution.py:174
  4.9 0.0 copy-start.1
  4.9 0.6 %collective-permute-start.5 = (bf16[512,512]{1,0:T(8,128)(2,1)S(1)}, bf16[512,512]{1,0:T(8,128)(2,1)S(1)}, u32[]{:S(2)}, u32[]{:S(2)}) collective-permute-start(bf16[512,512]{1,0:T(8,128)(2,1)S(1)} %get-tuple-element.23), channel_id=1, source_target_pairs={{0,2},{1,3},{2,0},{3,1},{4,6},{5,7},{6,4},{7,5},{8,10},{9,11},{10,... | collective-permute-start | bytes 1572872 | tf_op jit(solution)/shard_map/ppermute | solution.py:163
  5.5 0.9 %collective-permute-start = (bf16[256,512]{1,0:T(8,128)(2,1)S(1)}, bf16[256,512]{1,0:T(8,128)(2,1)S(1)}, u32[]{:S(2)}, u32[]{:S(2)}) collective-permute-start(bf16[256,512]{1,0:T(8,128)(2,1)S(1)} %copy-done), channel_id=1, source_target_pairs={{0,8},{1,4},{2,10},{3,6},{4,12},{5,0},{6,14},{7,2},{8,13},{9,1},{1... | collective-permute-start | bytes 786440 | tf_op jit(solution)/shard_map/ppermute | solution.py:163
  6.5 3.8 %collective-permute-done.1.refs_3_ = bf16[256,512]{1,0:T(8,128)(2,1)S(1)} collective-permute-done((bf16[256,512]{1,0:T(8,128)(2,1)}, bf16[256,512]{1,0:T(8,128)(2,1)S(1)}, u32[]{:S(2)}, u32[]{:S(2)}) %collective-permute-start.1) | collective-permute-done | bytes 262176 | tf_op jit(solution)/shard_map/ppermute | solution.py:163
  10.3 2.1 %collective-permute-start.3 = (bf16[256,512]{1,0:T(8,128)(2,1)S(1)}, bf16[256,512]{1,0:T(8,128)(2,1)S(1)}, u32[]{:S(2)}, u32[]{:S(2)}) collective-permute-start(bf16[256,512]{1,0:T(8,128)(2,1)S(1)} %collective-permute-done.1.refs_3_), channel_id=1, source_target_pairs={{0,8},{1,4},{2,10},{3,6},{4,12},{5,0},{6,14},{7,2},{8,13},{9,1},{1... | collective-permute-start | bytes 786440 | tf_op jit(solution)/shard_map/ppermute | solution.py:163
  12.4 0.0 collective-permute-start.4
  12.4 0.0 collective-permute-done.refs_1_.refs_0_
  12.4 2.0 %collective-permute-start.7 = (bf16[256,512]{1,0:T(8,128)(2,1)S(1)}, bf16[256,512]{1,0:T(8,128)(2,1)S(1)}, u32[]{:S(2)}, u32[]{:S(2)}) collective-permute-start(bf16[256,512]{1,0:T(8,128)(2,1)S(1)} %collective-permute-done.refs_1_.refs_0_), channel_id=1, source_target_pairs={{0,8},{1,4},{2,10},{3,6},{4,12},{5,0},{6,14},{7,2},{8,13},{9,1},{1... | collective-permute-start | bytes 786440 | tf_op jit(solution)/shard_map/ppermute | solution.py:163
  14.4 4.1 %collective-permute-done.3.refs_4_.refs_3_ = bf16[256,512]{1,0:T(8,128)(2,1)S(1)} collective-permute-done((bf16[256,512]{1,0:T(8,128)(2,1)S(1)}, bf16[256,512]{1,0:T(8,128)(2,1)S(1)}, u32[]{:S(2)}, u32[]{:S(2)}) %collective-permute-start.3) | collective-permute-done | bytes 262176 | tf_op jit(solution)/shard_map/ppermute | solution.py:163
  18.5 2.5 %collective-permute-start.6 = (bf16[256,512]{1,0:T(8,128)(2,1)S(1)}, bf16[256,512]{1,0:T(8,128)(2,1)S(1)}, u32[]{:S(2)}, u32[]{:S(2)}) collective-permute-start(bf16[256,512]{1,0:T(8,128)(2,1)S(1)} %collective-permute-done.3.refs_4_.refs_3_), channel_id=1, source_target_pairs={{0,8},{1,4},{2,10},{3,6},{4,12},{5,0},{6,14},{7,2},{8,13},{9,1},{1... | collective-permute-start | bytes 786440 | tf_op jit(solution)/shard_map/ppermute | solution.py:163
  21.0 0.9 %multiply.7 = (f32[2,256,256]{2,1,0:T(8,128)S(1)}, f32[2,256,256]{2,1,0:T(8,128)S(1)}) custom-call(s32[4,4]{1,0:T(4,128)S(1)} %copy-done.1, bf16[256,512]{1,0:T(8,128)(2,1)S(1)} %copy-done, bf16[256,512]{1,0:T(8,128)(2,1)S(1)} %collective-permute-done.refs_1_.refs_0_, bf16[256,512]{1,0:T(8,128)(2,1)S(1)} %collective-permute-done.2.refs_2_.refs_1_, ...), custom_call_target="tpu_custom_call" | custom-call | flops 268435456 | bytes 1048576 | tf_op jit(solution)/shard_map/multiply/pallas_call | solution.py:96
  21.9 0.5 %collective-permute-start.9 = (f32[2,256,256]{2,1,0:T(8,128)S(1)}, f32[2,256,256]{2,1,0:T(8,128)S(1)}, u32[]{:S(2)}, u32[]{:S(2)}) collective-permute-start(f32[2,256,256]{2,1,0:T(8,128)S(1)} %get-tuple-element.21), channel_id=1, source_target_pairs={{0,1},{1,0},{2,3},{3,2},{4,5},{5,4},{6,7},{7,6},{8,9},{9,8},{10,11... | collective-permute-start | bytes 1572872 | tf_op jit(solution)/shard_map/ppermute | solution.py:163
  22.4 0.5 %multiply.8 = (f32[1,256,256]{2,1,0:T(8,128)S(1)}, f32[1,256,256]{2,1,0:T(8,128)S(1)}, f32[256,512]{1,0:T(8,128)S(1)}) custom-call(s32[4,4]{1,0:T(4,128)S(1)} %copy-done.1, bf16[256,512]{1,0:T(8,128)(2,1)S(1)} %collective-permute-done.refs_1_.refs_0_, bf16[256,512]{1,0:T(8,128)(2,1)S(1)} %collective-permute-done.2.refs_2_.refs_1_, ...), custom_call_target="tpu_custom_call" | custom-call | flops 134217728 | bytes 1048576 | tf_op jit(solution)/shard_map/multiply/pallas_call | solution.py:96
  23.0 0.4 %collective-permute-start.10 = (f32[1,256,256]{2,1,0:T(8,128)S(1)}, f32[1,256,256]{2,1,0:T(8,128)S(1)}, u32[]{:S(2)}, u32[]{:S(2)}) collective-permute-start(f32[1,256,256]{2,1,0:T(8,128)S(1)} %get-tuple-element.22), channel_id=1, source_target_pairs={{0,1},{1,0},{2,3},{3,2},{4,5},{5,4},{6,7},{7,6},{8,9},{9,8},{10,11... | collective-permute-start | bytes 786440 | tf_op jit(solution)/shard_map/ppermute | solution.py:163
  23.4 1.5 %collective-permute-done.6.refs_0_ = bf16[256,512]{1,0:T(8,128)(2,1)S(1)} collective-permute-done((bf16[256,512]{1,0:T(8,128)(2,1)S(1)}, bf16[256,512]{1,0:T(8,128)(2,1)S(1)}, u32[]{:S(2)}, u32[]{:S(2)}) %collective-permute-start.6) | collective-permute-done | bytes 262176 | tf_op jit(solution)/shard_map/ppermute | solution.py:163
  24.9 0.5 %multiply.9 = (f32[1,256,256]{2,1,0:T(8,128)S(1)}, f32[1,256,256]{2,1,0:T(8,128)S(1)}) custom-call(s32[4,4]{1,0:T(4,128)S(1)} %copy-done.1, bf16[256,512]{1,0:T(8,128)(2,1)S(1)} %collective-permute-done.6.refs_0_, bf16[512,512]{1,0:T(8,128)(2,1)S(1)} %get-tuple-element.24.refs_6_.refs_5_.refs_1_, ...), custom_call_target="tpu_custom_call" | custom-call | flops 134217728 | bytes 1048576 | tf_op jit(solution)/shard_map/multiply/pallas_call | solution.py:96
  25.3 0.1 collective-permute-start.8
  25.4 0.0 collective-permute-done.9.refs_3_
  25.4 0.9 %add.11.refs_2_ = f32[256,1024]{1,0:T(8,128)} custom-call(f32[2,256,256]{2,1,0:T(8,128)S(1)} %get-tuple-element.16.refs_0_, f32[1,256,256]{2,1,0:T(8,128)S(1)} %get-tuple-element.19.refs_1_, f32[1,256,256]{2,1,0:T(8,128)S(1)} %get-tuple-element.20.refs_2_, f32[2,256,256]{2,1,0:T(8,128)S(1)} %collective-permute-done.9.refs_3_, ...), custom_call_target="tpu_custom_call" | custom-call | tf_op jit(solution)/shard_map/add/pallas_call | solution.py:137
  26.4 0.6 %collective-permute-done.8.refs_1_ = f32[1,256,256]{2,1,0:T(8,128)S(1)} collective-permute-done((f32[1,256,256]{2,1,0:T(8,128)S(1)}, f32[1,256,256]{2,1,0:T(8,128)S(1)}, u32[]{:S(2)}, u32[]{:S(2)}) %collective-permute-start.8) | collective-permute-done | bytes 262176 | tf_op jit(solution)/shard_map/ppermute | solution.py:163
  26.9 0.7 %add.12 = f32[256,1024]{1,0:T(8,128)} custom-call(f32[2,256,256]{2,1,0:T(8,128)S(1)} %get-tuple-element.16.refs_0_, f32[1,256,256]{2,1,0:T(8,128)S(1)} %collective-permute-done.8.refs_1_, f32[256,1024]{1,0:T(8,128)} %add.11.refs_2_), custom_call_target="tpu_custom_call", output_to_operand_aliasing={{}: (2, {})} | custom-call | tf_op jit(solution)/shard_map/add/pallas_call | solution.py:137
  (8 shorter events, 0.0 us)
Async XLA Ops:
  0.0 10.3 %collective-permute-start.1 = (bf16[256,512]{1,0:T(8,128)(2,1)}, bf16[256,512]{1,0:T(8,128)(2,1)S(1)}, u32[]{:S(2)}, u32[]{:S(2)}) collective-permute-start(bf16[256,512]{1,0:T(8,128)(2,1)} %refs_0_.1), channel_id=1, source_target_pairs={{0,2},{1,3},{2,0},{3,1},{4,6},{5,7},{6,4},{7,5},{8,10},{9,11},{10,... | collective-permute-start | bytes 786440 | tf_op jit(solution)/shard_map/ppermute | solution.py:163
  2.9 9.4 %collective-permute-start.2 = (bf16[256,512]{1,0:T(8,128)(2,1)}, bf16[256,512]{1,0:T(8,128)(2,1)S(1)}, u32[]{:S(2)}, u32[]{:S(2)}) collective-permute-start(bf16[256,512]{1,0:T(8,128)(2,1)} %refs_0_.1), channel_id=1, source_target_pairs={{0,5},{1,9},{2,7},{3,11},{4,1},{5,13},{6,3},{7,15},{8,0},{9,12},{1... | collective-permute-start | bytes 786440 | tf_op jit(solution)/shard_map/ppermute | solution.py:163
  3.6 1.9 %copy-start = (bf16[256,512]{1,0:T(8,128)(2,1)S(1)}, bf16[256,512]{1,0:T(8,128)(2,1)}, u32[]{:S(2)}) copy-start(bf16[256,512]{1,0:T(8,128)(2,1)} %refs_0_.1) | copy-start | bytes 786436
  4.9 16.1 %copy-start.1 = (s32[4,4]{1,0:T(4,128)S(1)}, s32[4,4]{1,0:T(4,128)}, u32[]{:S(2)}) copy-start(s32[4,4]{1,0:T(4,128)} %pairs.5) | copy-start | bytes 196
  4.9 16.0 %collective-permute-start.5 = (bf16[512,512]{1,0:T(8,128)(2,1)S(1)}, bf16[512,512]{1,0:T(8,128)(2,1)S(1)}, u32[]{:S(2)}, u32[]{:S(2)}) collective-permute-start(bf16[512,512]{1,0:T(8,128)(2,1)S(1)} %get-tuple-element.23), channel_id=1, source_target_pairs={{0,2},{1,3},{2,0},{3,1},{4,6},{5,7},{6,4},{7,5},{8,10},{9,11},{10,... | collective-permute-start | bytes 1572872 | tf_op jit(solution)/shard_map/ppermute | solution.py:163
  5.5 6.8 %collective-permute-start = (bf16[256,512]{1,0:T(8,128)(2,1)S(1)}, bf16[256,512]{1,0:T(8,128)(2,1)S(1)}, u32[]{:S(2)}, u32[]{:S(2)}) collective-permute-start(bf16[256,512]{1,0:T(8,128)(2,1)S(1)} %copy-done), channel_id=1, source_target_pairs={{0,8},{1,4},{2,10},{3,6},{4,12},{5,0},{6,14},{7,2},{8,13},{9,1},{1... | collective-permute-start | bytes 786440 | tf_op jit(solution)/shard_map/ppermute | solution.py:163
  10.3 8.2 %collective-permute-start.3 = (bf16[256,512]{1,0:T(8,128)(2,1)S(1)}, bf16[256,512]{1,0:T(8,128)(2,1)S(1)}, u32[]{:S(2)}, u32[]{:S(2)}) collective-permute-start(bf16[256,512]{1,0:T(8,128)(2,1)S(1)} %collective-permute-done.1.refs_3_), channel_id=1, source_target_pairs={{0,8},{1,4},{2,10},{3,6},{4,12},{5,0},{6,14},{7,2},{8,13},{9,1},{1... | collective-permute-start | bytes 786440 | tf_op jit(solution)/shard_map/ppermute | solution.py:163
  12.4 8.6 %collective-permute-start.4 = (bf16[256,512]{1,0:T(8,128)(2,1)S(1)}, bf16[256,512]{1,0:T(8,128)(2,1)S(1)}, u32[]{:S(2)}, u32[]{:S(2)}) collective-permute-start(bf16[256,512]{1,0:T(8,128)(2,1)S(1)} %collective-permute-done.1.refs_3_), channel_id=1, source_target_pairs={{0,5},{1,9},{2,7},{3,11},{4,1},{5,13},{6,3},{7,15},{8,0},{9,12},{1... | collective-permute-start | bytes 786440 | tf_op jit(solution)/shard_map/ppermute | solution.py:163
  12.4 10.0 %collective-permute-start.7 = (bf16[256,512]{1,0:T(8,128)(2,1)S(1)}, bf16[256,512]{1,0:T(8,128)(2,1)S(1)}, u32[]{:S(2)}, u32[]{:S(2)}) collective-permute-start(bf16[256,512]{1,0:T(8,128)(2,1)S(1)} %collective-permute-done.refs_1_.refs_0_), channel_id=1, source_target_pairs={{0,8},{1,4},{2,10},{3,6},{4,12},{5,0},{6,14},{7,2},{8,13},{9,1},{1... | collective-permute-start | bytes 786440 | tf_op jit(solution)/shard_map/ppermute | solution.py:163
  18.5 6.4 %collective-permute-start.6 = (bf16[256,512]{1,0:T(8,128)(2,1)S(1)}, bf16[256,512]{1,0:T(8,128)(2,1)S(1)}, u32[]{:S(2)}, u32[]{:S(2)}) collective-permute-start(bf16[256,512]{1,0:T(8,128)(2,1)S(1)} %collective-permute-done.3.refs_4_.refs_3_), channel_id=1, source_target_pairs={{0,8},{1,4},{2,10},{3,6},{4,12},{5,0},{6,14},{7,2},{8,13},{9,1},{1... | collective-permute-start | bytes 786440 | tf_op jit(solution)/shard_map/ppermute | solution.py:163
  21.9 3.6 %collective-permute-start.9 = (f32[2,256,256]{2,1,0:T(8,128)S(1)}, f32[2,256,256]{2,1,0:T(8,128)S(1)}, u32[]{:S(2)}, u32[]{:S(2)}) collective-permute-start(f32[2,256,256]{2,1,0:T(8,128)S(1)} %get-tuple-element.21), channel_id=1, source_target_pairs={{0,1},{1,0},{2,3},{3,2},{4,5},{5,4},{6,7},{7,6},{8,9},{9,8},{10,11... | collective-permute-start | bytes 1572872 | tf_op jit(solution)/shard_map/ppermute | solution.py:163
  23.0 2.5 %collective-permute-start.10 = (f32[1,256,256]{2,1,0:T(8,128)S(1)}, f32[1,256,256]{2,1,0:T(8,128)S(1)}, u32[]{:S(2)}, u32[]{:S(2)}) collective-permute-start(f32[1,256,256]{2,1,0:T(8,128)S(1)} %get-tuple-element.22), channel_id=1, source_target_pairs={{0,1},{1,0},{2,3},{3,2},{4,5},{5,4},{6,7},{7,6},{8,9},{9,8},{10,11... | collective-permute-start | bytes 786440 | tf_op jit(solution)/shard_map/ppermute | solution.py:163
  25.3 1.6 %collective-permute-start.8 = (f32[1,256,256]{2,1,0:T(8,128)S(1)}, f32[1,256,256]{2,1,0:T(8,128)S(1)}, u32[]{:S(2)}, u32[]{:S(2)}) collective-permute-start(f32[1,256,256]{2,1,0:T(8,128)S(1)} %get-tuple-element.18), channel_id=1, source_target_pairs={{0,1},{1,0},{2,3},{3,2},{4,5},{5,4},{6,7},{7,6},{8,9},{9,8},{10,11... | collective-permute-start | bytes 786440 | tf_op jit(solution)/shard_map/ppermute | solution.py:163

commit v10 on v9

--- a/solution.py
+++ b/solution.py
@@ -117,14 +117,19 @@
     col = lax.axis_index("col")
     width = held.shape[2]
     copies = []
+    step = held.shape[1] // 2
     for place, (part, kept, received) in enumerate(terms):
-        held[place] = refs[kept[0]][kept[1]] + refs[received[0]][received[1]]
         start = pl.multiple_of((col ^ part) * width, width)
-        copy = pltpu.make_async_copy(
-            held.at[place], out.at[:, pl.ds(start, width)], sems.at[place]
-        )
-        copy.start()
-        copies.append(copy)
+        for piece in range(2):
+            rows = pl.ds(piece * step, step)
+            held[place, rows] = (
+                refs[kept[0]][kept[1], rows] + refs[received[0]][received[1], rows]
+            )
+            copy = pltpu.make_async_copy(
+                held.at[place, rows], out.at[rows, pl.ds(start, width)], sems.at[place, piece]
+            )
+            copy.start()
+            copies.append(copy)
     for copy in copies:
         copy.wait()
 
@@ -141,7 +146,7 @@
         out_specs=anywhere,
         scratch_shapes=[
             pltpu.VMEM((len(terms), rows, width), jnp.float32),
-            pltpu.SemaphoreType.DMA((len(terms),)),
+            pltpu.SemaphoreType.DMA((len(terms), 2)),
         ],
         input_output_aliases={len(sums): 0} if aliased else {},
         compiler_params=pltpu.CompilerParams(vmem_limit_bytes=8 * 2**20),

time: 27.7 us -> 27.7 us (level); the launches traced: 27.7 us -> 27.4 us
  starting transfers between devices: 12.7 us -> 12.4 us
    ppermute x11, starting transfers between devices: 12.7 us -> 12.4 us  [moved(): return lax.ppermute(block, GRID, route)]
where the time goes in v10:
time: 27.7 us; the launch traced here: 27.4 us
  starting transfers between devices  12.4 us (45%)
  waiting for transfers between devices  10.1 us (36%)
  Pallas kernels  3.52 us (13%)
  local copies, waits for them, and re-layouts  1.32 us (5%)
    ppermute x11, starting transfers between devices, moved(): return lax.ppermute(block, GRID, route)  12.4 us
    ppermute x11, waiting for transfers between devices, moved(): return lax.ppermute(block, GRID, route)  10.1 us
    pallas_call x3, Pallas kernels, multiply(): pl.pallas_call(functools.partial(multiply_kernel, groups=used, parts=part...  1.86 us
    pallas_call x2, Pallas kernels, add(): pl.pallas_call(functools.partial(add_kernel, terms=terms), out_shape=jax....  1.67 us
    dynamic_slice x1, local copies, waits for them, and re-layouts, chip_columns(): return lax.dynamic_slice_in_dim(ints, chip * 2 * width, 2 * width, 1)  1.31 us
  transfers between devices with their start and end apart: 11, of which 4 were waited for; matrix products, arithmetic and copies ran while one was open for 5% of the time, Pallas kernels for 10%

profile of v10, /device:TPU:0, one launch (start us, length us, event | category | flops | bytes accessed | tf_op | source)
XLA Modules:
  0.0 27.4 jit_solution(16258879499882461133)
XLA Ops:
  0.0 2.9 %collective-permute-start.1 = (bf16[256,512]{1,0:T(8,128)(2,1)}, bf16[256,512]{1,0:T(8,128)(2,1)S(1)}, u32[]{:S(2)}, u32[]{:S(2)}) collective-permute-start(bf16[256,512]{1,0:T(8,128)(2,1)} %refs_0_.1), channel_id=1, source_target_pairs={{0,2},{1,3},{2,0},{3,1},{4,6},{5,7},{6,4},{7,5},{8,10},{9,11},{10,... | collective-permute-start | bytes 786440 | tf_op jit(solution)/shard_map/ppermute | solution.py:168
  2.9 0.7 %collective-permute-start.2 = (bf16[256,512]{1,0:T(8,128)(2,1)}, bf16[256,512]{1,0:T(8,128)(2,1)S(1)}, u32[]{:S(2)}, u32[]{:S(2)}) collective-permute-start(bf16[256,512]{1,0:T(8,128)(2,1)} %refs_0_.1), channel_id=1, source_target_pairs={{0,5},{1,9},{2,7},{3,11},{4,1},{5,13},{6,3},{7,15},{8,0},{9,12},{1... | collective-permute-start | bytes 786440 | tf_op jit(solution)/shard_map/ppermute | solution.py:168
  3.6 1.3 %constant_dynamic-slice_fusion = (bf16[512,512]{1,0:T(8,128)(2,1)S(1)}, bf16[512,512]{1,0:T(8,128)(2,1)S(1)}) fusion(bf16[512,1024]{1,0:T(8,128)(2,1)} %param.4, s32[]{:T(128)S(6)} %select_n.13, s32[]{:T(128)S(6)} %select_n.12), kind=kLoop, calls=%fused_computation | loop fusion | bytes 2097160 | tf_op jit(solution)/shard_map/dynamic_slice | solution.py:179
  4.9 0.0 copy-start.1
  4.9 0.6 %collective-permute-start.5 = (bf16[512,512]{1,0:T(8,128)(2,1)S(1)}, bf16[512,512]{1,0:T(8,128)(2,1)S(1)}, u32[]{:S(2)}, u32[]{:S(2)}) collective-permute-start(bf16[512,512]{1,0:T(8,128)(2,1)S(1)} %get-tuple-element.23), channel_id=1, source_target_pairs={{0,2},{1,3},{2,0},{3,1},{4,6},{5,7},{6,4},{7,5},{8,10},{9,11},{10,... | collective-permute-start | bytes 1572872 | tf_op jit(solution)/shard_map/ppermute | solution.py:168
  5.5 0.9 %collective-permute-start = (bf16[256,512]{1,0:T(8,128)(2,1)S(1)}, bf16[256,512]{1,0:T(8,128)(2,1)S(1)}, u32[]{:S(2)}, u32[]{:S(2)}) collective-permute-start(bf16[256,512]{1,0:T(8,128)(2,1)S(1)} %copy-done), channel_id=1, source_target_pairs={{0,8},{1,4},{2,10},{3,6},{4,12},{5,0},{6,14},{7,2},{8,13},{9,1},{1... | collective-permute-start | bytes 786440 | tf_op jit(solution)/shard_map/ppermute | solution.py:168
  6.5 3.8 %collective-permute-done.1.refs_3_ = bf16[256,512]{1,0:T(8,128)(2,1)S(1)} collective-permute-done((bf16[256,512]{1,0:T(8,128)(2,1)}, bf16[256,512]{1,0:T(8,128)(2,1)S(1)}, u32[]{:S(2)}, u32[]{:S(2)}) %collective-permute-start.1) | collective-permute-done | bytes 262176 | tf_op jit(solution)/shard_map/ppermute | solution.py:168
  10.3 2.1 %collective-permute-start.3 = (bf16[256,512]{1,0:T(8,128)(2,1)S(1)}, bf16[256,512]{1,0:T(8,128)(2,1)S(1)}, u32[]{:S(2)}, u32[]{:S(2)}) collective-permute-start(bf16[256,512]{1,0:T(8,128)(2,1)S(1)} %collective-permute-done.1.refs_3_), channel_id=1, source_target_pairs={{0,8},{1,4},{2,10},{3,6},{4,12},{5,0},{6,14},{7,2},{8,13},{9,1},{1... | collective-permute-start | bytes 786440 | tf_op jit(solution)/shard_map/ppermute | solution.py:168
  12.4 2.0 %collective-permute-start.7 = (bf16[256,512]{1,0:T(8,128)(2,1)S(1)}, bf16[256,512]{1,0:T(8,128)(2,1)S(1)}, u32[]{:S(2)}, u32[]{:S(2)}) collective-permute-start(bf16[256,512]{1,0:T(8,128)(2,1)S(1)} %collective-permute-done.refs_1_.refs_0_), channel_id=1, source_target_pairs={{0,8},{1,4},{2,10},{3,6},{4,12},{5,0},{6,14},{7,2},{8,13},{9,1},{1... | collective-permute-start | bytes 786440 | tf_op jit(solution)/shard_map/ppermute | solution.py:168
  14.4 4.1 %collective-permute-done.3.refs_4_.refs_3_ = bf16[256,512]{1,0:T(8,128)(2,1)S(1)} collective-permute-done((bf16[256,512]{1,0:T(8,128)(2,1)S(1)}, bf16[256,512]{1,0:T(8,128)(2,1)S(1)}, u32[]{:S(2)}, u32[]{:S(2)}) %collective-permute-start.3) | collective-permute-done | bytes 262176 | tf_op jit(solution)/shard_map/ppermute | solution.py:168
  18.5 2.5 %collective-permute-start.6 = (bf16[256,512]{1,0:T(8,128)(2,1)S(1)}, bf16[256,512]{1,0:T(8,128)(2,1)S(1)}, u32[]{:S(2)}, u32[]{:S(2)}) collective-permute-start(bf16[256,512]{1,0:T(8,128)(2,1)S(1)} %collective-permute-done.3.refs_4_.refs_3_), channel_id=1, source_target_pairs={{0,8},{1,4},{2,10},{3,6},{4,12},{5,0},{6,14},{7,2},{8,13},{9,1},{1... | collective-permute-start | bytes 786440 | tf_op jit(solution)/shard_map/ppermute | solution.py:168
  21.0 0.0 collective-permute-done.5.refs_7_.refs_6_.refs_2_
  21.0 0.0 collective-permute-done.4.refs_5_.refs_4_
  21.0 0.9 %multiply.7 = (f32[2,256,256]{2,1,0:T(8,128)S(1)}, f32[2,256,256]{2,1,0:T(8,128)S(1)}) custom-call(s32[4,4]{1,0:T(4,128)S(1)} %copy-done.1, bf16[256,512]{1,0:T(8,128)(2,1)S(1)} %copy-done, bf16[256,512]{1,0:T(8,128)(2,1)S(1)} %collective-permute-done.refs_1_.refs_0_, bf16[256,512]{1,0:T(8,128)(2,1)S(1)} %collective-permute-done.2.refs_2_.refs_1_, ...), custom_call_target="tpu_custom_call" | custom-call | flops 268435456 | bytes 1048576 | tf_op jit(solution)/shard_map/multiply/pallas_call | solution.py:96
  21.9 0.5 %collective-permute-start.9 = (f32[2,256,256]{2,1,0:T(8,128)S(1)}, f32[2,256,256]{2,1,0:T(8,128)S(1)}, u32[]{:S(2)}, u32[]{:S(2)}) collective-permute-start(f32[2,256,256]{2,1,0:T(8,128)S(1)} %get-tuple-element.21), channel_id=1, source_target_pairs={{0,1},{1,0},{2,3},{3,2},{4,5},{5,4},{6,7},{7,6},{8,9},{9,8},{10,11... | collective-permute-start | bytes 1572872 | tf_op jit(solution)/shard_map/ppermute | solution.py:168
  22.4 0.0 collective-permute-done.7.refs_2_
  22.4 0.8 %multiply.8 = (f32[1,256,256]{2,1,0:T(8,128)S(1)}, f32[1,256,256]{2,1,0:T(8,128)S(1)}, f32[256,512]{1,0:T(8,128)S(1)}) custom-call(s32[4,4]{1,0:T(4,128)S(1)} %copy-done.1, bf16[256,512]{1,0:T(8,128)(2,1)S(1)} %collective-permute-done.refs_1_.refs_0_, bf16[256,512]{1,0:T(8,128)(2,1)S(1)} %collective-permute-done.2.refs_2_.refs_1_, ...), custom_call_target="tpu_custom_call" | custom-call | flops 134217728 | bytes 1048576 | tf_op jit(solution)/shard_map/multiply/pallas_call | solution.py:96
  23.2 0.1 collective-permute-start.10
  23.3 1.6 %collective-permute-done.6.refs_0_ = bf16[256,512]{1,0:T(8,128)(2,1)S(1)} collective-permute-done((bf16[256,512]{1,0:T(8,128)(2,1)S(1)}, bf16[256,512]{1,0:T(8,128)(2,1)S(1)}, u32[]{:S(2)}, u32[]{:S(2)}) %collective-permute-start.6) | collective-permute-done | bytes 262176 | tf_op jit(solution)/shard_map/ppermute | solution.py:168
  24.9 0.2 multiply.9
  25.1 0.1 collective-permute-start.8
  25.2 0.9 %add.11.refs_2_ = f32[256,1024]{1,0:T(8,128)} custom-call(f32[2,256,256]{2,1,0:T(8,128)S(1)} %get-tuple-element.16.refs_0_, f32[1,256,256]{2,1,0:T(8,128)S(1)} %get-tuple-element.19.refs_1_, f32[1,256,256]{2,1,0:T(8,128)S(1)} %get-tuple-element.20.refs_2_, f32[2,256,256]{2,1,0:T(8,128)S(1)} %collective-permute-done.9.refs_3_, ...), custom_call_target="tpu_custom_call" | custom-call | tf_op jit(solution)/shard_map/add/pallas_call | solution.py:142
  26.1 0.5 %collective-permute-done.8.refs_1_ = f32[1,256,256]{2,1,0:T(8,128)S(1)} collective-permute-done((f32[1,256,256]{2,1,0:T(8,128)S(1)}, f32[1,256,256]{2,1,0:T(8,128)S(1)}, u32[]{:S(2)}, u32[]{:S(2)}) %collective-permute-start.8) | collective-permute-done | bytes 262176 | tf_op jit(solution)/shard_map/ppermute | solution.py:168
  26.7 0.7 %add.12 = f32[256,1024]{1,0:T(8,128)} custom-call(f32[2,256,256]{2,1,0:T(8,128)S(1)} %get-tuple-element.16.refs_0_, f32[1,256,256]{2,1,0:T(8,128)S(1)} %collective-permute-done.8.refs_1_, f32[256,1024]{1,0:T(8,128)} %add.11.refs_2_), custom_call_target="tpu_custom_call", output_to_operand_aliasing={{}: (2, {})} | custom-call | tf_op jit(solution)/shard_map/add/pallas_call | solution.py:142
  (8 shorter events, 0.0 us)
Async XLA Ops:
  0.0 10.3 %collective-permute-start.1 = (bf16[256,512]{1,0:T(8,128)(2,1)}, bf16[256,512]{1,0:T(8,128)(2,1)S(1)}, u32[]{:S(2)}, u32[]{:S(2)}) collective-permute-start(bf16[256,512]{1,0:T(8,128)(2,1)} %refs_0_.1), channel_id=1, source_target_pairs={{0,2},{1,3},{2,0},{3,1},{4,6},{5,7},{6,4},{7,5},{8,10},{9,11},{10,... | collective-permute-start | bytes 786440 | tf_op jit(solution)/shard_map/ppermute | solution.py:168
  2.9 9.4 %collective-permute-start.2 = (bf16[256,512]{1,0:T(8,128)(2,1)}, bf16[256,512]{1,0:T(8,128)(2,1)S(1)}, u32[]{:S(2)}, u32[]{:S(2)}) collective-permute-start(bf16[256,512]{1,0:T(8,128)(2,1)} %refs_0_.1), channel_id=1, source_target_pairs={{0,5},{1,9},{2,7},{3,11},{4,1},{5,13},{6,3},{7,15},{8,0},{9,12},{1... | collective-permute-start | bytes 786440 | tf_op jit(solution)/shard_map/ppermute | solution.py:168
  3.6 1.9 %copy-start = (bf16[256,512]{1,0:T(8,128)(2,1)S(1)}, bf16[256,512]{1,0:T(8,128)(2,1)}, u32[]{:S(2)}) copy-start(bf16[256,512]{1,0:T(8,128)(2,1)} %refs_0_.1) | copy-start | bytes 786436
  4.9 16.1 %copy-start.1 = (s32[4,4]{1,0:T(4,128)S(1)}, s32[4,4]{1,0:T(4,128)}, u32[]{:S(2)}) copy-start(s32[4,4]{1,0:T(4,128)} %pairs.5) | copy-start | bytes 196
  4.9 16.0 %collective-permute-start.5 = (bf16[512,512]{1,0:T(8,128)(2,1)S(1)}, bf16[512,512]{1,0:T(8,128)(2,1)S(1)}, u32[]{:S(2)}, u32[]{:S(2)}) collective-permute-start(bf16[512,512]{1,0:T(8,128)(2,1)S(1)} %get-tuple-element.23), channel_id=1, source_target_pairs={{0,2},{1,3},{2,0},{3,1},{4,6},{5,7},{6,4},{7,5},{8,10},{9,11},{10,... | collective-permute-start | bytes 1572872 | tf_op jit(solution)/shard_map/ppermute | solution.py:168
  5.5 6.8 %collective-permute-start = (bf16[256,512]{1,0:T(8,128)(2,1)S(1)}, bf16[256,512]{1,0:T(8,128)(2,1)S(1)}, u32[]{:S(2)}, u32[]{:S(2)}) collective-permute-start(bf16[256,512]{1,0:T(8,128)(2,1)S(1)} %copy-done), channel_id=1, source_target_pairs={{0,8},{1,4},{2,10},{3,6},{4,12},{5,0},{6,14},{7,2},{8,13},{9,1},{1... | collective-permute-start | bytes 786440 | tf_op jit(solution)/shard_map/ppermute | solution.py:168
  10.3 8.2 %collective-permute-start.3 = (bf16[256,512]{1,0:T(8,128)(2,1)S(1)}, bf16[256,512]{1,0:T(8,128)(2,1)S(1)}, u32[]{:S(2)}, u32[]{:S(2)}) collective-permute-start(bf16[256,512]{1,0:T(8,128)(2,1)S(1)} %collective-permute-done.1.refs_3_), channel_id=1, source_target_pairs={{0,8},{1,4},{2,10},{3,6},{4,12},{5,0},{6,14},{7,2},{8,13},{9,1},{1... | collective-permute-start | bytes 786440 | tf_op jit(solution)/shard_map/ppermute | solution.py:168
  12.4 8.6 %collective-permute-start.4 = (bf16[256,512]{1,0:T(8,128)(2,1)S(1)}, bf16[256,512]{1,0:T(8,128)(2,1)S(1)}, u32[]{:S(2)}, u32[]{:S(2)}) collective-permute-start(bf16[256,512]{1,0:T(8,128)(2,1)S(1)} %collective-permute-done.1.refs_3_), channel_id=1, source_target_pairs={{0,5},{1,9},{2,7},{3,11},{4,1},{5,13},{6,3},{7,15},{8,0},{9,12},{1... | collective-permute-start | bytes 786440 | tf_op jit(solution)/shard_map/ppermute | solution.py:168
  12.4 10.0 %collective-permute-start.7 = (bf16[256,512]{1,0:T(8,128)(2,1)S(1)}, bf16[256,512]{1,0:T(8,128)(2,1)S(1)}, u32[]{:S(2)}, u32[]{:S(2)}) collective-permute-start(bf16[256,512]{1,0:T(8,128)(2,1)S(1)} %collective-permute-done.refs_1_.refs_0_), channel_id=1, source_target_pairs={{0,8},{1,4},{2,10},{3,6},{4,12},{5,0},{6,14},{7,2},{8,13},{9,1},{1... | collective-permute-start | bytes 786440 | tf_op jit(solution)/shard_map/ppermute | solution.py:168
  18.5 6.4 %collective-permute-start.6 = (bf16[256,512]{1,0:T(8,128)(2,1)S(1)}, bf16[256,512]{1,0:T(8,128)(2,1)S(1)}, u32[]{:S(2)}, u32[]{:S(2)}) collective-permute-start(bf16[256,512]{1,0:T(8,128)(2,1)S(1)} %collective-permute-done.3.refs_4_.refs_3_), channel_id=1, source_target_pairs={{0,8},{1,4},{2,10},{3,6},{4,12},{5,0},{6,14},{7,2},{8,13},{9,1},{1... | collective-permute-start | bytes 786440 | tf_op jit(solution)/shard_map/ppermute | solution.py:168
  21.9 3.3 %collective-permute-start.9 = (f32[2,256,256]{2,1,0:T(8,128)S(1)}, f32[2,256,256]{2,1,0:T(8,128)S(1)}, u32[]{:S(2)}, u32[]{:S(2)}) collective-permute-start(f32[2,256,256]{2,1,0:T(8,128)S(1)} %get-tuple-element.21), channel_id=1, source_target_pairs={{0,1},{1,0},{2,3},{3,2},{4,5},{5,4},{6,7},{7,6},{8,9},{9,8},{10,11... | collective-permute-start | bytes 1572872 | tf_op jit(solution)/shard_map/ppermute | solution.py:168
  23.2 1.9 %collective-permute-start.10 = (f32[1,256,256]{2,1,0:T(8,128)S(1)}, f32[1,256,256]{2,1,0:T(8,128)S(1)}, u32[]{:S(2)}, u32[]{:S(2)}) collective-permute-start(f32[1,256,256]{2,1,0:T(8,128)S(1)} %get-tuple-element.22), channel_id=1, source_target_pairs={{0,1},{1,0},{2,3},{3,2},{4,5},{5,4},{6,7},{7,6},{8,9},{9,8},{10,11... | collective-permute-start | bytes 786440 | tf_op jit(solution)/shard_map/ppermute | solution.py:168
  25.1 1.6 %collective-permute-start.8 = (f32[1,256,256]{2,1,0:T(8,128)S(1)}, f32[1,256,256]{2,1,0:T(8,128)S(1)}, u32[]{:S(2)}, u32[]{:S(2)}) collective-permute-start(f32[1,256,256]{2,1,0:T(8,128)S(1)} %get-tuple-element.18), channel_id=1, source_target_pairs={{0,1},{1,0},{2,3},{3,2},{4,5},{5,4},{6,7},{7,6},{8,9},{9,8},{10,11... | collective-permute-start | bytes 786440 | tf_op jit(solution)/shard_map/ppermute | solution.py:168
